TPU v7x, 32 devices: a whole 2x2x4 slice. The times are simulated.
32 devices in a mesh: we: 4 (over y, x), sn: 8 (over z, core).
Axes of the slice: x: 2, y: 2, z: 4, core: 2. Of those that a mesh axis runs over, the one named last changes fastest.
Arguments:
- velocity: float32 [3, 16, 96, 128], P(None, 'we', 'sn'), may hold values from -6 to 6
- stress: float32 [6, 16, 96, 128], P(None, 'we', 'sn'), may hold values from -6 to 6
- memory: float32 [6, 16, 96, 128], P(None, 'we', 'sn'), may hold values from -3 to 3
- material_code: int32 [16, 96, 128], P('we', 'sn'), may hold values from 0 to 15
- block_scale: float32 [4, 24, 4], P('we', 'sn'), may hold values from 0.5 to 2
- material_table: float32 [6, 16], replicated, may hold values from 0.2 to 3, as said below
- source_cell: int32 [4, 8, 4], P('we', 'sn'), may hold values from 0 to 6143, as said below
- source_amp: float32 [4, 8, 4, 4], P('we', 'sn'), may hold values from -24 to 24
Outputs:
- velocity_out: float32 [3, 16, 96, 128], P(None, 'we', 'sn')
- stress_out: float32 [6, 16, 96, 128], P(None, 'we', 'sn')
- memory_out: float32 [6, 16, 96, 128], P(None, 'we', 'sn')
Inputs may be any that keep to these rules, and one draw needn't show every extreme that they name: Rows of material_table lie in: buoyancy 0.6 to 1.4, first Lame parameter 0.5 to 2, shear modulus 0.3 to 1.5, decay 0.5 to 0.98, weight 0.2 to 0.8, cohesion 0.3 to 3. `source_cell`: each entry is c = x 12 * 128 + y * 128 + z for a cell (x, y, z) of the device's own block; cells may repeat.
All inputs are finite; a program needn't handle non-finite values.
Results may differ from a plain program's by a relative error of at most 0.0001.
Values sent between devices are 32-bit elements; how exact they have to be, the bound alone decides.
No kernel may reach another device: no remote copies, remote signals or barrier semaphores. Data moves between devices by JAX's collectives and lax.ppermute only.
A program may use at most 64 MiB of HBM per device.

v0:
```python
import jax
import jax.numpy as jnp
from jax import lax
from jax.sharding import PartitionSpec as P

STEPS = 4
BLK = 4
BLKZ = 32


inner_coef = 9.0 / 8.0
outer_coef = 1.0 / 24.0
time_step = 0.08
friction = 0.4


def with_halo(block, sides, width):
    for axis, dim in sides:
        count = lax.axis_size(axis)
        forward = [(i, i + 1) for i in range(count - 1)]
        backward = [(target, source) for source, target in forward]
        low = lax.ppermute(
            lax.slice_in_dim(block, block.shape[dim] - width, None, axis=dim), axis, forward
        )
        high = lax.ppermute(lax.slice_in_dim(block, 0, width, axis=dim), axis, backward)
        block = jnp.concatenate([low, block, high], axis=dim)
    return block


def shifted(padded, along_dim, offset):
    length = padded.shape[along_dim] - 4
    return lax.slice_in_dim(padded, 2 + offset, 2 + offset + length, axis=along_dim)


def forward(padded, along_dim):
    return inner_coef * (
        shifted(padded, along_dim, 1) - shifted(padded, along_dim, 0)
    ) - outer_coef * (shifted(padded, along_dim, 2) - shifted(padded, along_dim, -1))


def backward(padded, along_dim):
    return inner_coef * (
        shifted(padded, along_dim, 0) - shifted(padded, along_dim, -1)
    ) - outer_coef * (shifted(padded, along_dim, 1) - shifted(padded, along_dim, -2))


def depth_pad(fields):
    return jnp.pad(fields, ((0, 0), (0, 0), (0, 0), (2, 2)))


def velocity_step(velocity, stress, east_pad, north_pad, buoyancy):
    depth_stress = depth_pad(stress[1::2])
    force_east = forward(east_pad[0], 0) + backward(north_pad[0], 1) + backward(depth_stress[0], 2)
    force_north = backward(east_pad[2], 0) + forward(north_pad[2], 1) + backward(depth_stress[1], 2)
    force_depth = backward(east_pad[1], 0) + backward(north_pad[1], 1) + forward(depth_stress[2], 2)
    return velocity + time_step * buoyancy * jnp.stack([force_east, force_north, force_depth])


def stress_step(stress, memory, east_vel, north_vel, velocity, lame, shear_mod, decay, weight):
    depth_vel = depth_pad(velocity)
    rate_ee = backward(east_vel[0], 0)
    north_east = forward(east_vel[1], 0)
    depth_east = forward(east_vel[2], 0)
    east_north = forward(north_vel[0], 1)
    rate_nn = backward(north_vel[1], 1)
    depth_north = forward(north_vel[2], 1)
    east_depth = forward(depth_vel[0], 2)
    north_depth = forward(depth_vel[1], 2)
    rate_dd = backward(depth_vel[2], 2)
    volume_rate = rate_ee + rate_nn + rate_dd
    rates = jnp.stack(
        [
            lame * volume_rate + 2.0 * shear_mod * rate_ee,
            shear_mod * (east_depth + depth_east),
            shear_mod * (east_north + north_east),
            shear_mod * (north_depth + depth_north),
            lame * volume_rate + 2.0 * shear_mod * rate_nn,
            lame * volume_rate + 2.0 * shear_mod * rate_dd,
        ]
    )
    memory_new = decay * memory + (1.0 - decay) * weight * rates
    trial = stress + time_step * (rates - 0.5 * (memory + memory_new))
    return (trial, memory_new)


def plastic(trial, cohesion):
    normal_mask = jnp.array([1.0, 0.0, 0.0, 0.0, 1.0, 1.0], jnp.float32)[:, None, None, None]
    square_weights = jnp.array([0.5, 1.0, 1.0, 1.0, 0.5, 0.5], jnp.float32)[:, None, None, None]
    mean_stress = (trial[0] + trial[4] + trial[5]) / 3.0
    deviator = trial - normal_mask * mean_stress
    second_inv = jnp.sum(square_weights * deviator * deviator, 0)
    yield_level = cohesion + friction * jax.nn.softplus(-mean_stress)
    scaled = second_inv / (yield_level * yield_level)
    factor = lax.rsqrt(jnp.sqrt(1.0 + scaled * scaled))
    return normal_mask * mean_stress + factor * deviator


def shards(
    velocity, stress, memory, material_code, block_scale, material_table, source_cell, source_amp
):
    entries = material_table.shape[1]
    levels = lax.broadcasted_iota(jnp.int32, (entries, 1, 1, 1), 0)
    one_hot = (material_code[None] == levels).astype(jnp.float32)
    table_rows = jnp.tensordot(material_table, one_hot, axes=1, precision=lax.Precision.HIGHEST)
    scale_full = jnp.repeat(jnp.repeat(jnp.repeat(block_scale, BLK, 0), BLK, 1), BLKZ, 2)
    buoyancy = table_rows[0]
    lame = table_rows[1] * scale_full
    shear_mod = table_rows[2] * scale_full
    decay = table_rows[3]
    weight = table_rows[4]
    cohesion = table_rows[5]
    source_cells = source_cell.reshape(-1)
    strengths = source_amp.reshape(-1, source_amp.shape[-1])
    normal_rows = jnp.array([0, 4, 5], jnp.int32)
    for turn_index in range(STEPS):
        east_pad = with_halo(stress[0:3], (("we", 1),), 2)
        north_pad = with_halo(stress[2:5], (("sn", 2),), 2)
        velocity = velocity_step(velocity, stress, east_pad, north_pad, buoyancy)
        moved = with_halo(velocity, (("we", 1), ("sn", 2)), 2)
        east_vel = moved[:, :, 2:-2]
        north_vel = moved[:, 2:-2]
        trial, memory = stress_step(
            stress, memory, east_vel, north_vel, velocity, lame, shear_mod, decay, weight
        )
        flat = trial.reshape(6, -1)
        flat = flat.at[normal_rows[:, None], source_cells[None, :]].add(
            time_step * strengths[:, turn_index][None, :]
        )
        trial = flat.reshape(stress.shape)
        stress = plastic(trial, cohesion)
    return (velocity, stress, memory)


def solution(mesh):
    in_specs = (
        P(None, "we", "sn", None),
        P(None, "we", "sn", None),
        P(None, "we", "sn", None),
        P("we", "sn", None),
        P("we", "sn", None),
        P(),
        P("we", "sn", None),
        P("we", "sn", None, None),
    )
    out_specs = (P(None, "we", "sn", None), P(None, "we", "sn", None), P(None, "we", "sn", None))
    return jax.shard_map(shards, mesh=mesh, in_specs=in_specs, out_specs=out_specs, check_vma=False)
```

profile of v0, /device:TPU:1, one launch (start us, length us, event | category | flops | bytes accessed | tf_op | source)
XLA Modules:
  0.0 155.2 jit_solution(7660401597029214256)
XLA Ops:
  1.4 4.6 %collective-permute-start.2 = (f32[3,4,2,128]{3,1,2,0:T(4,128)S(1)}, f32[3,4,2,128]{3,1,2,0:T(4,128)S(1)}, u32[]{:S(2)}, u32[]{:S(2)}) collective-permute-start(f32[3,4,2,128]{3,1,2,0:T(4,128)S(1)} %get-tuple-element.99), channel_id=1, source_target_pairs={{0,1},{1,2},{2,3},{3,4},{4,5},{5,6},{6,7},{8,9},{9,10},{10,11},{11... | collective-permute-start | bytes 36872 | tf_op jit(solution)/shard_map/ppermute | solution.py:22
  6.0 1.9 %collective-permute-start.3 = (f32[3,4,2,128]{3,1,2,0:T(4,128)S(1)}, f32[3,4,2,128]{3,1,2,0:T(4,128)S(1)}, u32[]{:S(2)}, u32[]{:S(2)}) collective-permute-start(f32[3,4,2,128]{3,1,2,0:T(4,128)S(1)} %get-tuple-element.100), channel_id=1, source_target_pairs={{1,0},{2,1},{3,2},{4,3},{5,4},{6,5},{7,6},{9,8},{10,9},{11,10},{12... | collective-permute-start | bytes 36872 | tf_op jit(solution)/shard_map/ppermute | solution.py:25
  7.9 1.0 fusion.413
  8.9 1.3 collective-permute-start
  10.3 4.0 %collective-permute-start.1 = (f32[3,2,12,128]{3,1,2,0:T(2,128)S(1)}, f32[3,2,12,128]{3,1,2,0:T(2,128)S(1)}, u32[]{:S(2)}, u32[]{:S(2)}) collective-permute-start(f32[3,2,12,128]{3,1,2,0:T(2,128)S(1)} %get-tuple-element.95), channel_id=1, source_target_pairs={{0,8},{8,16},{16,24},{1,9},{9,17},{17,25},{2,10},{10,18},{18,26},{... | collective-permute-start | bytes 110600 | tf_op jit(solution)/shard_map/ppermute | solution.py:22
  16.9 4.0 %collective-permute-start.4 = (f32[3,2,12,128]{3,1,2,0:T(2,128)S(1)}, f32[3,2,12,128]{3,1,2,0:T(2,128)S(1)}, u32[]{:S(2)}, u32[]{:S(2)}) collective-permute-start(f32[3,2,12,128]{3,1,2,0:T(2,128)S(1)} %get-tuple-element.141), channel_id=1, source_target_pairs={{0,8},{8,16},{16,24},{1,9},{9,17},{17,25},{2,10},{10,18},{18,26},{... | collective-permute-start | bytes 110600 | tf_op jit(solution)/shard_map/ppermute | solution.py:22
  20.9 1.3 collective-permute-start.5
  23.6 3.3 %collective-permute-done.5 = f32[3,2,12,128]{3,1,2,0:T(2,128)S(1)} collective-permute-done((f32[3,2,12,128]{3,1,2,0:T(2,128)S(1)}, f32[3,2,12,128]{3,1,2,0:T(2,128)S(1)}, u32[]{:S(2)}, u32[]{:S(2)}) %collective-permute-start.5) | collective-permute-done | bytes 36896 | tf_op jit(solution)/shard_map/ppermute | solution.py:25
  27.0 5.7 %collective-permute-start.6 = (f32[3,8,2,128]{3,1,2,0:T(8,128)S(1)}, f32[3,8,2,128]{3,1,2,0:T(8,128)S(1)}, u32[]{:S(2)}, u32[]{:S(2)}) collective-permute-start(f32[3,8,2,128]{3,1,2,0:T(8,128)S(1)} %get-tuple-element.92), channel_id=1, source_target_pairs={{0,1},{1,2},{2,3},{3,4},{4,5},{5,6},{6,7},{8,9},{9,10},{10,11},{11... | collective-permute-start | bytes 73736 | tf_op jit(solution)/shard_map/ppermute | solution.py:22
  32.7 1.9 %collective-permute-start.7 = (f32[3,8,2,128]{3,1,2,0:T(8,128)S(1)}, f32[3,8,2,128]{3,1,2,0:T(8,128)S(1)}, u32[]{:S(2)}, u32[]{:S(2)}) collective-permute-start(f32[3,8,2,128]{3,1,2,0:T(8,128)S(1)} %get-tuple-element.93), channel_id=1, source_target_pairs={{1,0},{2,1},{3,2},{4,3},{5,4},{6,5},{7,6},{9,8},{10,9},{11,10},{12... | collective-permute-start | bytes 73736 | tf_op jit(solution)/shard_map/ppermute | solution.py:25
  34.8 3.1 %collective-permute-done.7 = f32[3,8,2,128]{3,1,2,0:T(8,128)S(1)} collective-permute-done((f32[3,8,2,128]{3,1,2,0:T(8,128)S(1)}, f32[3,8,2,128]{3,1,2,0:T(8,128)S(1)}, u32[]{:S(2)}, u32[]{:S(2)}) %collective-permute-start.7) | collective-permute-done | bytes 24608 | tf_op jit(solution)/shard_map/ppermute | solution.py:25
  39.4 1.1 scatter_fusion
  43.2 1.9 %collective-permute-start.10 = (f32[3,4,2,128]{3,1,2,0:T(4,128)S(1)}, f32[3,4,2,128]{3,1,2,0:T(4,128)S(1)}, u32[]{:S(2)}, u32[]{:S(2)}) collective-permute-start(f32[3,4,2,128]{3,1,2,0:T(4,128)S(1)} %get-tuple-element.83), channel_id=1, source_target_pairs={{0,1},{1,2},{2,3},{3,4},{4,5},{5,6},{6,7},{8,9},{9,10},{10,11},{11... | collective-permute-start | bytes 36872 | tf_op jit(solution)/shard_map/ppermute | solution.py:22
  45.1 2.4 %collective-permute-start.11 = (f32[3,4,2,128]{3,1,2,0:T(4,128)S(1)}, f32[3,4,2,128]{3,1,2,0:T(4,128)S(1)}, u32[]{:S(2)}, u32[]{:S(2)}) collective-permute-start(f32[3,4,2,128]{3,1,2,0:T(4,128)S(1)} %get-tuple-element.84), channel_id=1, source_target_pairs={{1,0},{2,1},{3,2},{4,3},{5,4},{6,5},{7,6},{9,8},{10,9},{11,10},{12... | collective-permute-start | bytes 36872 | tf_op jit(solution)/shard_map/ppermute | solution.py:25
  47.7 1.3 collective-permute-start.8
  49.0 5.2 %collective-permute-start.9 = (f32[3,2,12,128]{3,1,2,0:T(2,128)S(1)}, f32[3,2,12,128]{3,1,2,0:T(2,128)S(1)}, u32[]{:S(2)}, u32[]{:S(2)}) collective-permute-start(f32[3,2,12,128]{3,1,2,0:T(2,128)S(1)} %get-tuple-element.79), channel_id=1, source_target_pairs={{0,8},{8,16},{16,24},{1,9},{9,17},{17,25},{2,10},{10,18},{18,26},{... | collective-permute-start | bytes 110600 | tf_op jit(solution)/shard_map/ppermute | solution.py:22
  54.2 1.1 collective-permute-done.9
  55.8 4.2 %collective-permute-start.12 = (f32[3,2,12,128]{3,1,2,0:T(2,128)S(1)}, f32[3,2,12,128]{3,1,2,0:T(2,128)S(1)}, u32[]{:S(2)}, u32[]{:S(2)}) collective-permute-start(f32[3,2,12,128]{3,1,2,0:T(2,128)S(1)} %get-tuple-element.133), channel_id=1, source_target_pairs={{0,8},{8,16},{16,24},{1,9},{9,17},{17,25},{2,10},{10,18},{18,26},{... | collective-permute-start | bytes 110600 | tf_op jit(solution)/shard_map/ppermute | solution.py:22
  60.0 1.3 collective-permute-start.13
  61.4 5.0 %collective-permute-done.13 = f32[3,2,12,128]{3,1,2,0:T(2,128)S(1)} collective-permute-done((f32[3,2,12,128]{3,1,2,0:T(2,128)S(1)}, f32[3,2,12,128]{3,1,2,0:T(2,128)S(1)}, u32[]{:S(2)}, u32[]{:S(2)}) %collective-permute-start.13) | collective-permute-done | bytes 36896 | tf_op jit(solution)/shard_map/ppermute | solution.py:25
  66.4 5.2 %collective-permute-start.14 = (f32[3,8,2,128]{3,1,2,0:T(8,128)S(1)}, f32[3,8,2,128]{3,1,2,0:T(8,128)S(1)}, u32[]{:S(2)}, u32[]{:S(2)}) collective-permute-start(f32[3,8,2,128]{3,1,2,0:T(8,128)S(1)} %get-tuple-element.76), channel_id=1, source_target_pairs={{0,1},{1,2},{2,3},{3,4},{4,5},{5,6},{6,7},{8,9},{9,10},{10,11},{11... | collective-permute-start | bytes 73736 | tf_op jit(solution)/shard_map/ppermute | solution.py:22
  71.6 1.9 %collective-permute-start.15 = (f32[3,8,2,128]{3,1,2,0:T(8,128)S(1)}, f32[3,8,2,128]{3,1,2,0:T(8,128)S(1)}, u32[]{:S(2)}, u32[]{:S(2)}) collective-permute-start(f32[3,8,2,128]{3,1,2,0:T(8,128)S(1)} %get-tuple-element.77), channel_id=1, source_target_pairs={{1,0},{2,1},{3,2},{4,3},{5,4},{6,5},{7,6},{9,8},{10,9},{11,10},{12... | collective-permute-start | bytes 73736 | tf_op jit(solution)/shard_map/ppermute | solution.py:25
  73.6 3.1 %collective-permute-done.15 = f32[3,8,2,128]{3,1,2,0:T(8,128)S(1)} collective-permute-done((f32[3,8,2,128]{3,1,2,0:T(8,128)S(1)}, f32[3,8,2,128]{3,1,2,0:T(8,128)S(1)}, u32[]{:S(2)}, u32[]{:S(2)}) %collective-permute-start.15) | collective-permute-done | bytes 24608 | tf_op jit(solution)/shard_map/ppermute | solution.py:25
  77.6 1.1 scatter_fusion.1
  80.1 1.9 %collective-permute-start.18 = (f32[3,4,2,128]{3,1,2,0:T(4,128)S(1)}, f32[3,4,2,128]{3,1,2,0:T(4,128)S(1)}, u32[]{:S(2)}, u32[]{:S(2)}) collective-permute-start(f32[3,4,2,128]{3,1,2,0:T(4,128)S(1)} %get-tuple-element.74), channel_id=1, source_target_pairs={{0,1},{1,2},{2,3},{3,4},{4,5},{5,6},{6,7},{8,9},{9,10},{10,11},{11... | collective-permute-start | bytes 36872 | tf_op jit(solution)/shard_map/ppermute | solution.py:22
  82.0 2.4 %collective-permute-start.19 = (f32[3,4,2,128]{3,1,2,0:T(4,128)S(1)}, f32[3,4,2,128]{3,1,2,0:T(4,128)S(1)}, u32[]{:S(2)}, u32[]{:S(2)}) collective-permute-start(f32[3,4,2,128]{3,1,2,0:T(4,128)S(1)} %get-tuple-element.75), channel_id=1, source_target_pairs={{1,0},{2,1},{3,2},{4,3},{5,4},{6,5},{7,6},{9,8},{10,9},{11,10},{12... | collective-permute-start | bytes 36872 | tf_op jit(solution)/shard_map/ppermute | solution.py:25
  84.6 1.3 collective-permute-start.16
  85.9 5.2 %collective-permute-start.17 = (f32[3,2,12,128]{3,1,2,0:T(2,128)S(1)}, f32[3,2,12,128]{3,1,2,0:T(2,128)S(1)}, u32[]{:S(2)}, u32[]{:S(2)}) collective-permute-start(f32[3,2,12,128]{3,1,2,0:T(2,128)S(1)} %get-tuple-element.70), channel_id=1, source_target_pairs={{0,8},{8,16},{16,24},{1,9},{9,17},{17,25},{2,10},{10,18},{18,26},{... | collective-permute-start | bytes 110600 | tf_op jit(solution)/shard_map/ppermute | solution.py:22
  91.2 1.1 collective-permute-done.17
  92.7 4.2 %collective-permute-start.20 = (f32[3,2,12,128]{3,1,2,0:T(2,128)S(1)}, f32[3,2,12,128]{3,1,2,0:T(2,128)S(1)}, u32[]{:S(2)}, u32[]{:S(2)}) collective-permute-start(f32[3,2,12,128]{3,1,2,0:T(2,128)S(1)} %get-tuple-element.125), channel_id=1, source_target_pairs={{0,8},{8,16},{16,24},{1,9},{9,17},{17,25},{2,10},{10,18},{18,26},{... | collective-permute-start | bytes 110600 | tf_op jit(solution)/shard_map/ppermute | solution.py:22
  96.9 1.3 collective-permute-start.21
  98.3 5.0 %collective-permute-done.21 = f32[3,2,12,128]{3,1,2,0:T(2,128)S(1)} collective-permute-done((f32[3,2,12,128]{3,1,2,0:T(2,128)S(1)}, f32[3,2,12,128]{3,1,2,0:T(2,128)S(1)}, u32[]{:S(2)}, u32[]{:S(2)}) %collective-permute-start.21) | collective-permute-done | bytes 36896 | tf_op jit(solution)/shard_map/ppermute | solution.py:25
  103.3 5.2 %collective-permute-start.22 = (f32[3,8,2,128]{3,1,2,0:T(8,128)S(1)}, f32[3,8,2,128]{3,1,2,0:T(8,128)S(1)}, u32[]{:S(2)}, u32[]{:S(2)}) collective-permute-start(f32[3,8,2,128]{3,1,2,0:T(8,128)S(1)} %get-tuple-element.67), channel_id=1, source_target_pairs={{0,1},{1,2},{2,3},{3,4},{4,5},{5,6},{6,7},{8,9},{9,10},{10,11},{11... | collective-permute-start | bytes 73736 | tf_op jit(solution)/shard_map/ppermute | solution.py:22
  108.5 1.9 %collective-permute-start.23 = (f32[3,8,2,128]{3,1,2,0:T(8,128)S(1)}, f32[3,8,2,128]{3,1,2,0:T(8,128)S(1)}, u32[]{:S(2)}, u32[]{:S(2)}) collective-permute-start(f32[3,8,2,128]{3,1,2,0:T(8,128)S(1)} %get-tuple-element.68), channel_id=1, source_target_pairs={{1,0},{2,1},{3,2},{4,3},{5,4},{6,5},{7,6},{9,8},{10,9},{11,10},{12... | collective-permute-start | bytes 73736 | tf_op jit(solution)/shard_map/ppermute | solution.py:25
  110.6 3.1 %collective-permute-done.23 = f32[3,8,2,128]{3,1,2,0:T(8,128)S(1)} collective-permute-done((f32[3,8,2,128]{3,1,2,0:T(8,128)S(1)}, f32[3,8,2,128]{3,1,2,0:T(8,128)S(1)}, u32[]{:S(2)}, u32[]{:S(2)}) %collective-permute-start.23) | collective-permute-done | bytes 24608 | tf_op jit(solution)/shard_map/ppermute | solution.py:25
  114.5 1.1 scatter_fusion.2
  117.0 1.9 %collective-permute-start.26 = (f32[3,4,2,128]{3,1,2,0:T(4,128)S(1)}, f32[3,4,2,128]{3,1,2,0:T(4,128)S(1)}, u32[]{:S(2)}, u32[]{:S(2)}) collective-permute-start(f32[3,4,2,128]{3,1,2,0:T(4,128)S(1)} %get-tuple-element.65), channel_id=1, source_target_pairs={{0,1},{1,2},{2,3},{3,4},{4,5},{5,6},{6,7},{8,9},{9,10},{10,11},{11... | collective-permute-start | bytes 36872 | tf_op jit(solution)/shard_map/ppermute | solution.py:22
  119.0 2.4 %collective-permute-start.27 = (f32[3,4,2,128]{3,1,2,0:T(4,128)S(1)}, f32[3,4,2,128]{3,1,2,0:T(4,128)S(1)}, u32[]{:S(2)}, u32[]{:S(2)}) collective-permute-start(f32[3,4,2,128]{3,1,2,0:T(4,128)S(1)} %get-tuple-element.66), channel_id=1, source_target_pairs={{1,0},{2,1},{3,2},{4,3},{5,4},{6,5},{7,6},{9,8},{10,9},{11,10},{12... | collective-permute-start | bytes 36872 | tf_op jit(solution)/shard_map/ppermute | solution.py:25
  121.5 1.3 collective-permute-start.24
  122.8 5.2 %collective-permute-start.25 = (f32[3,2,12,128]{3,1,2,0:T(2,128)S(1)}, f32[3,2,12,128]{3,1,2,0:T(2,128)S(1)}, u32[]{:S(2)}, u32[]{:S(2)}) collective-permute-start(f32[3,2,12,128]{3,1,2,0:T(2,128)S(1)} %get-tuple-element.61), channel_id=1, source_target_pairs={{0,8},{8,16},{16,24},{1,9},{9,17},{17,25},{2,10},{10,18},{18,26},{... | collective-permute-start | bytes 110600 | tf_op jit(solution)/shard_map/ppermute | solution.py:22
  128.1 1.1 collective-permute-done.25
  129.7 4.2 %collective-permute-start.28 = (f32[3,2,12,128]{3,1,2,0:T(2,128)S(1)}, f32[3,2,12,128]{3,1,2,0:T(2,128)S(1)}, u32[]{:S(2)}, u32[]{:S(2)}) collective-permute-start(f32[3,2,12,128]{3,1,2,0:T(2,128)S(1)} %get-tuple-element.117), channel_id=1, source_target_pairs={{0,8},{8,16},{16,24},{1,9},{9,17},{17,25},{2,10},{10,18},{18,26},{... | collective-permute-start | bytes 110600 | tf_op jit(solution)/shard_map/ppermute | solution.py:22
  133.9 1.3 collective-permute-start.29
  135.3 5.0 %collective-permute-done.29 = f32[3,2,12,128]{3,1,2,0:T(2,128)S(1)} collective-permute-done((f32[3,2,12,128]{3,1,2,0:T(2,128)S(1)}, f32[3,2,12,128]{3,1,2,0:T(2,128)S(1)}, u32[]{:S(2)}, u32[]{:S(2)}) %collective-permute-start.29) | collective-permute-done | bytes 36896 | tf_op jit(solution)/shard_map/ppermute | solution.py:25
  140.3 5.2 %collective-permute-start.30 = (f32[3,8,2,128]{3,1,2,0:T(8,128)S(1)}, f32[3,8,2,128]{3,1,2,0:T(8,128)S(1)}, u32[]{:S(2)}, u32[]{:S(2)}) collective-permute-start(f32[3,8,2,128]{3,1,2,0:T(8,128)S(1)} %get-tuple-element.58), channel_id=1, source_target_pairs={{0,1},{1,2},{2,3},{3,4},{4,5},{5,6},{6,7},{8,9},{9,10},{10,11},{11... | collective-permute-start | bytes 73736 | tf_op jit(solution)/shard_map/ppermute | solution.py:22
  145.5 1.9 %collective-permute-start.31 = (f32[3,8,2,128]{3,1,2,0:T(8,128)S(1)}, f32[3,8,2,128]{3,1,2,0:T(8,128)S(1)}, u32[]{:S(2)}, u32[]{:S(2)}) collective-permute-start(f32[3,8,2,128]{3,1,2,0:T(8,128)S(1)} %get-tuple-element.59), channel_id=1, source_target_pairs={{1,0},{2,1},{3,2},{4,3},{5,4},{6,5},{7,6},{9,8},{10,9},{11,10},{12... | collective-permute-start | bytes 73736 | tf_op jit(solution)/shard_map/ppermute | solution.py:25
  147.5 3.1 %collective-permute-done.31 = f32[3,8,2,128]{3,1,2,0:T(8,128)S(1)} collective-permute-done((f32[3,8,2,128]{3,1,2,0:T(8,128)S(1)}, f32[3,8,2,128]{3,1,2,0:T(8,128)S(1)}, u32[]{:S(2)}, u32[]{:S(2)}) %collective-permute-start.31) | collective-permute-done | bytes 24608 | tf_op jit(solution)/shard_map/ppermute | solution.py:25
  152.1 1.1 scatter_fusion.3
  (196 shorter events, 19.1 us)
Async XLA Ops:
  0.6 13.7 %copy-start = (f32[6,16]{1,0:T(8,128)S(1)}, f32[6,16]{1,0:T(8,128)}, u32[]{:S(2)}) copy-start(f32[6,16]{1,0:T(8,128)} %param.22) | copy-start | bytes 1156
  0.6 13.6 %copy-start.2 = (f32[6,4,12,128]{3,1,2,0:T(4,128)S(1)}, f32[6,4,12,128]{3,1,2,0:T(4,128)}, u32[]{:S(2)}) copy-start(f32[6,4,12,128]{3,1,2,0:T(4,128)} %param.18) | copy-start | bytes 442372
  1.4 14.2 %collective-permute-start.2 = (f32[3,4,2,128]{3,1,2,0:T(4,128)S(1)}, f32[3,4,2,128]{3,1,2,0:T(4,128)S(1)}, u32[]{:S(2)}, u32[]{:S(2)}) collective-permute-start(f32[3,4,2,128]{3,1,2,0:T(4,128)S(1)} %get-tuple-element.99), channel_id=1, source_target_pairs={{0,1},{1,2},{2,3},{3,4},{4,5},{5,6},{6,7},{8,9},{9,10},{10,11},{11... | collective-permute-start | bytes 36872 | tf_op jit(solution)/shard_map/ppermute | solution.py:22
  6.0 9.6 %collective-permute-start.3 = (f32[3,4,2,128]{3,1,2,0:T(4,128)S(1)}, f32[3,4,2,128]{3,1,2,0:T(4,128)S(1)}, u32[]{:S(2)}, u32[]{:S(2)}) collective-permute-start(f32[3,4,2,128]{3,1,2,0:T(4,128)S(1)} %get-tuple-element.100), channel_id=1, source_target_pairs={{1,0},{2,1},{3,2},{4,3},{5,4},{6,5},{7,6},{9,8},{10,9},{11,10},{12... | collective-permute-start | bytes 36872 | tf_op jit(solution)/shard_map/ppermute | solution.py:25
  8.9 6.7 %collective-permute-start = (f32[3,2,12,128]{3,1,2,0:T(2,128)S(1)}, f32[3,2,12,128]{3,1,2,0:T(2,128)S(1)}, u32[]{:S(2)}, u32[]{:S(2)}) collective-permute-start(f32[3,2,12,128]{3,1,2,0:T(2,128)S(1)} %get-tuple-element.94), channel_id=1, source_target_pairs={{8,0},{16,8},{24,16},{9,1},{17,9},{25,17},{10,2},{18,10},{26,18},{... | collective-permute-start | bytes 110600 | tf_op jit(solution)/shard_map/ppermute | solution.py:25
  10.2 4.1 %copy-start.11 = (s32[1,1,4]{2,1,0:T(1,128)S(1)}, s32[1,1,4]{2,1,0:T(1,128)}, u32[]{:S(2)}) copy-start(s32[1,1,4]{2,1,0:T(1,128)} %param.23) | copy-start | bytes 52
  10.3 4.1 %copy-start.7 = (s32[4,12,128]{2,0,1:T(4,128)S(1)}, s32[4,12,128]{2,0,1:T(4,128)}, u32[]{:S(2)}) copy-start(s32[4,12,128]{2,0,1:T(4,128)} %param.20) | copy-start | bytes 73732
  10.3 5.4 %collective-permute-start.1 = (f32[3,2,12,128]{3,1,2,0:T(2,128)S(1)}, f32[3,2,12,128]{3,1,2,0:T(2,128)S(1)}, u32[]{:S(2)}, u32[]{:S(2)}) collective-permute-start(f32[3,2,12,128]{3,1,2,0:T(2,128)S(1)} %get-tuple-element.95), channel_id=1, source_target_pairs={{0,8},{8,16},{16,24},{1,9},{9,17},{17,25},{2,10},{10,18},{18,26},{... | collective-permute-start | bytes 110600 | tf_op jit(solution)/shard_map/ppermute | solution.py:22
  14.7 0.7 copy-start.10
  15.9 0.9 copy-start.3
  16.9 5.3 %copy-start.6 = (f32[1,1,4,4]{3,2,1,0:T(4,128)S(1)}, f32[1,1,4,4]{3,2,1,0:T(4,128)}, u32[]{:S(2)}) copy-start(f32[1,1,4,4]{3,2,1,0:T(4,128)} %param.24) | copy-start | bytes 196
  16.9 6.7 %collective-permute-start.4 = (f32[3,2,12,128]{3,1,2,0:T(2,128)S(1)}, f32[3,2,12,128]{3,1,2,0:T(2,128)S(1)}, u32[]{:S(2)}, u32[]{:S(2)}) collective-permute-start(f32[3,2,12,128]{3,1,2,0:T(2,128)S(1)} %get-tuple-element.141), channel_id=1, source_target_pairs={{0,8},{8,16},{16,24},{1,9},{9,17},{17,25},{2,10},{10,18},{18,26},{... | collective-permute-start | bytes 110600 | tf_op jit(solution)/shard_map/ppermute | solution.py:22
  20.9 6.0 %collective-permute-start.5 = (f32[3,2,12,128]{3,1,2,0:T(2,128)S(1)}, f32[3,2,12,128]{3,1,2,0:T(2,128)S(1)}, u32[]{:S(2)}, u32[]{:S(2)}) collective-permute-start(f32[3,2,12,128]{3,1,2,0:T(2,128)S(1)} %get-tuple-element.140), channel_id=1, source_target_pairs={{8,0},{16,8},{24,16},{9,1},{17,9},{25,17},{10,2},{18,10},{26,18},{... | collective-permute-start | bytes 110600 | tf_op jit(solution)/shard_map/ppermute | solution.py:25
  22.2 0.7 copy-start.9
  27.0 7.8 %collective-permute-start.6 = (f32[3,8,2,128]{3,1,2,0:T(8,128)S(1)}, f32[3,8,2,128]{3,1,2,0:T(8,128)S(1)}, u32[]{:S(2)}, u32[]{:S(2)}) collective-permute-start(f32[3,8,2,128]{3,1,2,0:T(8,128)S(1)} %get-tuple-element.92), channel_id=1, source_target_pairs={{0,1},{1,2},{2,3},{3,4},{4,5},{5,6},{6,7},{8,9},{9,10},{10,11},{11... | collective-permute-start | bytes 73736 | tf_op jit(solution)/shard_map/ppermute | solution.py:22
  32.7 5.1 %collective-permute-start.7 = (f32[3,8,2,128]{3,1,2,0:T(8,128)S(1)}, f32[3,8,2,128]{3,1,2,0:T(8,128)S(1)}, u32[]{:S(2)}, u32[]{:S(2)}) collective-permute-start(f32[3,8,2,128]{3,1,2,0:T(8,128)S(1)} %get-tuple-element.93), channel_id=1, source_target_pairs={{1,0},{2,1},{3,2},{4,3},{5,4},{6,5},{7,6},{9,8},{10,9},{11,10},{12... | collective-permute-start | bytes 73736 | tf_op jit(solution)/shard_map/ppermute | solution.py:25
  38.4 0.9 copy-start.4
  42.0 0.7 copy-start.5
  42.0 0.7 copy-start.8
  43.2 11.0 %collective-permute-start.10 = (f32[3,4,2,128]{3,1,2,0:T(4,128)S(1)}, f32[3,4,2,128]{3,1,2,0:T(4,128)S(1)}, u32[]{:S(2)}, u32[]{:S(2)}) collective-permute-start(f32[3,4,2,128]{3,1,2,0:T(4,128)S(1)} %get-tuple-element.83), channel_id=1, source_target_pairs={{0,1},{1,2},{2,3},{3,4},{4,5},{5,6},{6,7},{8,9},{9,10},{10,11},{11... | collective-permute-start | bytes 36872 | tf_op jit(solution)/shard_map/ppermute | solution.py:22
  45.1 9.0 %collective-permute-start.11 = (f32[3,4,2,128]{3,1,2,0:T(4,128)S(1)}, f32[3,4,2,128]{3,1,2,0:T(4,128)S(1)}, u32[]{:S(2)}, u32[]{:S(2)}) collective-permute-start(f32[3,4,2,128]{3,1,2,0:T(4,128)S(1)} %get-tuple-element.84), channel_id=1, source_target_pairs={{1,0},{2,1},{3,2},{4,3},{5,4},{6,5},{7,6},{9,8},{10,9},{11,10},{12... | collective-permute-start | bytes 36872 | tf_op jit(solution)/shard_map/ppermute | solution.py:25
  47.7 6.5 %collective-permute-start.8 = (f32[3,2,12,128]{3,1,2,0:T(2,128)S(1)}, f32[3,2,12,128]{3,1,2,0:T(2,128)S(1)}, u32[]{:S(2)}, u32[]{:S(2)}) collective-permute-start(f32[3,2,12,128]{3,1,2,0:T(2,128)S(1)} %get-tuple-element.78), channel_id=1, source_target_pairs={{8,0},{16,8},{24,16},{9,1},{17,9},{25,17},{10,2},{18,10},{26,18},{... | collective-permute-start | bytes 110600 | tf_op jit(solution)/shard_map/ppermute | solution.py:25
  49.0 6.4 %collective-permute-start.9 = (f32[3,2,12,128]{3,1,2,0:T(2,128)S(1)}, f32[3,2,12,128]{3,1,2,0:T(2,128)S(1)}, u32[]{:S(2)}, u32[]{:S(2)}) collective-permute-start(f32[3,2,12,128]{3,1,2,0:T(2,128)S(1)} %get-tuple-element.79), channel_id=1, source_target_pairs={{0,8},{8,16},{16,24},{1,9},{9,17},{17,25},{2,10},{10,18},{18,26},{... | collective-permute-start | bytes 110600 | tf_op jit(solution)/shard_map/ppermute | solution.py:22
  55.8 5.6 %collective-permute-start.12 = (f32[3,2,12,128]{3,1,2,0:T(2,128)S(1)}, f32[3,2,12,128]{3,1,2,0:T(2,128)S(1)}, u32[]{:S(2)}, u32[]{:S(2)}) collective-permute-start(f32[3,2,12,128]{3,1,2,0:T(2,128)S(1)} %get-tuple-element.133), channel_id=1, source_target_pairs={{0,8},{8,16},{16,24},{1,9},{9,17},{17,25},{2,10},{10,18},{18,26},{... | collective-permute-start | bytes 110600 | tf_op jit(solution)/shard_map/ppermute | solution.py:22
  60.0 6.4 %collective-permute-start.13 = (f32[3,2,12,128]{3,1,2,0:T(2,128)S(1)}, f32[3,2,12,128]{3,1,2,0:T(2,128)S(1)}, u32[]{:S(2)}, u32[]{:S(2)}) collective-permute-start(f32[3,2,12,128]{3,1,2,0:T(2,128)S(1)} %get-tuple-element.132), channel_id=1, source_target_pairs={{8,0},{16,8},{24,16},{9,1},{17,9},{25,17},{10,2},{18,10},{26,18},{... | collective-permute-start | bytes 110600 | tf_op jit(solution)/shard_map/ppermute | solution.py:25
  66.4 7.3 %collective-permute-start.14 = (f32[3,8,2,128]{3,1,2,0:T(8,128)S(1)}, f32[3,8,2,128]{3,1,2,0:T(8,128)S(1)}, u32[]{:S(2)}, u32[]{:S(2)}) collective-permute-start(f32[3,8,2,128]{3,1,2,0:T(8,128)S(1)} %get-tuple-element.76), channel_id=1, source_target_pairs={{0,1},{1,2},{2,3},{3,4},{4,5},{5,6},{6,7},{8,9},{9,10},{10,11},{11... | collective-permute-start | bytes 73736 | tf_op jit(solution)/shard_map/ppermute | solution.py:22
  71.6 5.1 %collective-permute-start.15 = (f32[3,8,2,128]{3,1,2,0:T(8,128)S(1)}, f32[3,8,2,128]{3,1,2,0:T(8,128)S(1)}, u32[]{:S(2)}, u32[]{:S(2)}) collective-permute-start(f32[3,8,2,128]{3,1,2,0:T(8,128)S(1)} %get-tuple-element.77), channel_id=1, source_target_pairs={{1,0},{2,1},{3,2},{4,3},{5,4},{6,5},{7,6},{9,8},{10,9},{11,10},{12... | collective-permute-start | bytes 73736 | tf_op jit(solution)/shard_map/ppermute | solution.py:25
  80.1 11.0 %collective-permute-start.18 = (f32[3,4,2,128]{3,1,2,0:T(4,128)S(1)}, f32[3,4,2,128]{3,1,2,0:T(4,128)S(1)}, u32[]{:S(2)}, u32[]{:S(2)}) collective-permute-start(f32[3,4,2,128]{3,1,2,0:T(4,128)S(1)} %get-tuple-element.74), channel_id=1, source_target_pairs={{0,1},{1,2},{2,3},{3,4},{4,5},{5,6},{6,7},{8,9},{9,10},{10,11},{11... | collective-permute-start | bytes 36872 | tf_op jit(solution)/shard_map/ppermute | solution.py:22
  82.0 9.0 %collective-permute-start.19 = (f32[3,4,2,128]{3,1,2,0:T(4,128)S(1)}, f32[3,4,2,128]{3,1,2,0:T(4,128)S(1)}, u32[]{:S(2)}, u32[]{:S(2)}) collective-permute-start(f32[3,4,2,128]{3,1,2,0:T(4,128)S(1)} %get-tuple-element.75), channel_id=1, source_target_pairs={{1,0},{2,1},{3,2},{4,3},{5,4},{6,5},{7,6},{9,8},{10,9},{11,10},{12... | collective-permute-start | bytes 36872 | tf_op jit(solution)/shard_map/ppermute | solution.py:25
  84.6 6.5 %collective-permute-start.16 = (f32[3,2,12,128]{3,1,2,0:T(2,128)S(1)}, f32[3,2,12,128]{3,1,2,0:T(2,128)S(1)}, u32[]{:S(2)}, u32[]{:S(2)}) collective-permute-start(f32[3,2,12,128]{3,1,2,0:T(2,128)S(1)} %get-tuple-element.69), channel_id=1, source_target_pairs={{8,0},{16,8},{24,16},{9,1},{17,9},{25,17},{10,2},{18,10},{26,18},{... | collective-permute-start | bytes 110600 | tf_op jit(solution)/shard_map/ppermute | solution.py:25
  85.9 6.4 %collective-permute-start.17 = (f32[3,2,12,128]{3,1,2,0:T(2,128)S(1)}, f32[3,2,12,128]{3,1,2,0:T(2,128)S(1)}, u32[]{:S(2)}, u32[]{:S(2)}) collective-permute-start(f32[3,2,12,128]{3,1,2,0:T(2,128)S(1)} %get-tuple-element.70), channel_id=1, source_target_pairs={{0,8},{8,16},{16,24},{1,9},{9,17},{17,25},{2,10},{10,18},{18,26},{... | collective-permute-start | bytes 110600 | tf_op jit(solution)/shard_map/ppermute | solution.py:22
  92.7 5.6 %collective-permute-start.20 = (f32[3,2,12,128]{3,1,2,0:T(2,128)S(1)}, f32[3,2,12,128]{3,1,2,0:T(2,128)S(1)}, u32[]{:S(2)}, u32[]{:S(2)}) collective-permute-start(f32[3,2,12,128]{3,1,2,0:T(2,128)S(1)} %get-tuple-element.125), channel_id=1, source_target_pairs={{0,8},{8,16},{16,24},{1,9},{9,17},{17,25},{2,10},{10,18},{18,26},{... | collective-permute-start | bytes 110600 | tf_op jit(solution)/shard_map/ppermute | solution.py:22
  96.9 6.4 %collective-permute-start.21 = (f32[3,2,12,128]{3,1,2,0:T(2,128)S(1)}, f32[3,2,12,128]{3,1,2,0:T(2,128)S(1)}, u32[]{:S(2)}, u32[]{:S(2)}) collective-permute-start(f32[3,2,12,128]{3,1,2,0:T(2,128)S(1)} %get-tuple-element.124), channel_id=1, source_target_pairs={{8,0},{16,8},{24,16},{9,1},{17,9},{25,17},{10,2},{18,10},{26,18},{... | collective-permute-start | bytes 110600 | tf_op jit(solution)/shard_map/ppermute | solution.py:25
  103.3 7.3 %collective-permute-start.22 = (f32[3,8,2,128]{3,1,2,0:T(8,128)S(1)}, f32[3,8,2,128]{3,1,2,0:T(8,128)S(1)}, u32[]{:S(2)}, u32[]{:S(2)}) collective-permute-start(f32[3,8,2,128]{3,1,2,0:T(8,128)S(1)} %get-tuple-element.67), channel_id=1, source_target_pairs={{0,1},{1,2},{2,3},{3,4},{4,5},{5,6},{6,7},{8,9},{9,10},{10,11},{11... | collective-permute-start | bytes 73736 | tf_op jit(solution)/shard_map/ppermute | solution.py:22
  108.5 5.1 %collective-permute-start.23 = (f32[3,8,2,128]{3,1,2,0:T(8,128)S(1)}, f32[3,8,2,128]{3,1,2,0:T(8,128)S(1)}, u32[]{:S(2)}, u32[]{:S(2)}) collective-permute-start(f32[3,8,2,128]{3,1,2,0:T(8,128)S(1)} %get-tuple-element.68), channel_id=1, source_target_pairs={{1,0},{2,1},{3,2},{4,3},{5,4},{6,5},{7,6},{9,8},{10,9},{11,10},{12... | collective-permute-start | bytes 73736 | tf_op jit(solution)/shard_map/ppermute | solution.py:25
  117.0 11.0 %collective-permute-start.26 = (f32[3,4,2,128]{3,1,2,0:T(4,128)S(1)}, f32[3,4,2,128]{3,1,2,0:T(4,128)S(1)}, u32[]{:S(2)}, u32[]{:S(2)}) collective-permute-start(f32[3,4,2,128]{3,1,2,0:T(4,128)S(1)} %get-tuple-element.65), channel_id=1, source_target_pairs={{0,1},{1,2},{2,3},{3,4},{4,5},{5,6},{6,7},{8,9},{9,10},{10,11},{11... | collective-permute-start | bytes 36872 | tf_op jit(solution)/shard_map/ppermute | solution.py:22
  119.0 9.0 %collective-permute-start.27 = (f32[3,4,2,128]{3,1,2,0:T(4,128)S(1)}, f32[3,4,2,128]{3,1,2,0:T(4,128)S(1)}, u32[]{:S(2)}, u32[]{:S(2)}) collective-permute-start(f32[3,4,2,128]{3,1,2,0:T(4,128)S(1)} %get-tuple-element.66), channel_id=1, source_target_pairs={{1,0},{2,1},{3,2},{4,3},{5,4},{6,5},{7,6},{9,8},{10,9},{11,10},{12... | collective-permute-start | bytes 36872 | tf_op jit(solution)/shard_map/ppermute | solution.py:25
  121.5 6.5 %collective-permute-start.24 = (f32[3,2,12,128]{3,1,2,0:T(2,128)S(1)}, f32[3,2,12,128]{3,1,2,0:T(2,128)S(1)}, u32[]{:S(2)}, u32[]{:S(2)}) collective-permute-start(f32[3,2,12,128]{3,1,2,0:T(2,128)S(1)} %get-tuple-element.60), channel_id=1, source_target_pairs={{8,0},{16,8},{24,16},{9,1},{17,9},{25,17},{10,2},{18,10},{26,18},{... | collective-permute-start | bytes 110600 | tf_op jit(solution)/shard_map/ppermute | solution.py:25
  122.8 6.4 %collective-permute-start.25 = (f32[3,2,12,128]{3,1,2,0:T(2,128)S(1)}, f32[3,2,12,128]{3,1,2,0:T(2,128)S(1)}, u32[]{:S(2)}, u32[]{:S(2)}) collective-permute-start(f32[3,2,12,128]{3,1,2,0:T(2,128)S(1)} %get-tuple-element.61), channel_id=1, source_target_pairs={{0,8},{8,16},{16,24},{1,9},{9,17},{17,25},{2,10},{10,18},{18,26},{... | collective-permute-start | bytes 110600 | tf_op jit(solution)/shard_map/ppermute | solution.py:22
  129.6 21.3 %copy-start.1 = (f32[3,4,12,128]{3,1,2,0:T(4,128)}, f32[3,4,12,128]{3,1,2,0:T(4,128)S(1)}, u32[]{:S(2)}) copy-start(f32[3,4,12,128]{3,1,2,0:T(4,128)S(1)} %fusion.13) | copy-start | bytes 221188
  129.7 5.6 %collective-permute-start.28 = (f32[3,2,12,128]{3,1,2,0:T(2,128)S(1)}, f32[3,2,12,128]{3,1,2,0:T(2,128)S(1)}, u32[]{:S(2)}, u32[]{:S(2)}) collective-permute-start(f32[3,2,12,128]{3,1,2,0:T(2,128)S(1)} %get-tuple-element.117), channel_id=1, source_target_pairs={{0,8},{8,16},{16,24},{1,9},{9,17},{17,25},{2,10},{10,18},{18,26},{... | collective-permute-start | bytes 110600 | tf_op jit(solution)/shard_map/ppermute | solution.py:22
  133.9 6.4 %collective-permute-start.29 = (f32[3,2,12,128]{3,1,2,0:T(2,128)S(1)}, f32[3,2,12,128]{3,1,2,0:T(2,128)S(1)}, u32[]{:S(2)}, u32[]{:S(2)}) collective-permute-start(f32[3,2,12,128]{3,1,2,0:T(2,128)S(1)} %get-tuple-element.116), channel_id=1, source_target_pairs={{8,0},{16,8},{24,16},{9,1},{17,9},{25,17},{10,2},{18,10},{26,18},{... | collective-permute-start | bytes 110600 | tf_op jit(solution)/shard_map/ppermute | solution.py:25
  140.3 7.3 %collective-permute-start.30 = (f32[3,8,2,128]{3,1,2,0:T(8,128)S(1)}, f32[3,8,2,128]{3,1,2,0:T(8,128)S(1)}, u32[]{:S(2)}, u32[]{:S(2)}) collective-permute-start(f32[3,8,2,128]{3,1,2,0:T(8,128)S(1)} %get-tuple-element.58), channel_id=1, source_target_pairs={{0,1},{1,2},{2,3},{3,4},{4,5},{5,6},{6,7},{8,9},{9,10},{10,11},{11... | collective-permute-start | bytes 73736 | tf_op jit(solution)/shard_map/ppermute | solution.py:22
  145.5 5.1 %collective-permute-start.31 = (f32[3,8,2,128]{3,1,2,0:T(8,128)S(1)}, f32[3,8,2,128]{3,1,2,0:T(8,128)S(1)}, u32[]{:S(2)}, u32[]{:S(2)}) collective-permute-start(f32[3,8,2,128]{3,1,2,0:T(8,128)S(1)} %get-tuple-element.59), channel_id=1, source_target_pairs={{1,0},{2,1},{3,2},{4,3},{5,4},{6,5},{7,6},{9,8},{10,9},{11,10},{12... | collective-permute-start | bytes 73736 | tf_op jit(solution)/shard_map/ppermute | solution.py:25
where the time goes:
time: 157 us; the launch traced here: 155 us
  starting transfers between devices  94.9 us (60%)
  waiting for transfers between devices  33.9 us (22%)
  other arithmetic  15.6 us (10%)
  local copies, waits for them, and re-layouts  8.75 us (6%)
  between operations  1.91 us (1%)
    ppermute x16, starting transfers between devices, with_halo(): lax.ppermute(lax.slice_in_dim(block, block.shape[dim] - width, None, axis...  67.7 us
    ppermute x16, waiting for transfers between devices, with_halo(): lax.ppermute(lax.slice_in_dim(block, 0, width, axis=dim), axis, backward)  30.5 us
    ppermute x16, starting transfers between devices, with_halo(): lax.ppermute(lax.slice_in_dim(block, 0, width, axis=dim), axis, backward)  27.1 us
    scatter-add x4, other arithmetic, shards(): flat.at[normal_rows[:, None], source_cells[None, :]]  4.56 us
    unnamed x25, local copies, waits for them, and re-layouts  3.41 us
    ppermute x16, waiting for transfers between devices, with_halo(): lax.ppermute(lax.slice_in_dim(block, block.shape[dim] - width, None, axis...  3.37 us
    div x4, other arithmetic, plastic(): mean_stress = (trial[0] + trial[4] + trial[5]) / 3.0  3.24 us
  transfers between devices with their start and end apart: 32, of which 11 were waited for; matrix products, arithmetic and copies ran while one was open for 2% of the time, Pallas kernels for 0%

commit v1 on v0

v1 whole, which is shorter than its diff:
```python
import functools

import jax
import jax.numpy as jnp
from jax import lax
from jax.experimental import pallas as pl
from jax.experimental.pallas import tpu as pltpu
from jax.sharding import PartitionSpec as P

BLK = 4
BLKZ = 32
LANES = 128
SUB = 8

inner_coef = 9.0 / 8.0
outer_coef = 1.0 / 24.0
ratio = outer_coef / inner_coef
time_step = 0.08
friction = 0.4

VEL, STR, MEM, COD = 0, 3, 9, 15
FIELDS = 16
NORMAL = (0, 4, 5)


def round_up(value, step):
    return -(-value // step) * step


def pack_kernel(vel, stress, mem, code, scale, cell, amp, out, *, cx, cy):
    plane = cy
    field = cx * cy
    for c in range(3):
        for p in range(cx):
            at = (VEL + c) * field + p * plane
            out[at : at + cy, :] = vel[c, p]
    for c in range(6):
        for p in range(cx):
            at = (STR + c) * field + p * plane
            out[at : at + cy, :] = stress[c, p]
            at = (MEM + c) * field + p * plane
            out[at : at + cy, :] = mem[c, p]
    for p in range(cx):
        at = COD * field + p * plane
        out[at : at + cy, :] = (code[p] + 1).astype(jnp.float32)
    tail = FIELDS * field
    lane = lax.broadcasted_iota(jnp.int32, (1, LANES), 1)
    here = tail
    for i in range(scale.shape[0]):
        for j in range(scale.shape[1]):
            row = jnp.zeros((1, LANES), jnp.float32)
            for k in range(scale.shape[2]):
                row = jnp.where(lane // BLKZ == k, scale[i, j, k], row)
            out[here : here + 1, :] = row
            here += 1
    out[here : out.shape[0], :] = jnp.zeros((out.shape[0] - here, LANES), jnp.float32)
    count, steps = amp.shape[2], amp.shape[3]
    row = jnp.zeros((1, LANES), jnp.float32)
    for k in range(count):
        row = jnp.where(lane == k, cell[0, 0, k].astype(jnp.float32), row)
        for t in range(steps):
            row = jnp.where(lane == count + k * steps + t, amp[0, 0, k, t], row)
    out[out.shape[0] - 1 : out.shape[0], :] = row


def step_kernel(*refs, cx, cy, steps, sources, window, dests, fixed):
    count = 3 * len(dests)
    blocks = refs[:count]
    table, place_ref = refs[count : count + 2]
    out_vel, out_str, out_mem = refs[count + 2 : count + 5]
    vel, stress, mem, codes, scales, buoy, lame, shear, decay, weight, cohesion = refs[
        count + 5 : count + 16
    ]
    points, sem = refs[count + 16 :]
    field = cx * cy
    tail = FIELDS * field
    size = blocks[0].shape[0]
    margin = 4
    rows = codes.shape[1]

    me_we = place_ref[0]
    odd = lax.rem(place_ref[1], 2)
    if fixed is None:
        own = me_we * cx
    else:
        own = fixed

    copies = []
    for b in range(count):
        copy = pltpu.make_async_copy(
            blocks[b].at[size - SUB : size, :], points.at[b * SUB : (b + 1) * SUB, :], sem.at[b]
        )
        copy.start()
        copies.append(copy)

    zero = jnp.zeros((rows, LANES), jnp.float32)
    for p in (0, 1, window + 2, window + 3):
        for c in range(3):
            vel[c, p] = zero
            stress[c, p] = zero

    def base_plane(s):
        if fixed is None:
            return jnp.bitwise_xor(me_we, dests[s]) * cx
        return fixed - dests[s] * cx

    def place(block, plane, row):
        def piece(f, p):
            at = f * field + p * cy
            return block[at : at + cy, :]

        for p in range(cx):
            for c in range(3):
                vel[c, plane + p + 2, pl.ds(row, cy), :] = piece(VEL + c, p)
            for c in range(6):
                stress[c, plane + p + 2, pl.ds(row, cy), :] = piece(STR + c, p)
                mem[c, plane + p, pl.ds(row, cy), :] = piece(MEM + c, p)
            codes[plane + p, pl.ds(row, cy), :] = piece(COD, p)
        across = cy // BLK
        for i in range(cx // BLK):
            for j in range(across):
                at = tail + i * across + j
                line = jnp.broadcast_to(block[at : at + 1, :], (BLK, LANES))
                scales[plane // BLK + i, pl.ds(row + j * BLK, BLK), :] = line

    for s in range(len(dests)):
        plane = base_plane(s)
        center, outer, inner = blocks[3 * s : 3 * s + 3]
        place(center, plane, margin + cy)

        @pl.when(odd == 0)
        def _():
            place(outer, plane, margin)
            place(inner, plane, margin + 2 * cy)

        @pl.when(odd == 1)
        def _():
            place(inner, plane, margin)
            place(outer, plane, margin + 2 * cy)

    def properties(p, carry):
        for r in range(0, rows, SUB):
            index = codes[p, r : r + SUB, :].astype(jnp.int32)
            index = jnp.clip(index, 0, LANES - 1)

            def row_of(k):
                line = jnp.broadcast_to(table[k : k + 1, :], (SUB, LANES))
                return jnp.take_along_axis(line, index, axis=1)

            grow = scales[p // BLK, r : r + SUB, :]
            kept = row_of(3)
            buoy[p, r : r + SUB, :] = row_of(0)
            lame[p, r : r + SUB, :] = row_of(1) * grow
            shear[p, r : r + SUB, :] = row_of(2) * grow
            decay[p, r : r + SUB, :] = kept
            weight[p, r : r + SUB, :] = row_of(4)
            cohesion[p, r : r + SUB, :] = row_of(5)
        return carry

    lax.fori_loop(0, window, properties, 0)
    for copy in copies:
        copy.wait()

    lane = lax.broadcasted_iota(jnp.int32, (SUB, LANES), 1)

    def deep(f, k):
        moved = pltpu.roll(f, (-k) % LANES, 1)
        return jnp.where((lane + k >= 0) & (lane + k < LANES), moved, 0.0)

    def z_back(f):
        return f - deep(f, -1), deep(f, 1) - deep(f, -2)

    def z_fore(f):
        return deep(f, 1) - f, deep(f, 2) - deep(f, -1)

    def add(*pairs):
        one, two = pairs[0]
        for a, b in pairs[1:]:
            one = one + a
            two = two + b
        return one - ratio * two

    def reader(ref, c, p, r):
        def at(dp, dr):
            return ref[c, p + 2 + dp, r + dr : r + dr + SUB, :]

        def x_fore():
            return at(1, 0) - at(0, 0), at(2, 0) - at(-1, 0)

        def x_back():
            return at(0, 0) - at(-1, 0), at(1, 0) - at(-2, 0)

        def y_fore():
            return at(0, 1) - at(0, 0), at(0, 2) - at(0, -1)

        def y_back():
            return at(0, 0) - at(0, -1), at(0, 1) - at(0, -2)

        return at, x_fore, x_back, y_fore, y_back

    def tiles(reach):
        need = cy + 2 * reach
        n = -(-need // SUB)
        start = margin + cy - reach
        return [start + SUB * i for i in range(n)]

    def planes(reach):
        need = min(cx + 2 * reach, window)
        if fixed is not None:
            return fixed - reach, cx + 2 * reach
        devices = window // cx
        need = max(
            min(w * cx + cx + reach, window) - max(w * cx - reach, 0) for w in range(devices)
        )
        return jnp.clip(own - reach, 0, window - need), need

    def velocity_phase(reach):
        first, n = planes(reach)

        def body(i, carry):
            p = first + i
            for r in tiles(reach):
                _, xx_fore, _, _, _ = reader(stress, 0, p, r)
                xz, _, xz_back, _, _ = reader(stress, 1, p, r)
                _, _, xy_xback, _, xy_yback = reader(stress, 2, p, r)
                yz, _, _, _, yz_back = reader(stress, 3, p, r)
                _, _, _, yy_fore, _ = reader(stress, 4, p, r)
                zz, _, _, _, _ = reader(stress, 5, p, r)
                push = buoy[p, r : r + SUB, :]
                forces = (
                    add(xx_fore(), xy_yback(), z_back(xz(0, 0))),
                    add(xy_xback(), yy_fore(), z_back(yz(0, 0))),
                    add(xz_back(), yz_back(), z_fore(zz(0, 0))),
                )
                for c in range(3):
                    vel[c, p + 2, r : r + SUB, :] = vel[c, p + 2, r : r + SUB, :] + push * forces[c]
            return carry

        lax.fori_loop(0, n, body, 0)

    def add_sources(t):
        for s in range(len(dests)):
            plane = base_plane(s)
            for which in range(3):
                b = 3 * s + which
                if which == 0:
                    row = margin + cy
                elif which == 1:
                    row = jnp.where(odd == 0, margin, margin + 2 * cy)
                else:
                    row = jnp.where(odd == 0, margin + 2 * cy, margin)
                for k in range(sources):
                    cell = points[b * SUB + SUB - 1, k].astype(jnp.int32)
                    size_plane = cy * LANES
                    p = plane + cell // size_plane
                    r = row + lax.rem(cell, size_plane) // LANES
                    z = lax.rem(cell, LANES)
                    amount = time_step * points[b * SUB + SUB - 1, sources + k * steps + t]
                    line = jnp.where(lane[0:1] == z, amount, 0.0)
                    for c in NORMAL:
                        stress[c, p + 2, pl.ds(r, 1), :] = stress[c, p + 2, pl.ds(r, 1), :] + line

    def stress_phase(reach, last):
        first, n = planes(reach)

        def body(i, carry):
            p = first + i
            for j, r in enumerate(tiles(reach)):
                ve, _, ve_xback, ve_yfore, _ = reader(vel, 0, p, r)
                vn, vn_xfore, _, _, vn_yback = reader(vel, 1, p, r)
                vd, vd_xfore, _, vd_yfore, _ = reader(vel, 2, p, r)
                exx = add(ve_xback())
                eyy = add(vn_yback())
                ezz = add(z_back(vd(0, 0)))
                exz = add(z_fore(ve(0, 0)), vd_xfore())
                exy = add(ve_yfore(), vn_xfore())
                eyz = add(z_fore(vn(0, 0)), vd_yfore())
                mu = shear[p, r : r + SUB, :]
                twice = mu + mu
                bulk = lame[p, r : r + SUB, :] * (exx + eyy + ezz)
                moves = (
                    bulk + twice * exx,
                    mu * exz,
                    mu * exy,
                    mu * eyz,
                    bulk + twice * eyy,
                    bulk + twice * ezz,
                )
                keep = decay[p, r : r + SUB, :]
                gain = weight[p, r : r + SUB, :]
                trial = []
                rest = []
                for c in range(6):
                    old = mem[c, p, r : r + SUB, :]
                    new = keep * old + gain * moves[c]
                    rest.append(new)
                    now = stress[c, p + 2, r : r + SUB, :]
                    trial.append((now + moves[c]) - (0.5 * time_step) * (old + new))
                mean = (trial[0] + trial[4] + trial[5]) * (1.0 / 3.0)
                dxx, dyy, dzz = trial[0] - mean, trial[4] - mean, trial[5] - mean
                dxz, dxy, dyz = trial[1], trial[2], trial[3]
                second = 0.5 * (dxx * dxx + dyy * dyy + dzz * dzz) + (
                    dxz * dxz + dxy * dxy + dyz * dyz
                )
                soft = jnp.maximum(-mean, 0.0) + jnp.log(1.0 + jnp.exp(-jnp.abs(mean)))
                level = cohesion[p, r : r + SUB, :] + friction * soft
                scaled = second / (level * level)
                factor = lax.rsqrt(jnp.sqrt(1.0 + scaled * scaled))
                done = (
                    mean + factor * dxx,
                    factor * dxz,
                    factor * dxy,
                    factor * dyz,
                    mean + factor * dyy,
                    mean + factor * dzz,
                )
                if last:
                    lo = SUB * j
                    n_rows = min(SUB, cy - lo)
                    now_vel = (ve(0, 0), vn(0, 0), vd(0, 0))
                    for c in range(3):
                        out_vel[c, i, lo : lo + n_rows, :] = now_vel[c][:n_rows]
                    for c in range(6):
                        out_str[c, i, lo : lo + n_rows, :] = done[c][:n_rows]
                        out_mem[c, i, lo : lo + n_rows, :] = rest[c][:n_rows]
                else:
                    for c in range(6):
                        stress[c, p + 2, r : r + SUB, :] = done[c]
                        mem[c, p, r : r + SUB, :] = rest[c]
            return carry

        lax.fori_loop(0, n, body, 0)

    for t in range(steps):
        left = 3 * (steps - 1 - t)
        velocity_phase(left + 2)
        add_sources(t)
        stress_phase(left, t == steps - 1)


def shards(
    velocity, stress, memory, material_code, block_scale, material_table, source_cell, source_amp
):
    _, cx, cy, cz = velocity.shape
    sources, steps = source_amp.shape[2:]
    n_we, n_sn = lax.axis_size("we"), lax.axis_size("sn")
    reach = 3 * steps
    assert cz == LANES and cy >= reach and cx % BLK == 0 and cy % BLK == 0
    assert sources * (steps + 1) <= LANES

    used = FIELDS * cx * cy + (cx // BLK) * (cy // BLK) + 1
    vmem = pl.BlockSpec(memory_space=pltpu.VMEM)
    smem = pl.BlockSpec(memory_space=pltpu.SMEM)
    own = pl.pallas_call(
        functools.partial(pack_kernel, cx=cx, cy=cy),
        out_shape=jax.ShapeDtypeStruct((round_up(used, SUB), LANES), jnp.float32),
        in_specs=[vmem, vmem, vmem, vmem, smem, smem, smem],
        out_specs=vmem,
        name="pack",
    )(velocity, stress, memory, material_code, block_scale, source_cell, source_amp)

    width = -(-reach // cx)
    everything = n_we <= 2 * width + 1 and n_we & (n_we - 1) == 0
    if everything:
        dests = list(range(n_we))
        window, fixed = n_we * cx, None
        moves = [[(i, i ^ k) for i in range(n_we)] for k in dests]
    else:
        dests = [0] + [sign * k for k in range(1, width + 1) for sign in (1, -1)]
        window, fixed = (2 * width + 1) * cx, width * cx
        moves = [[(i, i + k) for i in range(n_we) if 0 <= i + k < n_we] for k in dests]
    inner = [(i, i ^ 1) for i in range(n_sn) if i ^ 1 < n_sn]
    outer = [(i, i - 1 + 2 * (i % 2)) for i in range(n_sn)]
    outer = [(a, b) for a, b in outer if 0 <= b < n_sn]
    blocks = []
    for k, move in zip(dests, moves):
        block = own if k == 0 else lax.ppermute(own, "we", move)
        blocks += [block, lax.ppermute(block, "sn", outer), lax.ppermute(block, "sn", inner)]

    decay = material_table[3]
    per_step = time_step * inner_coef
    table = jnp.stack(
        [
            material_table[0] * per_step,
            material_table[1] * per_step,
            material_table[2] * per_step,
            decay,
            (1.0 - decay) * material_table[4] / time_step,
            material_table[5],
        ]
    )
    table = jnp.pad(table, ((0, 2), (1, LANES - 1 - table.shape[1])))

    place = jnp.stack([lax.axis_index("we"), lax.axis_index("sn")])

    margin = 4
    rows = round_up(3 * cy + 2 * margin, SUB) + SUB
    frame = pltpu.VMEM((window, rows, LANES), jnp.float32)

    def frames(n, extra):
        return pltpu.VMEM((n, window + extra, rows, LANES), jnp.float32)

    count = len(blocks)
    return pl.pallas_call(
        functools.partial(
            step_kernel,
            cx=cx,
            cy=cy,
            steps=steps,
            sources=sources,
            window=window,
            dests=dests,
            fixed=fixed,
        ),
        out_shape=[
            jax.ShapeDtypeStruct(velocity.shape, jnp.float32),
            jax.ShapeDtypeStruct(stress.shape, jnp.float32),
            jax.ShapeDtypeStruct(memory.shape, jnp.float32),
        ],
        in_specs=[vmem] * (count + 1) + [smem],
        out_specs=[vmem] * 3,
        scratch_shapes=[
            frames(3, 4),
            frames(6, 4),
            frames(6, 0),
            frame,
            pltpu.VMEM((window // BLK, rows, LANES), jnp.float32),
            frame,
            frame,
            frame,
            frame,
            frame,
            frame,
            pltpu.SMEM((count * SUB, LANES), jnp.float32),
            pltpu.SemaphoreType.DMA((count,)),
        ],
        compiler_params=pltpu.CompilerParams(vmem_limit_bytes=40 << 20),
        name="steps",
    )(*blocks, table, place)


def solution(mesh):
    in_specs = (
        P(None, "we", "sn", None),
        P(None, "we", "sn", None),
        P(None, "we", "sn", None),
        P("we", "sn", None),
        P("we", "sn", None),
        P(),
        P("we", "sn", None),
        P("we", "sn", None, None),
    )
    out_specs = (P(None, "we", "sn", None), P(None, "we", "sn", None), P(None, "we", "sn", None))
    return jax.shard_map(shards, mesh=mesh, in_specs=in_specs, out_specs=out_specs, check_vma=False)
```

time: 157 us -> 70.7 us (0.45)
  starting transfers between devices: 94.9 us -> 21.2 us
  Pallas kernels: 0 us -> 21.4 us
  waiting for transfers between devices: 33.9 us -> 17.1 us
  other arithmetic: 15.6 us -> 0.08 us
    ppermute x32 -> x11, starting transfers between devices: 94.9 us -> 21.2 us  [the longest x4 14.5 us: shards(): lax.ppermute(block, 'sn', outer)]
    pallas_call x0 -> x2, Pallas kernels: none -> 21.4 us  [the longest x1 19.5 us: shards(): pl.pallas_call(functools.partial(step_kernel, cx=cx, cy=cy, steps=steps,...]
    ppermute x32 -> x11, waiting for transfers between devices: 33.9 us -> 17.1 us  [the longest x3 11.2 us: shards(): block = own if k == 0 else lax.ppermute(own, 'we', move)]
    scatter-add x4 -> x0, other arithmetic: 4.56 us -> none  [shards(): flat.at[normal_rows[:, None], source_cells[None, :]]]
    unnamed x25 -> x13, local copies, waits for them, and re-layouts: 3.41 us -> 7.54 us
    div x4 -> x0, other arithmetic: 3.24 us -> none  [plastic(): mean_stress = (trial[0] + trial[4] + trial[5]) / 3.0]
    add x12 -> x0, other arithmetic: 2.67 us -> none  [the longest x4 1.3 us: stress_step(): trial = stress + time_step * (rates - 0.5 * (memory + memory_new))]
    slice x16 -> x0, local copies, waits for them, and re-layouts: 2.1 us -> none  [the longest x8 1.21 us: with_halo(): lax.slice_in_dim(block, 0, width, axis=dim)]
  transfers between devices with their start and end apart: 32 -> 11, of which waited for: 11 -> 4; matrix products, arithmetic and copies ran while one was open for 2% -> 0% of each run, Pallas kernels for 0% -> 0%
where the time goes in v1:
time: 70.7 us; the launch traced here: 70.3 us
  Pallas kernels  21.4 us (30%)
  starting transfers between devices  21.2 us (30%)
  waiting for transfers between devices  17.1 us (24%)
  local copies, waits for them, and re-layouts  9.74 us (14%)
  between operations  0.75 us (1%)
    pallas_call x1, Pallas kernels, shards(): pl.pallas_call(functools.partial(step_kernel, cx=cx, cy=cy, steps=steps,...  19.5 us
    ppermute x4, starting transfers between devices, shards(): lax.ppermute(block, 'sn', outer)  14.5 us
    ppermute x3, waiting for transfers between devices, shards(): block = own if k == 0 else lax.ppermute(own, 'we', move)  11.2 us
    unnamed x13, local copies, waits for them, and re-layouts  7.54 us
    ppermute x4, waiting for transfers between devices, shards(): lax.ppermute(block, 'sn', outer)  5.87 us
    ppermute x4, starting transfers between devices, shards(): lax.ppermute(block, 'sn', inner)  3.48 us
    ppermute x3, starting transfers between devices, shards(): block = own if k == 0 else lax.ppermute(own, 'we', move)  3.27 us
    pallas_call x3, local copies, waits for them, and re-layouts, shards(): pl.pallas_call(functools.partial(step_kernel, cx=cx, cy=cy, steps=steps,...  2.1 us
  transfers between devices with their start and end apart: 11, of which 4 were waited for; matrix products, arithmetic and copies ran while one was open for 0% of the time, Pallas kernels for 0%

profile of v1, /device:TPU:1, one launch (start us, length us, event | category | flops | bytes accessed | tf_op | source)
XLA Modules:
  0.0 70.3 jit_solution(4818998271335072815)
XLA Ops:
  0.6 0.0 copy-start.1
  0.6 1.3 %copy.15.scale = f32[1,3,4]{2,1,0:T(4,128)} copy(f32[1,3,4]{2,0,1:T(1,128)} %param.12) | data formatting | bytes 96 | tf_op args[4]
  1.9 1.4 %copy.14.code = s32[4,12,128]{2,1,0:T(8,128)} copy(s32[4,12,128]{2,0,1:T(4,128)} %param.11) | data formatting | bytes 49152 | tf_op args[3]
  3.3 1.5 %copy.11.vel = f32[3,4,12,128]{3,2,1,0:T(8,128)} copy(f32[3,4,12,128]{3,1,2,0:T(4,128)} %param.8) | data formatting | bytes 147456 | tf_op args[0]
  4.8 0.0 copy-done.1
  4.8 0.0 copy-start.2
  4.8 0.7 copy.12.stress
  5.5 0.3 copy-done.2
  5.8 0.7 copy.13.mem
  6.5 1.9 %pack.1.refs_0_ = f32[776,128]{1,0:T(8,128)} custom-call(f32[3,4,12,128]{3,2,1,0:T(8,128)} %copy.11.vel, f32[6,4,12,128]{3,2,1,0:T(8,128)} %copy.12.stress, f32[6,4,12,128]{3,2,1,0:T(8,128)} %copy.13.mem, s32[4,12,128]{2,1,0:T(8,128)} %copy.14.code, f32[1,3,4]{2,1,0:T(4,128)} %copy.15.scale, s32[1,1,4]{2,1,0:T(1,128)} %cell.1, f32[1,1,4,4]{3,2,1,0:T(4,128)} %amp.1), custom_call_target="tpu_custom_call" | custom-call | tf_op jit(solution)/shard_map/pack/pallas_call | solution.py:354
  8.4 3.0 %collective-permute-start.8 = (f32[776,128]{1,0:T(8,128)}, f32[776,128]{1,0:T(8,128)S(1)}, u32[]{:S(2)}, u32[]{:S(2)}) collective-permute-start(f32[776,128]{1,0:T(8,128)} %pack.1.refs_0_), channel_id=1, source_target_pairs={{0,24},{8,16},{16,8},{24,0},{1,25},{9,17},{17,9},{25,1},{2,26},{10... | collective-permute-start | bytes 1191944 | tf_op jit(solution)/shard_map/ppermute | solution.py:377
  11.4 0.2 collective-permute-start.5
  11.6 0.1 collective-permute-start.2
  11.7 1.2 %collective-permute-start.1 = (f32[776,128]{1,0:T(8,128)}, f32[776,128]{1,0:T(8,128)S(1)}, u32[]{:S(2)}, u32[]{:S(2)}) collective-permute-start(f32[776,128]{1,0:T(8,128)} %pack.1.refs_0_), channel_id=1, source_target_pairs={{0,1},{1,0},{2,3},{3,2},{4,5},{5,4},{6,7},{7,6},{8,9},{9,8},{10,11... | collective-permute-start | bytes 1191944 | tf_op jit(solution)/shard_map/ppermute | solution.py:378
  12.9 3.6 %collective-permute-start = (f32[776,128]{1,0:T(8,128)}, f32[776,128]{1,0:T(8,128)S(1)}, u32[]{:S(2)}, u32[]{:S(2)}) collective-permute-start(f32[776,128]{1,0:T(8,128)} %pack.1.refs_0_), channel_id=1, source_target_pairs={{1,2},{2,1},{3,4},{4,3},{5,6},{6,5},{9,10},{10,9},{11,12},{12,11},... | collective-permute-start | bytes 1191944 | tf_op jit(solution)/shard_map/ppermute | solution.py:378
  16.5 4.1 %collective-permute-done.8.refs_9_ = f32[776,128]{1,0:T(8,128)S(1)} collective-permute-done((f32[776,128]{1,0:T(8,128)}, f32[776,128]{1,0:T(8,128)S(1)}, u32[]{:S(2)}, u32[]{:S(2)}) %collective-permute-start.8) | collective-permute-done | bytes 397344 | tf_op jit(solution)/shard_map/ppermute | solution.py:377
  20.5 2.1 %collective-permute-start.10 = (f32[776,128]{1,0:T(8,128)S(1)}, f32[776,128]{1,0:T(8,128)S(1)}, u32[]{:S(2)}, u32[]{:S(2)}) collective-permute-start(f32[776,128]{1,0:T(8,128)S(1)} %collective-permute-done.8.refs_9_), channel_id=1, source_target_pairs={{0,1},{1,0},{2,3},{3,2},{4,5},{5,4},{6,7},{7,6},{8,9},{9,8},{10,11... | collective-permute-start | bytes 1191944 | tf_op jit(solution)/shard_map/ppermute | solution.py:378
  22.6 7.1 %collective-permute-done.5.refs_6_ = f32[776,128]{1,0:T(8,128)S(1)} collective-permute-done((f32[776,128]{1,0:T(8,128)}, f32[776,128]{1,0:T(8,128)S(1)}, u32[]{:S(2)}, u32[]{:S(2)}) %collective-permute-start.5) | collective-permute-done | bytes 397344 | tf_op jit(solution)/shard_map/ppermute | solution.py:377
  29.8 3.8 %collective-permute-start.9 = (f32[776,128]{1,0:T(8,128)S(1)}, f32[776,128]{1,0:T(8,128)S(1)}, u32[]{:S(2)}, u32[]{:S(2)}) collective-permute-start(f32[776,128]{1,0:T(8,128)S(1)} %collective-permute-done.8.refs_9_), channel_id=1, source_target_pairs={{1,2},{2,1},{3,4},{4,3},{5,6},{6,5},{9,10},{10,9},{11,12},{12,11},... | collective-permute-start | bytes 1191944 | tf_op jit(solution)/shard_map/ppermute | solution.py:378
  33.5 0.0 collective-permute-done.2.refs_3_
  33.5 0.1 collective-permute-start.7
  33.6 0.0 collective-permute-done.1.refs_2_
  33.6 3.6 %collective-permute-start.6 = (f32[776,128]{1,0:T(8,128)S(1)}, f32[776,128]{1,0:T(8,128)}, u32[]{:S(2)}, u32[]{:S(2)}) collective-permute-start(f32[776,128]{1,0:T(8,128)S(1)} %collective-permute-done.5.refs_6_), channel_id=1, source_target_pairs={{1,2},{2,1},{3,4},{4,3},{5,6},{6,5},{9,10},{10,9},{11,12},{12,11},... | collective-permute-start | bytes 1191944 | tf_op jit(solution)/shard_map/ppermute | solution.py:378
  37.2 0.0 collective-permute-done.refs_1_
  37.2 0.1 collective-permute-start.4
  37.3 0.0 collective-permute-done.10.refs_11_
  37.3 3.6 %collective-permute-start.3 = (f32[776,128]{1,0:T(8,128)S(1)}, f32[776,128]{1,0:T(8,128)}, u32[]{:S(2)}, u32[]{:S(2)}) collective-permute-start(f32[776,128]{1,0:T(8,128)S(1)} %collective-permute-done.2.refs_3_), channel_id=1, source_target_pairs={{1,2},{2,1},{3,4},{4,3},{5,6},{6,5},{9,10},{10,9},{11,12},{12,11},... | collective-permute-start | bytes 1191944 | tf_op jit(solution)/shard_map/ppermute | solution.py:378
  40.9 0.0 copy-start.3
  40.9 0.7 copy-done.3
  41.6 0.1 pad.4.refs_12_
  41.7 0.1 pad_add_fusion.refs_13_
  41.8 0.0 collective-permute-done.9.refs_10_
  41.8 0.0 collective-permute-done.7.refs_8_
  41.8 1.6 %collective-permute-done.6.refs_7_ = f32[776,128]{1,0:T(8,128)} collective-permute-done((f32[776,128]{1,0:T(8,128)S(1)}, f32[776,128]{1,0:T(8,128)}, u32[]{:S(2)}, u32[]{:S(2)}) %collective-permute-start.6) | collective-permute-done | bytes 397344 | tf_op jit(solution)/shard_map/ppermute | solution.py:378
  43.4 0.0 collective-permute-done.4.refs_5_
  43.4 4.3 %collective-permute-done.3.refs_4_ = f32[776,128]{1,0:T(8,128)} collective-permute-done((f32[776,128]{1,0:T(8,128)S(1)}, f32[776,128]{1,0:T(8,128)}, u32[]{:S(2)}, u32[]{:S(2)}) %collective-permute-start.3) | collective-permute-done | bytes 397344 | tf_op jit(solution)/shard_map/ppermute | solution.py:378
  47.6 0.0 copy-start
  47.7 1.0 %copy-done = f32[776,128]{1,0:T(8,128)S(1)} copy-done((f32[776,128]{1,0:T(8,128)S(1)}, f32[776,128]{1,0:T(8,128)}, u32[]{:S(2)}) %copy-start) | copy-done | bytes 397336
  48.6 19.5 %steps.1 = (f32[3,4,12,128]{3,2,1,0:T(8,128)S(1)}, f32[6,4,12,128]{3,2,1,0:T(8,128)S(1)}, f32[6,4,12,128]{3,2,1,0:T(8,128)S(1)}) custom-call(f32[776,128]{1,0:T(8,128)S(1)} %copy-done, f32[776,128]{1,0:T(8,128)S(1)} %collective-permute-done.refs_1_, f32[776,128]{1,0:T(8,128)S(1)} %collective-permute-done.1.refs_2_, ...), custom_call_target="tpu_custom_call" | custom-call | tf_op jit(solution)/shard_map/steps/pallas_call | solution.py:404
  68.2 0.7 copy.16
  68.9 0.7 %copy.17 = f32[6,4,12,128]{3,1,2,0:T(4,128)} copy(f32[6,4,12,128]{3,2,1,0:T(8,128)S(1)} %get-tuple-element.4) | data formatting | bytes 294912 | tf_op jit(solution)/shard_map/steps/pallas_call | solution.py:404
  69.6 0.7 %copy.18 = f32[6,4,12,128]{3,1,2,0:T(4,128)} copy(f32[6,4,12,128]{3,2,1,0:T(8,128)S(1)} %get-tuple-element.5) | data formatting | bytes 294912 | tf_op jit(solution)/shard_map/steps/pallas_call | solution.py:404
  (2 shorter events, 0.0 us)
Async XLA Ops:
  0.6 4.2 %copy-start.1 = (f32[6,4,12,128]{3,1,2,0:T(4,128)S(1)}, f32[6,4,12,128]{3,1,2,0:T(4,128)}, u32[]{:S(2)}) copy-start(f32[6,4,12,128]{3,1,2,0:T(4,128)} %param.9) | copy-start | bytes 442372
  4.8 1.0 %copy-start.2 = (f32[6,4,12,128]{3,1,2,0:T(4,128)S(1)}, f32[6,4,12,128]{3,1,2,0:T(4,128)}, u32[]{:S(2)}) copy-start(f32[6,4,12,128]{3,1,2,0:T(4,128)} %param.10) | copy-start | bytes 442372
  8.4 12.1 %collective-permute-start.8 = (f32[776,128]{1,0:T(8,128)}, f32[776,128]{1,0:T(8,128)S(1)}, u32[]{:S(2)}, u32[]{:S(2)}) collective-permute-start(f32[776,128]{1,0:T(8,128)} %pack.1.refs_0_), channel_id=1, source_target_pairs={{0,24},{8,16},{16,8},{24,0},{1,25},{9,17},{17,9},{25,1},{2,26},{10... | collective-permute-start | bytes 1191944 | tf_op jit(solution)/shard_map/ppermute | solution.py:377
  11.4 18.4 %collective-permute-start.5 = (f32[776,128]{1,0:T(8,128)}, f32[776,128]{1,0:T(8,128)S(1)}, u32[]{:S(2)}, u32[]{:S(2)}) collective-permute-start(f32[776,128]{1,0:T(8,128)} %pack.1.refs_0_), channel_id=1, source_target_pairs={{0,16},{8,24},{16,0},{24,8},{1,17},{9,25},{17,1},{25,9},{2,18},{10... | collective-permute-start | bytes 1191944 | tf_op jit(solution)/shard_map/ppermute | solution.py:377
  11.6 21.9 %collective-permute-start.2 = (f32[776,128]{1,0:T(8,128)}, f32[776,128]{1,0:T(8,128)S(1)}, u32[]{:S(2)}, u32[]{:S(2)}) collective-permute-start(f32[776,128]{1,0:T(8,128)} %pack.1.refs_0_), channel_id=1, source_target_pairs={{0,8},{8,0},{16,24},{24,16},{1,9},{9,1},{17,25},{25,17},{2,10},{10... | collective-permute-start | bytes 1191944 | tf_op jit(solution)/shard_map/ppermute | solution.py:377
  11.7 22.0 %collective-permute-start.1 = (f32[776,128]{1,0:T(8,128)}, f32[776,128]{1,0:T(8,128)S(1)}, u32[]{:S(2)}, u32[]{:S(2)}) collective-permute-start(f32[776,128]{1,0:T(8,128)} %pack.1.refs_0_), channel_id=1, source_target_pairs={{0,1},{1,0},{2,3},{3,2},{4,5},{5,4},{6,7},{7,6},{8,9},{9,8},{10,11... | collective-permute-start | bytes 1191944 | tf_op jit(solution)/shard_map/ppermute | solution.py:378
  12.9 24.3 %collective-permute-start = (f32[776,128]{1,0:T(8,128)}, f32[776,128]{1,0:T(8,128)S(1)}, u32[]{:S(2)}, u32[]{:S(2)}) collective-permute-start(f32[776,128]{1,0:T(8,128)} %pack.1.refs_0_), channel_id=1, source_target_pairs={{1,2},{2,1},{3,4},{4,3},{5,6},{6,5},{9,10},{10,9},{11,12},{12,11},... | collective-permute-start | bytes 1191944 | tf_op jit(solution)/shard_map/ppermute | solution.py:378
  20.5 16.8 %collective-permute-start.10 = (f32[776,128]{1,0:T(8,128)S(1)}, f32[776,128]{1,0:T(8,128)S(1)}, u32[]{:S(2)}, u32[]{:S(2)}) collective-permute-start(f32[776,128]{1,0:T(8,128)S(1)} %collective-permute-done.8.refs_9_), channel_id=1, source_target_pairs={{0,1},{1,0},{2,3},{3,2},{4,5},{5,4},{6,7},{7,6},{8,9},{9,8},{10,11... | collective-permute-start | bytes 1191944 | tf_op jit(solution)/shard_map/ppermute | solution.py:378
  29.8 12.0 %collective-permute-start.9 = (f32[776,128]{1,0:T(8,128)S(1)}, f32[776,128]{1,0:T(8,128)S(1)}, u32[]{:S(2)}, u32[]{:S(2)}) collective-permute-start(f32[776,128]{1,0:T(8,128)S(1)} %collective-permute-done.8.refs_9_), channel_id=1, source_target_pairs={{1,2},{2,1},{3,4},{4,3},{5,6},{6,5},{9,10},{10,9},{11,12},{12,11},... | collective-permute-start | bytes 1191944 | tf_op jit(solution)/shard_map/ppermute | solution.py:378
  33.5 8.2 %collective-permute-start.7 = (f32[776,128]{1,0:T(8,128)S(1)}, f32[776,128]{1,0:T(8,128)S(1)}, u32[]{:S(2)}, u32[]{:S(2)}) collective-permute-start(f32[776,128]{1,0:T(8,128)S(1)} %collective-permute-done.5.refs_6_), channel_id=1, source_target_pairs={{0,1},{1,0},{2,3},{3,2},{4,5},{5,4},{6,7},{7,6},{8,9},{9,8},{10,11... | collective-permute-start | bytes 1191944 | tf_op jit(solution)/shard_map/ppermute | solution.py:378
  33.6 9.8 %collective-permute-start.6 = (f32[776,128]{1,0:T(8,128)S(1)}, f32[776,128]{1,0:T(8,128)}, u32[]{:S(2)}, u32[]{:S(2)}) collective-permute-start(f32[776,128]{1,0:T(8,128)S(1)} %collective-permute-done.5.refs_6_), channel_id=1, source_target_pairs={{1,2},{2,1},{3,4},{4,3},{5,6},{6,5},{9,10},{10,9},{11,12},{12,11},... | collective-permute-start | bytes 1191944 | tf_op jit(solution)/shard_map/ppermute | solution.py:378
  37.2 6.2 %collective-permute-start.4 = (f32[776,128]{1,0:T(8,128)S(1)}, f32[776,128]{1,0:T(8,128)}, u32[]{:S(2)}, u32[]{:S(2)}) collective-permute-start(f32[776,128]{1,0:T(8,128)S(1)} %collective-permute-done.2.refs_3_), channel_id=1, source_target_pairs={{0,1},{1,0},{2,3},{3,2},{4,5},{5,4},{6,7},{7,6},{8,9},{9,8},{10,11... | collective-permute-start | bytes 1191944 | tf_op jit(solution)/shard_map/ppermute | solution.py:378
  37.3 10.3 %collective-permute-start.3 = (f32[776,128]{1,0:T(8,128)S(1)}, f32[776,128]{1,0:T(8,128)}, u32[]{:S(2)}, u32[]{:S(2)}) collective-permute-start(f32[776,128]{1,0:T(8,128)S(1)} %collective-permute-done.2.refs_3_), channel_id=1, source_target_pairs={{1,2},{2,1},{3,4},{4,3},{5,6},{6,5},{9,10},{10,9},{11,12},{12,11},... | collective-permute-start | bytes 1191944 | tf_op jit(solution)/shard_map/ppermute | solution.py:378
  40.9 0.7 copy-start.3
  47.6 1.0 %copy-start = (f32[776,128]{1,0:T(8,128)S(1)}, f32[776,128]{1,0:T(8,128)}, u32[]{:S(2)}) copy-start(f32[776,128]{1,0:T(8,128)} %pack.1.refs_0_) | copy-start | bytes 1191940

commit v2 on v1

--- a/solution.py
+++ b/solution.py
@@ -27,40 +27,34 @@
     return -(-value // step) * step
 
 
-def pack_kernel(vel, stress, mem, code, scale, cell, amp, out, *, cx, cy):
-    plane = cy
-    field = cx * cy
-    for c in range(3):
-        for p in range(cx):
-            at = (VEL + c) * field + p * plane
-            out[at : at + cy, :] = vel[c, p]
-    for c in range(6):
-        for p in range(cx):
-            at = (STR + c) * field + p * plane
-            out[at : at + cy, :] = stress[c, p]
-            at = (MEM + c) * field + p * plane
-            out[at : at + cy, :] = mem[c, p]
-    for p in range(cx):
-        at = COD * field + p * plane
-        out[at : at + cy, :] = (code[p] + 1).astype(jnp.float32)
-    tail = FIELDS * field
+def pack_kernel(vel, stress, mem, code, scale, cell, amp, out, sem, *, field):
+    copies = []
+    for i, (at, part) in enumerate(((VEL, vel), (STR, stress), (MEM, mem))):
+        to = out.at[pl.ds(at * field, part.shape[0]), :]
+        copies.append(pltpu.make_async_copy(part, to, sem.at[i]))
+        copies[-1].start()
+    out[COD * field : (COD + 1) * field, :] = (code[...] + 1).astype(jnp.float32)
     lane = lax.broadcasted_iota(jnp.int32, (1, LANES), 1)
-    here = tail
-    for i in range(scale.shape[0]):
-        for j in range(scale.shape[1]):
+    here = FIELDS * field
+    for i in range(scale.shape[1]):
+        for j in range(scale.shape[0]):
             row = jnp.zeros((1, LANES), jnp.float32)
             for k in range(scale.shape[2]):
-                row = jnp.where(lane // BLKZ == k, scale[i, j, k], row)
+                row = jnp.where(lane // BLKZ == k, scale[j, i, k], row)
             out[here : here + 1, :] = row
             here += 1
-    out[here : out.shape[0], :] = jnp.zeros((out.shape[0] - here, LANES), jnp.float32)
+    size = out.shape[0]
+    if here < size - 1:
+        out[here : size - 1, :] = jnp.zeros((size - 1 - here, LANES), jnp.float32)
     count, steps = amp.shape[2], amp.shape[3]
     row = jnp.zeros((1, LANES), jnp.float32)
     for k in range(count):
         row = jnp.where(lane == k, cell[0, 0, k].astype(jnp.float32), row)
         for t in range(steps):
-            row = jnp.where(lane == count + k * steps + t, amp[0, 0, k, t], row)
-    out[out.shape[0] - 1 : out.shape[0], :] = row
+            row = jnp.where(lane == count + k * steps + t, time_step * amp[0, 0, k, t], row)
+    out[size - 1 : size, :] = row
+    for copy in copies:
+        copy.wait()
 
 
 def step_kernel(*refs, cx, cy, steps, sources, window, dests, fixed):
@@ -68,10 +62,9 @@
     blocks = refs[:count]
     table, place_ref = refs[count : count + 2]
     out_vel, out_str, out_mem = refs[count + 2 : count + 5]
-    vel, stress, mem, codes, scales, buoy, lame, shear, decay, weight, cohesion = refs[
-        count + 5 : count + 16
+    vel, stress, mem, codes, scales, buoy, lame, shear, decay, weight, cohesion, push_in = refs[
+        count + 5 :
     ]
-    points, sem = refs[count + 16 :]
     field = cx * cy
     tail = FIELDS * field
     size = blocks[0].shape[0]
@@ -85,14 +78,6 @@
     else:
         own = fixed
 
-    copies = []
-    for b in range(count):
-        copy = pltpu.make_async_copy(
-            blocks[b].at[size - SUB : size, :], points.at[b * SUB : (b + 1) * SUB, :], sem.at[b]
-        )
-        copy.start()
-        copies.append(copy)
-
     zero = jnp.zeros((rows, LANES), jnp.float32)
     for p in (0, 1, window + 2, window + 3):
         for c in range(3):
@@ -106,8 +91,13 @@
 
     def place(block, plane, row):
         def piece(f, p):
-            at = f * field + p * cy
-            return block[at : at + cy, :]
+            return block[pl.ds(f * field + p, cy, stride=cx), :]
+
+        line = block[size - 1 : size, :]
+        shape = (cy, LANES)
+        spot = [jnp.broadcast_to(line[:, k : k + 1], shape) for k in range(sources * (1 + steps))]
+        number = lax.broadcasted_iota(jnp.int32, shape, 0) * LANES
+        number = (number + lax.broadcasted_iota(jnp.int32, shape, 1)).astype(jnp.float32)
 
         for p in range(cx):
             for c in range(3):
@@ -116,12 +106,18 @@
                 stress[c, plane + p + 2, pl.ds(row, cy), :] = piece(STR + c, p)
                 mem[c, plane + p, pl.ds(row, cy), :] = piece(MEM + c, p)
             codes[plane + p, pl.ds(row, cy), :] = piece(COD, p)
+            hits = [spot[k] == number + float(p * cy * LANES) for k in range(sources)]
+            for t in range(steps):
+                total = jnp.zeros(shape, jnp.float32)
+                for k in range(sources):
+                    total = total + jnp.where(hits[k], spot[sources + k * steps + t], 0.0)
+                push_in[t, plane + p, pl.ds(row, cy), :] = total
         across = cy // BLK
         for i in range(cx // BLK):
             for j in range(across):
                 at = tail + i * across + j
-                line = jnp.broadcast_to(block[at : at + 1, :], (BLK, LANES))
-                scales[plane // BLK + i, pl.ds(row + j * BLK, BLK), :] = line
+                wide = jnp.broadcast_to(block[at : at + 1, :], (BLK, LANES))
+                scales[plane // BLK + i, pl.ds(row + j * BLK, BLK), :] = wide
 
     for s in range(len(dests)):
         plane = base_plane(s)
@@ -158,8 +154,6 @@
         return carry
 
     lax.fori_loop(0, window, properties, 0)
-    for copy in copies:
-        copy.wait()
 
     lane = lax.broadcasted_iota(jnp.int32, (SUB, LANES), 1)
 
@@ -238,29 +232,7 @@
 
         lax.fori_loop(0, n, body, 0)
 
-    def add_sources(t):
-        for s in range(len(dests)):
-            plane = base_plane(s)
-            for which in range(3):
-                b = 3 * s + which
-                if which == 0:
-                    row = margin + cy
-                elif which == 1:
-                    row = jnp.where(odd == 0, margin, margin + 2 * cy)
-                else:
-                    row = jnp.where(odd == 0, margin + 2 * cy, margin)
-                for k in range(sources):
-                    cell = points[b * SUB + SUB - 1, k].astype(jnp.int32)
-                    size_plane = cy * LANES
-                    p = plane + cell // size_plane
-                    r = row + lax.rem(cell, size_plane) // LANES
-                    z = lax.rem(cell, LANES)
-                    amount = time_step * points[b * SUB + SUB - 1, sources + k * steps + t]
-                    line = jnp.where(lane[0:1] == z, amount, 0.0)
-                    for c in NORMAL:
-                        stress[c, p + 2, pl.ds(r, 1), :] = stress[c, p + 2, pl.ds(r, 1), :] + line
-
-    def stress_phase(reach, last):
+    def stress_phase(reach, t):
         first, n = planes(reach)
 
         def body(i, carry):
@@ -288,6 +260,7 @@
                 )
                 keep = decay[p, r : r + SUB, :]
                 gain = weight[p, r : r + SUB, :]
+                source = push_in[t, p, r : r + SUB, :]
                 trial = []
                 rest = []
                 for c in range(6):
@@ -295,6 +268,8 @@
                     new = keep * old + gain * moves[c]
                     rest.append(new)
                     now = stress[c, p + 2, r : r + SUB, :]
+                    if c in NORMAL:
+                        now = now + source
                     trial.append((now + moves[c]) - (0.5 * time_step) * (old + new))
                 mean = (trial[0] + trial[4] + trial[5]) * (1.0 / 3.0)
                 dxx, dyy, dzz = trial[0] - mean, trial[4] - mean, trial[5] - mean
@@ -314,15 +289,20 @@
                     mean + factor * dyy,
                     mean + factor * dzz,
                 )
-                if last:
+                if t == steps - 1:
                     lo = SUB * j
                     n_rows = min(SUB, cy - lo)
                     now_vel = (ve(0, 0), vn(0, 0), vd(0, 0))
+
+                    def put(out, c, value):
+                        at = c * field + lo * cx + i
+                        out[pl.ds(at, n_rows, stride=cx), :] = value[:n_rows]
+
                     for c in range(3):
-                        out_vel[c, i, lo : lo + n_rows, :] = now_vel[c][:n_rows]
+                        put(out_vel, c, now_vel[c])
                     for c in range(6):
-                        out_str[c, i, lo : lo + n_rows, :] = done[c][:n_rows]
-                        out_mem[c, i, lo : lo + n_rows, :] = rest[c][:n_rows]
+                        put(out_str, c, done[c])
+                        put(out_mem, c, rest[c])
                 else:
                     for c in range(6):
                         stress[c, p + 2, r : r + SUB, :] = done[c]
@@ -334,8 +314,7 @@
     for t in range(steps):
         left = 3 * (steps - 1 - t)
         velocity_phase(left + 2)
-        add_sources(t)
-        stress_phase(left, t == steps - 1)
+        stress_phase(left, t)
 
 
 def shards(
@@ -351,13 +330,27 @@
     used = FIELDS * cx * cy + (cx // BLK) * (cy // BLK) + 1
     vmem = pl.BlockSpec(memory_space=pltpu.VMEM)
     smem = pl.BlockSpec(memory_space=pltpu.SMEM)
+    anywhere = pl.BlockSpec(memory_space=pl.ANY)
+
+    def flat(x):
+        return jnp.swapaxes(x, -3, -2).reshape(-1, LANES)
+
     own = pl.pallas_call(
-        functools.partial(pack_kernel, cx=cx, cy=cy),
+        functools.partial(pack_kernel, field=cx * cy),
         out_shape=jax.ShapeDtypeStruct((round_up(used, SUB), LANES), jnp.float32),
-        in_specs=[vmem, vmem, vmem, vmem, smem, smem, smem],
+        in_specs=[anywhere, anywhere, anywhere, vmem, smem, smem, smem],
         out_specs=vmem,
+        scratch_shapes=[pltpu.SemaphoreType.DMA((3,))],
         name="pack",
-    )(velocity, stress, memory, material_code, block_scale, source_cell, source_amp)
+    )(
+        flat(velocity),
+        flat(stress),
+        flat(memory),
+        flat(material_code),
+        jnp.swapaxes(block_scale, 0, 1),
+        source_cell,
+        source_amp,
+    )
 
     width = -(-reach // cx)
     everything = n_we <= 2 * width + 1 and n_we & (n_we - 1) == 0
@@ -394,14 +387,15 @@
     place = jnp.stack([lax.axis_index("we"), lax.axis_index("sn")])
 
     margin = 4
-    rows = round_up(3 * cy + 2 * margin, SUB) + SUB
+    low = margin + cy - reach + 1
+    rows = round_up(low + round_up(cy + 2 * reach - 2, SUB) + 2, SUB)
     frame = pltpu.VMEM((window, rows, LANES), jnp.float32)
 
     def frames(n, extra):
         return pltpu.VMEM((n, window + extra, rows, LANES), jnp.float32)
 
     count = len(blocks)
-    return pl.pallas_call(
+    outs = pl.pallas_call(
         functools.partial(
             step_kernel,
             cx=cx,
@@ -413,9 +407,7 @@
             fixed=fixed,
         ),
         out_shape=[
-            jax.ShapeDtypeStruct(velocity.shape, jnp.float32),
-            jax.ShapeDtypeStruct(stress.shape, jnp.float32),
-            jax.ShapeDtypeStruct(memory.shape, jnp.float32),
+            jax.ShapeDtypeStruct((n * cx * cy, LANES), jnp.float32) for n in (3, 6, 6)
         ],
         in_specs=[vmem] * (count + 1) + [smem],
         out_specs=[vmem] * 3,
@@ -431,12 +423,12 @@
             frame,
             frame,
             frame,
-            pltpu.SMEM((count * SUB, LANES), jnp.float32),
-            pltpu.SemaphoreType.DMA((count,)),
+            frames(steps, 0),
         ],
         compiler_params=pltpu.CompilerParams(vmem_limit_bytes=40 << 20),
         name="steps",
     )(*blocks, table, place)
+    return tuple(jnp.swapaxes(x.reshape(-1, cy, cx, cz), 1, 2) for x in outs)
 
 
 def solution(mesh):

time: 70.7 us -> 62.2 us (0.88)
  local copies, waits for them, and re-layouts: 9.74 us -> 1.78 us
    unnamed x13 -> x4, local copies, waits for them, and re-layouts: 7.54 us -> 1.68 us
    pallas_call x3 -> x0, local copies, waits for them, and re-layouts: 2.1 us -> none  [shards(): pl.pallas_call(functools.partial(step_kernel, cx=cx, cy=cy, steps=steps,...]
    pallas_call x1, Pallas kernels: 19.5 us -> 18.2 us  [shards(): pl.pallas_call(functools.partial(step_kernel, cx=cx, cy=cy, steps=steps,...]
    pallas_call x1, Pallas kernels: 1.89 us -> 2.64 us  [shards(): pl.pallas_call(functools.partial(pack_kernel, field=cx * cy), out_shape=j...]
where the time goes in v2:
time: 62.2 us; the launch traced here: 61.8 us
  starting transfers between devices  21.3 us (34%)
  Pallas kernels  20.9 us (34%)
  waiting for transfers between devices  17.1 us (27%)
  local copies, waits for them, and re-layouts  1.78 us (3%)
  between operations  0.74 us (1%)
    pallas_call x1, Pallas kernels, shards(): pl.pallas_call(functools.partial(step_kernel, cx=cx, cy=cy, steps=steps,...  18.2 us
    ppermute x4, starting transfers between devices, shards(): lax.ppermute(block, 'sn', outer)  14.4 us
    ppermute x3, waiting for transfers between devices, shards(): block = own if k == 0 else lax.ppermute(own, 'we', move)  11.2 us
    ppermute x4, waiting for transfers between devices, shards(): lax.ppermute(block, 'sn', outer)  5.87 us
    ppermute x4, starting transfers between devices, shards(): lax.ppermute(block, 'sn', inner)  3.48 us
    ppermute x3, starting transfers between devices, shards(): block = own if k == 0 else lax.ppermute(own, 'we', move)  3.41 us
    pallas_call x1, Pallas kernels, shards(): pl.pallas_call(functools.partial(pack_kernel, field=cx * cy), out_shape=j...  2.64 us
    unnamed x4, local copies, waits for them, and re-layouts  1.68 us
  transfers between devices with their start and end apart: 11, of which 4 were waited for; matrix products, arithmetic and copies ran while one was open for 0% of the time, Pallas kernels for 0%

profile of v2, /device:TPU:1, one launch (start us, length us, event | category | flops | bytes accessed | tf_op | source)
XLA Modules:
  0.0 61.8 jit_solution(14512614933286420485)
XLA Ops:
  0.6 2.6 %pack.1.refs_0_ = f32[776,128]{1,0:T(8,128)} custom-call(f32[144,128]{1,0:T(8,128)} %bitcast.26, f32[288,128]{1,0:T(8,128)} %bitcast.24, f32[288,128]{1,0:T(8,128)} %bitcast.25, s32[48,128]{1,0:T(8,128)} %bitcast.27, f32[3,1,4]{2,1,0:T(1,128)} %bitcast.28, s32[1,1,4]{2,1,0:T(1,128)} %cell.1, f32[1,1,4,4]{3,2,1,0:T(4,128)} %amp.1), custom_call_target="tpu_custom_call" | custom-call | tf_op jit(solution)/shard_map/pack/pallas_call | solution.py:338
  3.3 3.0 %collective-permute-start.8 = (f32[776,128]{1,0:T(8,128)}, f32[776,128]{1,0:T(8,128)S(1)}, u32[]{:S(2)}, u32[]{:S(2)}) collective-permute-start(f32[776,128]{1,0:T(8,128)} %pack.1.refs_0_), channel_id=1, source_target_pairs={{0,24},{8,16},{16,8},{24,0},{1,25},{9,17},{17,9},{25,1},{2,26},{10... | collective-permute-start | bytes 1191944 | tf_op jit(solution)/shard_map/ppermute | solution.py:370
  6.3 0.2 collective-permute-start.5
  6.6 0.1 collective-permute-start.2
  6.7 1.2 %collective-permute-start.1 = (f32[776,128]{1,0:T(8,128)}, f32[776,128]{1,0:T(8,128)S(1)}, u32[]{:S(2)}, u32[]{:S(2)}) collective-permute-start(f32[776,128]{1,0:T(8,128)} %pack.1.refs_0_), channel_id=1, source_target_pairs={{0,1},{1,0},{2,3},{3,2},{4,5},{5,4},{6,7},{7,6},{8,9},{9,8},{10,11... | collective-permute-start | bytes 1191944 | tf_op jit(solution)/shard_map/ppermute | solution.py:371
  7.9 3.5 %collective-permute-start = (f32[776,128]{1,0:T(8,128)}, f32[776,128]{1,0:T(8,128)S(1)}, u32[]{:S(2)}, u32[]{:S(2)}) collective-permute-start(f32[776,128]{1,0:T(8,128)} %pack.1.refs_0_), channel_id=1, source_target_pairs={{1,2},{2,1},{3,4},{4,3},{5,6},{6,5},{9,10},{10,9},{11,12},{12,11},... | collective-permute-start | bytes 1191944 | tf_op jit(solution)/shard_map/ppermute | solution.py:371
  11.4 4.1 %collective-permute-done.8.refs_9_ = f32[776,128]{1,0:T(8,128)S(1)} collective-permute-done((f32[776,128]{1,0:T(8,128)}, f32[776,128]{1,0:T(8,128)S(1)}, u32[]{:S(2)}, u32[]{:S(2)}) %collective-permute-start.8) | collective-permute-done | bytes 397344 | tf_op jit(solution)/shard_map/ppermute | solution.py:370
  15.5 2.1 %collective-permute-start.10 = (f32[776,128]{1,0:T(8,128)S(1)}, f32[776,128]{1,0:T(8,128)S(1)}, u32[]{:S(2)}, u32[]{:S(2)}) collective-permute-start(f32[776,128]{1,0:T(8,128)S(1)} %collective-permute-done.8.refs_9_), channel_id=1, source_target_pairs={{0,1},{1,0},{2,3},{3,2},{4,5},{5,4},{6,7},{7,6},{8,9},{9,8},{10,11... | collective-permute-start | bytes 1191944 | tf_op jit(solution)/shard_map/ppermute | solution.py:371
  17.6 7.1 %collective-permute-done.5.refs_6_ = f32[776,128]{1,0:T(8,128)S(1)} collective-permute-done((f32[776,128]{1,0:T(8,128)}, f32[776,128]{1,0:T(8,128)S(1)}, u32[]{:S(2)}, u32[]{:S(2)}) %collective-permute-start.5) | collective-permute-done | bytes 397344 | tf_op jit(solution)/shard_map/ppermute | solution.py:370
  24.7 3.8 %collective-permute-start.9 = (f32[776,128]{1,0:T(8,128)S(1)}, f32[776,128]{1,0:T(8,128)S(1)}, u32[]{:S(2)}, u32[]{:S(2)}) collective-permute-start(f32[776,128]{1,0:T(8,128)S(1)} %collective-permute-done.8.refs_9_), channel_id=1, source_target_pairs={{1,2},{2,1},{3,4},{4,3},{5,6},{6,5},{9,10},{10,9},{11,12},{12,11},... | collective-permute-start | bytes 1191944 | tf_op jit(solution)/shard_map/ppermute | solution.py:371
  28.5 0.0 collective-permute-done.2.refs_3_
  28.5 0.1 collective-permute-start.7
  28.6 0.0 collective-permute-done.1.refs_2_
  28.6 3.6 %collective-permute-start.6 = (f32[776,128]{1,0:T(8,128)S(1)}, f32[776,128]{1,0:T(8,128)}, u32[]{:S(2)}, u32[]{:S(2)}) collective-permute-start(f32[776,128]{1,0:T(8,128)S(1)} %collective-permute-done.5.refs_6_), channel_id=1, source_target_pairs={{1,2},{2,1},{3,4},{4,3},{5,6},{6,5},{9,10},{10,9},{11,12},{12,11},... | collective-permute-start | bytes 1191944 | tf_op jit(solution)/shard_map/ppermute | solution.py:371
  32.2 0.0 collective-permute-done.refs_1_
  32.2 0.1 collective-permute-start.4
  32.3 0.0 collective-permute-done.10.refs_11_
  32.3 3.6 %collective-permute-start.3 = (f32[776,128]{1,0:T(8,128)S(1)}, f32[776,128]{1,0:T(8,128)}, u32[]{:S(2)}, u32[]{:S(2)}) collective-permute-start(f32[776,128]{1,0:T(8,128)S(1)} %collective-permute-done.2.refs_3_), channel_id=1, source_target_pairs={{1,2},{2,1},{3,4},{4,3},{5,6},{6,5},{9,10},{10,9},{11,12},{12,11},... | collective-permute-start | bytes 1191944 | tf_op jit(solution)/shard_map/ppermute | solution.py:371
  35.8 0.0 copy-start.1
  35.9 0.7 %copy-done.1 = f32[6,16]{1,0:T(8,128)S(1)} copy-done((f32[6,16]{1,0:T(8,128)S(1)}, f32[6,16]{1,0:T(8,128)}, u32[]{:S(2)}) %copy-start.1) | copy-done | bytes 408
  36.6 0.1 pad.4.refs_12_
  36.6 0.1 pad_add_fusion.refs_13_
  36.7 0.0 collective-permute-done.9.refs_10_
  36.7 0.0 collective-permute-done.7.refs_8_
  36.7 1.6 %collective-permute-done.6.refs_7_ = f32[776,128]{1,0:T(8,128)} collective-permute-done((f32[776,128]{1,0:T(8,128)S(1)}, f32[776,128]{1,0:T(8,128)}, u32[]{:S(2)}, u32[]{:S(2)}) %collective-permute-start.6) | collective-permute-done | bytes 397344 | tf_op jit(solution)/shard_map/ppermute | solution.py:371
  38.3 0.0 collective-permute-done.4.refs_5_
  38.3 4.3 %collective-permute-done.3.refs_4_ = f32[776,128]{1,0:T(8,128)} collective-permute-done((f32[776,128]{1,0:T(8,128)S(1)}, f32[776,128]{1,0:T(8,128)}, u32[]{:S(2)}, u32[]{:S(2)}) %collective-permute-start.3) | collective-permute-done | bytes 397344 | tf_op jit(solution)/shard_map/ppermute | solution.py:371
  42.6 0.0 copy-start
  42.6 1.0 %copy-done = f32[776,128]{1,0:T(8,128)S(1)} copy-done((f32[776,128]{1,0:T(8,128)S(1)}, f32[776,128]{1,0:T(8,128)}, u32[]{:S(2)}) %copy-start) | copy-done | bytes 397336
  43.6 18.2 %steps.1 = (f32[144,128]{1,0:T(8,128)}, f32[288,128]{1,0:T(8,128)}, f32[288,128]{1,0:T(8,128)}) custom-call(f32[776,128]{1,0:T(8,128)S(1)} %copy-done, f32[776,128]{1,0:T(8,128)S(1)} %collective-permute-done.refs_1_, f32[776,128]{1,0:T(8,128)S(1)} %collective-permute-done.1.refs_2_, f32[776,128]{1,0:T(8,128)S(1)} %collective-permute-done.2.refs_3_, ...), custom_call_target="tpu_custom_call" | custom-call | tf_op jit(solution)/shard_map/steps/pallas_call | solution.py:398
  (2 shorter events, 0.0 us)
Async XLA Ops:
  3.3 12.2 %collective-permute-start.8 = (f32[776,128]{1,0:T(8,128)}, f32[776,128]{1,0:T(8,128)S(1)}, u32[]{:S(2)}, u32[]{:S(2)}) collective-permute-start(f32[776,128]{1,0:T(8,128)} %pack.1.refs_0_), channel_id=1, source_target_pairs={{0,24},{8,16},{16,8},{24,0},{1,25},{9,17},{17,9},{25,1},{2,26},{10... | collective-permute-start | bytes 1191944 | tf_op jit(solution)/shard_map/ppermute | solution.py:370
  6.3 18.4 %collective-permute-start.5 = (f32[776,128]{1,0:T(8,128)}, f32[776,128]{1,0:T(8,128)S(1)}, u32[]{:S(2)}, u32[]{:S(2)}) collective-permute-start(f32[776,128]{1,0:T(8,128)} %pack.1.refs_0_), channel_id=1, source_target_pairs={{0,16},{8,24},{16,0},{24,8},{1,17},{9,25},{17,1},{25,9},{2,18},{10... | collective-permute-start | bytes 1191944 | tf_op jit(solution)/shard_map/ppermute | solution.py:370
  6.6 21.9 %collective-permute-start.2 = (f32[776,128]{1,0:T(8,128)}, f32[776,128]{1,0:T(8,128)S(1)}, u32[]{:S(2)}, u32[]{:S(2)}) collective-permute-start(f32[776,128]{1,0:T(8,128)} %pack.1.refs_0_), channel_id=1, source_target_pairs={{0,8},{8,0},{16,24},{24,16},{1,9},{9,1},{17,25},{25,17},{2,10},{10... | collective-permute-start | bytes 1191944 | tf_op jit(solution)/shard_map/ppermute | solution.py:370
  6.7 21.9 %collective-permute-start.1 = (f32[776,128]{1,0:T(8,128)}, f32[776,128]{1,0:T(8,128)S(1)}, u32[]{:S(2)}, u32[]{:S(2)}) collective-permute-start(f32[776,128]{1,0:T(8,128)} %pack.1.refs_0_), channel_id=1, source_target_pairs={{0,1},{1,0},{2,3},{3,2},{4,5},{5,4},{6,7},{7,6},{8,9},{9,8},{10,11... | collective-permute-start | bytes 1191944 | tf_op jit(solution)/shard_map/ppermute | solution.py:371
  7.9 24.2 %collective-permute-start = (f32[776,128]{1,0:T(8,128)}, f32[776,128]{1,0:T(8,128)S(1)}, u32[]{:S(2)}, u32[]{:S(2)}) collective-permute-start(f32[776,128]{1,0:T(8,128)} %pack.1.refs_0_), channel_id=1, source_target_pairs={{1,2},{2,1},{3,4},{4,3},{5,6},{6,5},{9,10},{10,9},{11,12},{12,11},... | collective-permute-start | bytes 1191944 | tf_op jit(solution)/shard_map/ppermute | solution.py:371
  15.5 16.8 %collective-permute-start.10 = (f32[776,128]{1,0:T(8,128)S(1)}, f32[776,128]{1,0:T(8,128)S(1)}, u32[]{:S(2)}, u32[]{:S(2)}) collective-permute-start(f32[776,128]{1,0:T(8,128)S(1)} %collective-permute-done.8.refs_9_), channel_id=1, source_target_pairs={{0,1},{1,0},{2,3},{3,2},{4,5},{5,4},{6,7},{7,6},{8,9},{9,8},{10,11... | collective-permute-start | bytes 1191944 | tf_op jit(solution)/shard_map/ppermute | solution.py:371
  24.7 12.0 %collective-permute-start.9 = (f32[776,128]{1,0:T(8,128)S(1)}, f32[776,128]{1,0:T(8,128)S(1)}, u32[]{:S(2)}, u32[]{:S(2)}) collective-permute-start(f32[776,128]{1,0:T(8,128)S(1)} %collective-permute-done.8.refs_9_), channel_id=1, source_target_pairs={{1,2},{2,1},{3,4},{4,3},{5,6},{6,5},{9,10},{10,9},{11,12},{12,11},... | collective-permute-start | bytes 1191944 | tf_op jit(solution)/shard_map/ppermute | solution.py:371
  28.5 8.2 %collective-permute-start.7 = (f32[776,128]{1,0:T(8,128)S(1)}, f32[776,128]{1,0:T(8,128)S(1)}, u32[]{:S(2)}, u32[]{:S(2)}) collective-permute-start(f32[776,128]{1,0:T(8,128)S(1)} %collective-permute-done.5.refs_6_), channel_id=1, source_target_pairs={{0,1},{1,0},{2,3},{3,2},{4,5},{5,4},{6,7},{7,6},{8,9},{9,8},{10,11... | collective-permute-start | bytes 1191944 | tf_op jit(solution)/shard_map/ppermute | solution.py:371
  28.6 9.8 %collective-permute-start.6 = (f32[776,128]{1,0:T(8,128)S(1)}, f32[776,128]{1,0:T(8,128)}, u32[]{:S(2)}, u32[]{:S(2)}) collective-permute-start(f32[776,128]{1,0:T(8,128)S(1)} %collective-permute-done.5.refs_6_), channel_id=1, source_target_pairs={{1,2},{2,1},{3,4},{4,3},{5,6},{6,5},{9,10},{10,9},{11,12},{12,11},... | collective-permute-start | bytes 1191944 | tf_op jit(solution)/shard_map/ppermute | solution.py:371
  32.2 6.2 %collective-permute-start.4 = (f32[776,128]{1,0:T(8,128)S(1)}, f32[776,128]{1,0:T(8,128)}, u32[]{:S(2)}, u32[]{:S(2)}) collective-permute-start(f32[776,128]{1,0:T(8,128)S(1)} %collective-permute-done.2.refs_3_), channel_id=1, source_target_pairs={{0,1},{1,0},{2,3},{3,2},{4,5},{5,4},{6,7},{7,6},{8,9},{9,8},{10,11... | collective-permute-start | bytes 1191944 | tf_op jit(solution)/shard_map/ppermute | solution.py:371
  32.3 10.3 %collective-permute-start.3 = (f32[776,128]{1,0:T(8,128)S(1)}, f32[776,128]{1,0:T(8,128)}, u32[]{:S(2)}, u32[]{:S(2)}) collective-permute-start(f32[776,128]{1,0:T(8,128)S(1)} %collective-permute-done.2.refs_3_), channel_id=1, source_target_pairs={{1,2},{2,1},{3,4},{4,3},{5,6},{6,5},{9,10},{10,9},{11,12},{12,11},... | collective-permute-start | bytes 1191944 | tf_op jit(solution)/shard_map/ppermute | solution.py:371
  35.8 0.7 %copy-start.1 = (f32[6,16]{1,0:T(8,128)S(1)}, f32[6,16]{1,0:T(8,128)}, u32[]{:S(2)}) copy-start(f32[6,16]{1,0:T(8,128)} %param.13) | copy-start | bytes 1156
  42.6 1.0 %copy-start = (f32[776,128]{1,0:T(8,128)S(1)}, f32[776,128]{1,0:T(8,128)}, u32[]{:S(2)}) copy-start(f32[776,128]{1,0:T(8,128)} %pack.1.refs_0_) | copy-start | bytes 1191940

commit v3 on v0

v3 whole, which is shorter than its diff:
```python
import functools

import jax
import jax.numpy as jnp
from jax import lax
from jax.experimental import pallas as pl
from jax.experimental.pallas import tpu as pltpu
from jax.sharding import PartitionSpec as P


BLK = 4
BLKZ = 32
LANES = 128
SUB = 8

inner_coef = 9.0 / 8.0
outer_coef = 1.0 / 24.0
ratio = outer_coef / inner_coef
time_step = 0.08
friction = 0.4

VEL, STR, MEM, COD = 0, 3, 9, 15
FIELDS = 16
NORMAL = (0, 4, 5)
UNROLL = 1


def round_up(value, step):
    return -(-value // step) * step


def pack_kernel(vel, stress, mem, code, scale, cell, amp, kinds, out, table, sem, *, field):
    copies = []
    for i, (at, part) in enumerate(((VEL, vel), (STR, stress), (MEM, mem))):
        to = out.at[pl.ds(at * field, part.shape[0]), :]
        copies.append(pltpu.make_async_copy(part, to, sem.at[i]))
        copies[-1].start()
    out[COD * field : (COD + 1) * field, :] = (code[...] + 1).astype(jnp.float32)
    lane = lax.broadcasted_iota(jnp.int32, (1, LANES), 1)
    here = FIELDS * field
    for i in range(scale.shape[1]):
        for j in range(scale.shape[0]):
            row = jnp.zeros((1, LANES), jnp.float32)
            for k in range(scale.shape[2]):
                row = jnp.where(lane // BLKZ == k, scale[j, i, k], row)
            out[here : here + 1, :] = row
            here += 1
    size = out.shape[0]
    if here < size - 1:
        out[here : size - 1, :] = jnp.zeros((size - 1 - here, LANES), jnp.float32)
    count, steps = amp.shape[2], amp.shape[3]
    row = jnp.zeros((1, LANES), jnp.float32)
    for k in range(count):
        row = jnp.where(lane == k, cell[0, 0, k].astype(jnp.float32), row)
        for t in range(steps):
            row = jnp.where(lane == count + k * steps + t, time_step * amp[0, 0, k, t], row)
    out[size - 1 : size, :] = row
    per_step = time_step * inner_coef
    lines = [jnp.zeros((1, LANES), jnp.float32) for _ in range(table.shape[0])]
    for k in range(kinds.shape[1]):
        decay = kinds[3, k]
        values = (
            kinds[0, k] * per_step,
            kinds[1, k] * per_step,
            kinds[2, k] * per_step,
            decay,
            (1.0 - decay) * kinds[4, k] * (1.0 / time_step),
            kinds[5, k],
        )
        for i, value in enumerate(values):
            lines[i] = jnp.where(lane == k + 1, value, lines[i])
    for i, line in enumerate(lines):
        table[i : i + 1, :] = line
    for copy in copies:
        copy.wait()


class Layout:
    def __init__(self, cx, cy, steps, sources, window, dests, fixed):
        self.cx, self.cy, self.steps, self.sources = cx, cy, steps, sources
        self.window, self.dests, self.fixed = window, tuple(dests), fixed
        self.field = cx * cy
        self.margin = 4
        low = self.margin + cy - 3 * steps + 1
        self.rows = round_up(low + round_up(cy + 6 * steps - 2, SUB) + 2, SUB)

    def base_plane(self, s, me):
        if self.fixed is None:
            return jnp.bitwise_xor(me, self.dests[s]) * self.cx
        return self.fixed - self.dests[s] * self.cx

    def tiles(self, reach):
        return self.margin + self.cy - reach, -(-(self.cy + 2 * reach) // SUB)

    def planes(self, reach, me):
        if self.fixed is not None:
            return self.fixed - reach, self.cx + 2 * reach
        own = [w * self.cx for w in range(self.window // self.cx)]
        need = max(
            min(w + self.cx + reach, self.window) - max(w - reach, 0) for w in own
        )
        return jnp.clip(me * self.cx - reach, 0, self.window - need), need


class State:
    def __init__(self, vel, stress, mem):
        self.vel, self.stress, self.mem = vel, stress, mem


def unpack(lay, block, table, state, props, push_in, plane, row, last_step):
    cx, cy, sources, steps = lay.cx, lay.cy, lay.sources, lay.steps
    shape = (cy, LANES)
    size = block.shape[0]

    def piece(f, p):
        return block[pl.ds(f * lay.field + p, cy, stride=cx), :]

    line = block[size - 1 : size, :]
    spot = [
        jnp.broadcast_to(line[:, k : k + 1], shape) for k in range(sources * (1 + steps))
    ]
    number = lax.broadcasted_iota(jnp.int32, shape, 0) * LANES
    number = (number + lax.broadcasted_iota(jnp.int32, shape, 1)).astype(jnp.float32)
    lines = [jnp.broadcast_to(table[k : k + 1, :], (SUB, LANES)) for k in range(6)]
    across = cy // BLK
    for i in range(cx // BLK):
        first = FIELDS * lay.field + i * across
        grow = jnp.concatenate(
            [
                jnp.broadcast_to(block[first + j : first + j + 1, :], (BLK, LANES))
                for j in range(across)
            ],
            axis=0,
        )
        for p in range(i * BLK, (i + 1) * BLK):
            for c in range(3):
                state.vel[c, plane + p + 2, pl.ds(row, cy), :] = piece(VEL + c, p)
            for c in range(6):
                state.stress[c, plane + p + 2, pl.ds(row, cy), :] = piece(STR + c, p)
                state.mem[c, plane + p, pl.ds(row, cy), :] = piece(MEM + c, p)
            code = jnp.clip(piece(COD, p).astype(jnp.int32), 0, LANES - 1)
            for lo in range(0, cy, SUB):
                n = min(SUB, cy - lo)
                index = code[lo : lo + n]
                for k in range(6):
                    value = jnp.take_along_axis(lines[k][:n], index, axis=1)
                    if k in (1, 2):
                        value = value * grow[lo : lo + n]
                    props[k, plane + p, pl.ds(row + lo, n), :] = value
            hits = [spot[k] == number + float(p * cy * LANES) for k in range(sources)]
            for t in range(last_step):
                total = jnp.zeros(shape, jnp.float32)
                for k in range(sources):
                    total = total + jnp.where(hits[k], spot[sources + k * steps + t], 0.0)
                push_in[t, plane + p, pl.ds(row, cy), :] = total


def deep(f, k):
    lane = lax.broadcasted_iota(jnp.int32, f.shape, 1)
    moved = pltpu.roll(f, (-k) % LANES, 1)
    keep = lane < LANES - k if k > 0 else lane >= -k
    return jnp.where(keep, moved, 0.0)


def z_back(f):
    return f - deep(f, -1), deep(f, 1) - deep(f, -2)


def z_fore(f):
    return deep(f, 1) - f, deep(f, 2) - deep(f, -1)


def add(*pairs):
    one, two = pairs[0]
    for a, b in pairs[1:]:
        one = one + a
        two = two + b
    return one - ratio * two


class Reader:
    def __init__(self, ref, c, p, r):
        self.ref, self.c, self.p, self.r = ref, c, p, r

    def at(self, dp=0, dr=0):
        return self.ref[self.c, self.p + 2 + dp, pl.ds(self.r + dr, SUB), :]

    def x_fore(self):
        return self.at(1) - self.at(0), self.at(2) - self.at(-1)

    def x_back(self):
        return self.at(0) - self.at(-1), self.at(1) - self.at(-2)

    def y_fore(self):
        return self.at(0, 1) - self.at(0, 0), self.at(0, 2) - self.at(0, -1)

    def y_back(self):
        return self.at(0, 0) - self.at(0, -1), self.at(0, 1) - self.at(0, -2)


def velocity_phase(old, new, props, first, n, start, count):
    def body(i, carry):
        p = first + i
        for r in [start + SUB * j for j in range(count)]:
            sxx, sxz, sxy, syz, syy, szz = [Reader(old.stress, c, p, r) for c in range(6)]
            push = props[0, p, pl.ds(r, SUB), :]
            forces = (
                add(sxx.x_fore(), sxy.y_back(), z_back(sxz.at())),
                add(sxy.x_back(), syy.y_fore(), z_back(syz.at())),
                add(sxz.x_back(), syz.y_back(), z_fore(szz.at())),
            )
            for c in range(3):
                now = old.vel[c, p + 2, pl.ds(r, SUB), :]
                new.vel[c, p + 2, pl.ds(r, SUB), :] = now + push * forces[c]
        return carry

    lax.fori_loop(0, n, body, 0, unroll=UNROLL)


def stress_phase(lay, old, new, props, push_in, t, first, n, start, count, outs=None):
    def body(i, carry):
        p = first + i
        for j in range(count):
            r = start + SUB * j
            here = pl.ds(r, SUB)
            ve, vn, vd = [Reader(new.vel, c, p, r) for c in range(3)]
            exx = add(ve.x_back())
            eyy = add(vn.y_back())
            ezz = add(z_back(vd.at()))
            exz = add(z_fore(ve.at()), vd.x_fore())
            exy = add(ve.y_fore(), vn.x_fore())
            eyz = add(z_fore(vn.at()), vd.y_fore())
            mu = props[2, p, here, :]
            twice = mu + mu
            bulk = props[1, p, here, :] * (exx + eyy + ezz)
            moves = (
                bulk + twice * exx,
                mu * exz,
                mu * exy,
                mu * eyz,
                bulk + twice * eyy,
                bulk + twice * ezz,
            )
            keep = props[3, p, here, :]
            gain = props[4, p, here, :]
            source = push_in[t, p, here, :]
            trial = []
            rest = []
            for c in range(6):
                before = old.mem[c, p, here, :]
                after = keep * before + gain * moves[c]
                rest.append(after)
                now = old.stress[c, p + 2, here, :]
                if c in NORMAL:
                    now = now + source
                trial.append((now + moves[c]) - (0.5 * time_step) * (before + after))
            mean = (trial[0] + trial[4] + trial[5]) * (1.0 / 3.0)
            dxx, dyy, dzz = trial[0] - mean, trial[4] - mean, trial[5] - mean
            dxz, dxy, dyz = trial[1], trial[2], trial[3]
            second = 0.5 * (dxx * dxx + dyy * dyy + dzz * dzz) + (
                dxz * dxz + dxy * dxy + dyz * dyz
            )
            soft = jnp.maximum(-mean, 0.0) + jnp.log(1.0 + jnp.exp(-jnp.abs(mean)))
            level = props[5, p, here, :] + friction * soft
            scaled = second / (level * level)
            factor = lax.rsqrt(jnp.sqrt(1.0 + scaled * scaled))
            done = (
                mean + factor * dxx,
                factor * dxz,
                factor * dxy,
                factor * dyz,
                mean + factor * dyy,
                mean + factor * dzz,
            )
            if outs is not None:
                lo = SUB * j
                n_rows = min(SUB, lay.cy - lo)

                def put(out, c, value):
                    at = c * lay.field + lo * lay.cx + i
                    out[pl.ds(at, n_rows, stride=lay.cx), :] = value[:n_rows]

                for c, part in enumerate((ve, vn, vd)):
                    put(outs[0], c, part.at())
                for c in range(6):
                    put(outs[1], c, done[c])
                    put(outs[2], c, rest[c])
            else:
                for c in range(6):
                    new.stress[c, p + 2, here, :] = done[c]
                    new.mem[c, p, here, :] = rest[c]
        return carry

    lax.fori_loop(0, n, body, 0, unroll=UNROLL)


def stage_kernel(*refs, lay, jobs, initial, final):
    blocks = refs[: len(jobs)]
    table, place = refs[len(jobs) : len(jobs) + 2]
    v0, s0, m0, v1, s1, m1, props, push_in = refs[-8:]
    zero, one = State(v0, s0, m0), State(v1, s1, m1)
    me, odd = place[0], lax.rem(place[1], 2)
    cy, margin, steps = lay.cy, lay.margin, lay.steps

    if initial:
        blank = jnp.zeros((lay.rows, LANES), jnp.float32)
        for p in (0, 1, lay.window + 2, lay.window + 3):
            for c in range(3):
                v1[c, p] = blank
                s0[c, p] = blank
                s1[c, p] = blank

    inner_row = jnp.where(odd == 0, margin + 2 * cy, margin)
    for block, (s, inner) in zip(blocks, jobs):
        plane = lay.base_plane(s, me)
        row, pushes = (inner_row, steps - 1) if inner else (margin + cy, steps)
        unpack(lay, block, table, zero, props, push_in, plane, row, pushes)
    if not final:
        return

    reach = 3 * steps - 1
    start, count = lay.tiles(reach)
    late = late_tiles(lay, reach)
    first, n = lay.planes(reach, me)
    end = start + lay.cy + 2 * reach
    at = jnp.where(odd == 0, end - SUB * (count - late), start)
    velocity_phase(zero, one, props, first, n, at, count - late)
    reach -= 2
    start, count = lay.tiles(reach)
    late = late_tiles(lay, reach)
    first, n = lay.planes(reach, me)
    end = start + lay.cy + 2 * reach
    at = jnp.where(odd == 0, end - SUB * (count - late), start)
    stress_phase(lay, zero, one, props, push_in, 0, first, n, at, count - late)


def late_tiles(lay, reach):
    into = 2 if reach == 3 * lay.steps - 1 else 4
    return -(-(reach + into) // SUB)


def late_kernel(*refs, lay):
    count = len(lay.dests)
    blocks = refs[:count]
    table, place = refs[count : count + 2]
    out_vel, out_str, out_mem, v0, s0, m0, v1, s1, m1, props, push_in = refs[count + 10 :]
    zero, one = State(v0, s0, m0), State(v1, s1, m1)
    me, odd = place[0], lax.rem(place[1], 2)
    cy, margin, steps = lay.cy, lay.margin, lay.steps

    outer_row = jnp.where(odd == 0, margin, margin + 2 * cy)
    for s in range(count):
        plane = lay.base_plane(s, me)
        unpack(lay, blocks[s], table, zero, props, push_in, plane, outer_row, steps - 1)

    reach = 3 * steps - 1
    start, _ = lay.tiles(reach)
    late = late_tiles(lay, reach)
    first, n = lay.planes(reach, me)
    at = jnp.where(odd == 0, start, start + cy + 2 * reach - SUB * late)
    velocity_phase(zero, one, props, first, n, at, late)
    reach -= 2
    start, _ = lay.tiles(reach)
    late = late_tiles(lay, reach)
    first, n = lay.planes(reach, me)
    at = jnp.where(odd == 0, start, start + cy + 2 * reach - SUB * late)
    stress_phase(lay, zero, one, props, push_in, 0, first, n, at, late)

    for t in range(1, steps):
        left = 3 * (steps - 1 - t)
        velocity_phase(one, one, props, *lay.planes(left + 2, me), *lay.tiles(left + 2))
        outs = (out_vel, out_str, out_mem) if t == steps - 1 else None
        stress_phase(
            lay, one, one, props, push_in, t, *lay.planes(left, me), *lay.tiles(left), outs
        )


def sees_all(n_we, width):
    return n_we <= 2 * width + 1 and n_we & (n_we - 1) == 0


def devices_in_view(n_we, width):
    return n_we if sees_all(n_we, width) else 2 * width + 1


def shards(
    velocity, stress, memory, material_code, block_scale, material_table, source_cell, source_amp
):
    _, cx, cy, cz = velocity.shape
    sources, steps = source_amp.shape[2:]
    n_we, n_sn = lax.axis_size("we"), lax.axis_size("sn")
    reach = 3 * steps
    assert cz == LANES and cy >= reach and cx % BLK == 0 and cy % BLK == 0
    assert sources * (steps + 1) <= LANES

    used = FIELDS * cx * cy + (cx // BLK) * (cy // BLK) + 1
    vmem = pl.BlockSpec(memory_space=pltpu.VMEM)
    smem = pl.BlockSpec(memory_space=pltpu.SMEM)
    anywhere = pl.BlockSpec(memory_space=pl.ANY)

    def flat(x):
        return jnp.swapaxes(x, -3, -2).reshape(-1, LANES)

    assert material_table.shape[1] < LANES
    own, table = pl.pallas_call(
        functools.partial(pack_kernel, field=cx * cy),
        out_shape=[
            jax.ShapeDtypeStruct((n, LANES), jnp.float32) for n in (round_up(used, SUB), SUB)
        ],
        in_specs=[anywhere, anywhere, anywhere, vmem, smem, smem, smem, smem],
        out_specs=[vmem, vmem],
        scratch_shapes=[pltpu.SemaphoreType.DMA((3,))],
        name="pack",
    )(
        flat(velocity),
        flat(stress),
        flat(memory),
        flat(material_code),
        jnp.swapaxes(block_scale, 0, 1),
        source_cell,
        source_amp,
        material_table,
    )

    width = -(-reach // cx)
    everything = sees_all(n_we, width)
    if everything:
        dests = list(range(n_we))
        window, fixed = n_we * cx, None
        moves = [[(i, i ^ k) for i in range(n_we)] for k in dests]
    else:
        dests = [0] + [sign * k for k in range(1, width + 1) for sign in (1, -1)]
        window, fixed = (2 * width + 1) * cx, width * cx
        moves = [[(i, i + k) for i in range(n_we) if 0 <= i + k < n_we] for k in dests]
    inner = [(i, i ^ 1) for i in range(n_sn) if i ^ 1 < n_sn]
    outer = [(i, i - 1 + 2 * (i % 2)) for i in range(n_sn)]
    outer = [(a, b) for a, b in outer if 0 <= b < n_sn]
    place = jnp.stack([lax.axis_index("we"), lax.axis_index("sn")])

    lay = Layout(cx, cy, steps, sources, window, dests, fixed)

    def frames(n, extra):
        return jax.ShapeDtypeStruct((n, window + extra, lay.rows, LANES), jnp.float32)

    state = [frames(3, 4), frames(6, 4), frames(6, 0)]
    state = state + state + [frames(6, 0), frames(steps, 0)]
    params = pltpu.CompilerParams(vmem_limit_bytes=24 << 20)
    centers, inners, outers = [], [], []
    for i, move in enumerate(moves):
        block = own if i == 0 else lax.ppermute(own, "we", move)
        centers.append(block)
        outers.append(lax.ppermute(block, "sn", outer))
        inners.append(lax.ppermute(block, "sn", inner))

    held = []
    last = len(dests) - 1
    assert last + 1 == devices_in_view(n_we, width)
    for i in range(last + 1):
        jobs = [(i, False)] + ([(i - 1, True)] if i > 0 else [])
        if i == last:
            jobs.append((i, True))
        parts = [(inners if inner else centers)[k] for k, inner in jobs]
        extra = len(parts) + 2
        held = pl.pallas_call(
            functools.partial(stage_kernel, lay=lay, jobs=jobs, initial=i == 0, final=i == last),
            out_shape=state,
            in_specs=[vmem] * (extra - 1) + [smem] + [vmem] * len(held),
            out_specs=[vmem] * len(state),
            input_output_aliases={extra + k: k for k in range(len(held))},
            compiler_params=params,
        )(*parts, table, place, *held)
    results = [jax.ShapeDtypeStruct((n * cx * cy, LANES), jnp.float32) for n in (3, 6, 6)]
    outs = pl.pallas_call(
        functools.partial(late_kernel, lay=lay),
        out_shape=results + state,
        in_specs=[vmem] * (len(outers) + 1) + [smem] + [vmem] * len(state),
        out_specs=[vmem] * (3 + len(state)),
        input_output_aliases={len(outers) + 2 + i: 3 + i for i in range(len(state))},
        compiler_params=params,
        name="late",
    )(*outers, table, place, *held)
    return tuple(jnp.swapaxes(x.reshape(-1, cy, cx, cz), 1, 2) for x in outs[:3])


def solution(mesh):
    in_specs = (
        P(None, "we", "sn", None),
        P(None, "we", "sn", None),
        P(None, "we", "sn", None),
        P("we", "sn", None),
        P("we", "sn", None),
        P(),
        P("we", "sn", None),
        P("we", "sn", None, None),
    )
    out_specs = (P(None, "we", "sn", None), P(None, "we", "sn", None), P(None, "we", "sn", None))

    def call(*args):
        step = jax.shard_map(
            shards, mesh=mesh, in_specs=in_specs, out_specs=out_specs, check_vma=False
        )
        return step(*args)

    return call
```

time: 157 us -> 64.4 us (0.41)
  starting transfers between devices: 94.9 us -> 26.9 us
  waiting for transfers between devices: 33.9 us -> 6.65 us
  Pallas kernels: 0 us -> 24.5 us
  other arithmetic: 15.6 us -> 0.08 us
  local copies, waits for them, and re-layouts: 8.75 us -> 5.01 us
    ppermute x32 -> x11, starting transfers between devices: 94.9 us -> 26.9 us  [the longest x4 12.5 us: shards(): inners.append(lax.ppermute(block, 'sn', inner))]
    ppermute x32 -> x11, waiting for transfers between devices: 33.9 us -> 6.65 us  [the longest x3 6.63 us: shards(): block = own if i == 0 else lax.ppermute(own, 'we', move)]
    pallas_call x0 -> x6, Pallas kernels: none -> 24.5 us  [the longest x1 14.3 us: shards(): pl.pallas_call(functools.partial(late_kernel, lay=lay), out_shape=results...]
    scatter-add x4 -> x0, other arithmetic: 4.56 us -> none  [shards(): flat.at[normal_rows[:, None], source_cells[None, :]]]
    div x4 -> x0, other arithmetic: 3.24 us -> none  [plastic(): mean_stress = (trial[0] + trial[4] + trial[5]) / 3.0]
    add x12 -> x0, other arithmetic: 2.67 us -> none  [the longest x4 1.3 us: stress_step(): trial = stress + time_step * (rates - 0.5 * (memory + memory_new))]
    slice x16 -> x0, local copies, waits for them, and re-layouts: 2.1 us -> none  [the longest x8 1.21 us: with_halo(): lax.slice_in_dim(block, 0, width, axis=dim)]
    unnamed x19 -> x0, other arithmetic: 1.87 us -> none
  transfers between devices with their start and end apart: 32 -> 11, of which waited for: 11 -> 1; matrix products, arithmetic and copies ran while one was open for 2% -> 0% of each run, Pallas kernels for 0% -> 12%
where the time goes in v3:
time: 64.4 us; the launch traced here: 63.9 us
  starting transfers between devices  26.9 us (42%)
  Pallas kernels  24.5 us (38%)
  waiting for transfers between devices  6.65 us (10%)
  local copies, waits for them, and re-layouts  5.01 us (8%)
  between operations  0.77 us (1%)
    pallas_call x1, Pallas kernels, shards(): pl.pallas_call(functools.partial(late_kernel, lay=lay), out_shape=results...  14.3 us
    ppermute x4, starting transfers between devices, shards(): inners.append(lax.ppermute(block, 'sn', inner))  12.5 us
    ppermute x4, starting transfers between devices, shards(): outers.append(lax.ppermute(block, 'sn', outer))  11.1 us
    pallas_call x4, Pallas kernels, shards(): pl.pallas_call(functools.partial(stage_kernel, lay=lay, jobs=jobs, initia...  7.49 us
    ppermute x3, waiting for transfers between devices, shards(): block = own if i == 0 else lax.ppermute(own, 'we', move)  6.63 us
    unnamed x14, local copies, waits for them, and re-layouts  5.01 us
    ppermute x3, starting transfers between devices, shards(): block = own if i == 0 else lax.ppermute(own, 'we', move)  3.35 us
    pallas_call x1, Pallas kernels, shards(): pl.pallas_call(functools.partial(pack_kernel, field=cx * cy), out_shape=[...  2.72 us
  transfers between devices with their start and end apart: 11, of which 1 were waited for; matrix products, arithmetic and copies ran while one was open for 0% of the time, Pallas kernels for 12%

profile of v3, /device:TPU:1, one launch (start us, length us, event | category | flops | bytes accessed | tf_op | source)
XLA Modules:
  0.0 63.9 jit_solution(4099323737036562818)
XLA Ops:
  0.6 2.7 %pack.1 = (f32[776,128]{1,0:T(8,128)}, f32[8,128]{1,0:T(8,128)}) custom-call(f32[144,128]{1,0:T(8,128)} %bitcast.26, f32[288,128]{1,0:T(8,128)} %bitcast.24, f32[288,128]{1,0:T(8,128)} %bitcast.25, s32[48,128]{1,0:T(8,128)} %bitcast.27, f32[3,1,4]{2,1,0:T(1,128)} %bitcast.28, s32[1,1,4]{2,1,0:T(1,128)} %cell.1, f32[1,1,4,4]{3,2,1,0:T(4,128)} %amp.1, ...), custom_call_target="tpu_custom_call" | custom-call | tf_op jit(solution)/shard_map/pack/pallas_call | solution.py:405
  3.4 2.1 %collective-permute-start.1 = (f32[776,128]{1,0:T(8,128)}, f32[776,128]{1,0:T(8,128)S(1)}, u32[]{:S(2)}, u32[]{:S(2)}) collective-permute-start(f32[776,128]{1,0:T(8,128)} %get-tuple-element.40.refs_0_), channel_id=1, source_target_pairs={{0,8},{8,0},{16,24},{24,16},{1,9},{9,1},{17,25},{25,17},{2,10},{10... | collective-permute-start | bytes 1191944 | tf_op jit(solution)/shard_map/ppermute | solution.py:450
  5.5 1.2 %collective-permute-start.3 = (f32[776,128]{1,0:T(8,128)}, f32[776,128]{1,0:T(8,128)S(1)}, u32[]{:S(2)}, u32[]{:S(2)}) collective-permute-start(f32[776,128]{1,0:T(8,128)} %get-tuple-element.40.refs_0_), channel_id=1, source_target_pairs={{0,16},{8,24},{16,0},{24,8},{1,17},{9,25},{17,1},{25,9},{2,18},{10... | collective-permute-start | bytes 1191944 | tf_op jit(solution)/shard_map/ppermute | solution.py:450
  6.7 0.0 collective-permute-start.5
  6.7 1.2 %collective-permute-start.10 = (f32[776,128]{1,0:T(8,128)}, f32[776,128]{1,0:T(8,128)S(1)}, u32[]{:S(2)}, u32[]{:S(2)}) collective-permute-start(f32[776,128]{1,0:T(8,128)} %get-tuple-element.40.refs_0_), channel_id=1, source_target_pairs={{0,1},{1,0},{2,3},{3,2},{4,5},{5,4},{6,7},{7,6},{8,9},{9,8},{10,11... | collective-permute-start | bytes 1191944 | tf_op jit(solution)/shard_map/ppermute | solution.py:453
  8.0 6.6 %collective-permute-done.1.refs_0_ = f32[776,128]{1,0:T(8,128)S(1)} collective-permute-done((f32[776,128]{1,0:T(8,128)}, f32[776,128]{1,0:T(8,128)S(1)}, u32[]{:S(2)}, u32[]{:S(2)}) %collective-permute-start.1) | collective-permute-done | bytes 397344 | tf_op jit(solution)/shard_map/ppermute | solution.py:450
  14.6 2.1 %collective-permute-start.9 = (f32[776,128]{1,0:T(8,128)S(1)}, f32[776,128]{1,0:T(8,128)S(1)}, u32[]{:S(2)}, u32[]{:S(2)}) collective-permute-start(f32[776,128]{1,0:T(8,128)S(1)} %collective-permute-done.1.refs_0_), channel_id=1, source_target_pairs={{0,1},{1,0},{2,3},{3,2},{4,5},{5,4},{6,7},{7,6},{8,9},{9,8},{10,11... | collective-permute-start | bytes 1191944 | tf_op jit(solution)/shard_map/ppermute | solution.py:453
  16.7 0.0 collective-permute-done.3.refs_0_
  16.7 9.1 %collective-permute-start.7 = (f32[776,128]{1,0:T(8,128)S(1)}, f32[776,128]{1,0:T(8,128)S(1)}, u32[]{:S(2)}, u32[]{:S(2)}) collective-permute-start(f32[776,128]{1,0:T(8,128)S(1)} %collective-permute-done.3.refs_0_), channel_id=1, source_target_pairs={{0,1},{1,0},{2,3},{3,2},{4,5},{5,4},{6,7},{7,6},{8,9},{9,8},{10,11... | collective-permute-start | bytes 1191944 | tf_op jit(solution)/shard_map/ppermute | solution.py:453
  25.8 0.0 collective-permute-done.5.refs_0_
  25.8 0.0 collective-permute-start.8
  25.8 3.6 %collective-permute-start = (f32[776,128]{1,0:T(8,128)}, f32[776,128]{1,0:T(8,128)S(1)}, u32[]{:S(2)}, u32[]{:S(2)}) collective-permute-start(f32[776,128]{1,0:T(8,128)} %get-tuple-element.40.refs_0_), channel_id=1, source_target_pairs={{1,2},{2,1},{3,4},{4,3},{5,6},{6,5},{9,10},{10,9},{11,12},{12,11},... | collective-permute-start | bytes 1191944 | tf_op jit(solution)/shard_map/ppermute | solution.py:452
  29.4 0.0 collective-permute-done.10.refs_1_
  29.4 0.0 copy-start.3
  29.4 0.8 %copy-done.3 = f32[776,128]{1,0:T(8,128)} copy-done((f32[776,128]{1,0:T(8,128)}, f32[776,128]{1,0:T(8,128)S(1)}, u32[]{:S(2)}) %copy-start.3) | copy-done | bytes 397336
  30.2 2.0 %collective-permute-start.2 = (f32[776,128]{1,0:T(8,128)S(1)}, f32[776,128]{1,0:T(8,128)S(1)}, u32[]{:S(2)}, u32[]{:S(2)}) collective-permute-start(f32[776,128]{1,0:T(8,128)S(1)} %collective-permute-done.1.refs_0_), channel_id=1, source_target_pairs={{1,2},{2,1},{3,4},{4,3},{5,6},{6,5},{9,10},{10,9},{11,12},{12,11},... | collective-permute-start | bytes 1191944 | tf_op jit(solution)/shard_map/ppermute | solution.py:452
  32.1 0.0 collective-permute-done.9.refs_1_
  32.1 0.0 copy-start.1
  32.2 0.8 %copy-done.1 = f32[776,128]{1,0:T(8,128)} copy-done((f32[776,128]{1,0:T(8,128)}, f32[776,128]{1,0:T(8,128)S(1)}, u32[]{:S(2)}) %copy-start.1) | copy-done | bytes 397336
  32.9 3.6 %collective-permute-start.4 = (f32[776,128]{1,0:T(8,128)S(1)}, f32[776,128]{1,0:T(8,128)S(1)}, u32[]{:S(2)}, u32[]{:S(2)}) collective-permute-start(f32[776,128]{1,0:T(8,128)S(1)} %collective-permute-done.3.refs_0_), channel_id=1, source_target_pairs={{1,2},{2,1},{3,4},{4,3},{5,6},{6,5},{9,10},{10,9},{11,12},{12,11},... | collective-permute-start | bytes 1191944 | tf_op jit(solution)/shard_map/ppermute | solution.py:452
  36.5 0.0 collective-permute-done.7.refs_1_
  36.5 2.0 %collective-permute-start.6 = (f32[776,128]{1,0:T(8,128)S(1)}, f32[776,128]{1,0:T(8,128)}, u32[]{:S(2)}, u32[]{:S(2)}) collective-permute-start(f32[776,128]{1,0:T(8,128)S(1)} %collective-permute-done.5.refs_0_), channel_id=1, source_target_pairs={{1,2},{2,1},{3,4},{4,3},{5,6},{6,5},{9,10},{10,9},{11,12},{12,11},... | collective-permute-start | bytes 1191944 | tf_op jit(solution)/shard_map/ppermute | solution.py:452
  38.5 0.1 pad_add_fusion.refs_2_.refs_3_.refs_4_.refs_5_
  38.6 0.0 copy-start
  38.6 1.0 %copy-done = f32[776,128]{1,0:T(8,128)S(1)} copy-done((f32[776,128]{1,0:T(8,128)S(1)}, f32[776,128]{1,0:T(8,128)}, u32[]{:S(2)}) %copy-start) | copy-done | bytes 397336
  39.6 0.0 copy-start.5
  39.6 0.7 %copy-done.5 = f32[8,128]{1,0:T(8,128)S(1)} copy-done((f32[8,128]{1,0:T(8,128)S(1)}, f32[8,128]{1,0:T(8,128)}, u32[]{:S(2)}) %copy-start.5) | copy-done | bytes 4120
  40.3 0.8 %shard_map.103 = (f32[3,20,48,128]{3,2,1,0:T(8,128)S(1)}, f32[6,20,48,128]{3,2,1,0:T(8,128)S(1)}, f32[6,16,48,128]{3,2,1,0:T(8,128)S(1)}, f32[3,20,48,128]{3,2,1...) custom-call(f32[776,128]{1,0:T(8,128)S(1)} %copy-done, ...), custom_call_target="tpu_custom_call" | custom-call | tf_op jit(solution)/shard_map/pallas_call | solution.py:464
  41.0 0.0 copy-start.4
  41.0 1.0 %copy-done.4 = f32[776,128]{1,0:T(8,128)S(1)} copy-done((f32[776,128]{1,0:T(8,128)S(1)}, f32[776,128]{1,0:T(8,128)}, u32[]{:S(2)}) %copy-start.4) | copy-done | bytes 397336
  42.0 0.0 copy-start.6
  42.0 0.7 %copy-done.6 = f32[8,128]{1,0:T(8,128)S(1)} copy-done((f32[8,128]{1,0:T(8,128)S(1)}, f32[8,128]{1,0:T(8,128)}, u32[]{:S(2)}) %copy-start.6) | copy-done | bytes 4120
  42.7 0.0 copy-start.2
  42.7 0.9 %shard_map.104 = (f32[3,20,48,128]{3,2,1,0:T(8,128)S(1)}, f32[6,20,48,128]{3,2,1,0:T(8,128)S(1)}, f32[6,16,48,128]{3,2,1,0:T(8,128)S(1)}, f32[3,20,48,128]{3,2,1...) custom-call(f32[776,128]{1,0:T(8,128)S(1)} %collective-permute-done., ...), custom_call_target="tpu_custom_call", output_to_operand_aliasing={{0}: (4, {}), {1}: (5, {}), {2}: (6, {}), {3}: (7, {}), {4}... | custom-call | tf_op jit(solution)/shard_map/pallas_call | solution.py:464
  43.6 0.1 copy-done.2
  43.7 0.9 %shard_map.105 = (f32[3,20,48,128]{3,2,1,0:T(8,128)S(1)}, f32[6,20,48,128]{3,2,1,0:T(8,128)S(1)}, f32[6,16,48,128]{3,2,1,0:T(8,128)S(1)}, f32[3,20,48,128]{3,2,1...) custom-call(f32[776,128]{1,0:T(8,128)S(1)} %collective-permute-done., ...), custom_call_target="tpu_custom_call", output_to_operand_aliasing={{0}: (4, {}), {1}: (5, {}), {2}: (6, {}), {3}: (7, {}), {4}... | custom-call | tf_op jit(solution)/shard_map/pallas_call | solution.py:464
  44.6 0.0 collective-permute-done.8.refs_2_
  44.6 5.0 %shard_map.106 = (f32[3,20,48,128]{3,2,1,0:T(8,128)S(1)}, f32[6,20,48,128]{3,2,1,0:T(8,128)S(1)}, f32[6,16,48,128]{3,2,1,0:T(8,128)S(1)}, f32[3,20,48,128]{3,2,1...) custom-call(f32[776,128]{1,0:T(8,128)S(1)} %collective-permute-done., ...), custom_call_target="tpu_custom_call", output_to_operand_aliasing={{0}: (5, {}), {1}: (6, {}), {2}: (7, {}), {3}: (8, {}), {4}... | custom-call | tf_op jit(solution)/shard_map/pallas_call | solution.py:464
  49.6 0.0 collective-permute-done.refs_0_
  49.6 0.0 collective-permute-done.2.refs_1_
  49.6 0.0 collective-permute-done.4.refs_2_
  49.6 0.0 collective-permute-done.6.refs_3_
  49.6 14.3 %late.1 = (f32[144,128]{1,0:T(8,128)}, f32[288,128]{1,0:T(8,128)}, f32[288,128]{1,0:T(8,128)}, f32[3,20,48,128]{3,2,1,0:T(8,128)S(1)}, f32[6,20,48,128]{3,2,1,0:...) custom-call(f32[776,128]{1,0:T(8,128)S(1)} %collective-permute-done., ...), custom_call_target="tpu_custom_call", output_to_operand_aliasing={{3}: (6, {}), {4}: (7, {}), {5}: (8, {}), {6}: (9, {}), {7}... | custom-call | tf_op jit(solution)/shard_map/late/pallas_call | solution.py:473
Async XLA Ops:
  3.4 11.2 %collective-permute-start.1 = (f32[776,128]{1,0:T(8,128)}, f32[776,128]{1,0:T(8,128)S(1)}, u32[]{:S(2)}, u32[]{:S(2)}) collective-permute-start(f32[776,128]{1,0:T(8,128)} %get-tuple-element.40.refs_0_), channel_id=1, source_target_pairs={{0,8},{8,0},{16,24},{24,16},{1,9},{9,1},{17,25},{25,17},{2,10},{10... | collective-permute-start | bytes 1191944 | tf_op jit(solution)/shard_map/ppermute | solution.py:450
  5.5 11.2 %collective-permute-start.3 = (f32[776,128]{1,0:T(8,128)}, f32[776,128]{1,0:T(8,128)S(1)}, u32[]{:S(2)}, u32[]{:S(2)}) collective-permute-start(f32[776,128]{1,0:T(8,128)} %get-tuple-element.40.refs_0_), channel_id=1, source_target_pairs={{0,16},{8,24},{16,0},{24,8},{1,17},{9,25},{17,1},{25,9},{2,18},{10... | collective-permute-start | bytes 1191944 | tf_op jit(solution)/shard_map/ppermute | solution.py:450
  6.7 19.1 %collective-permute-start.5 = (f32[776,128]{1,0:T(8,128)}, f32[776,128]{1,0:T(8,128)S(1)}, u32[]{:S(2)}, u32[]{:S(2)}) collective-permute-start(f32[776,128]{1,0:T(8,128)} %get-tuple-element.40.refs_0_), channel_id=1, source_target_pairs={{0,24},{8,16},{16,8},{24,0},{1,25},{9,17},{17,9},{25,1},{2,26},{10... | collective-permute-start | bytes 1191944 | tf_op jit(solution)/shard_map/ppermute | solution.py:450
  6.7 22.7 %collective-permute-start.10 = (f32[776,128]{1,0:T(8,128)}, f32[776,128]{1,0:T(8,128)S(1)}, u32[]{:S(2)}, u32[]{:S(2)}) collective-permute-start(f32[776,128]{1,0:T(8,128)} %get-tuple-element.40.refs_0_), channel_id=1, source_target_pairs={{0,1},{1,0},{2,3},{3,2},{4,5},{5,4},{6,7},{7,6},{8,9},{9,8},{10,11... | collective-permute-start | bytes 1191944 | tf_op jit(solution)/shard_map/ppermute | solution.py:453
  14.6 17.6 %collective-permute-start.9 = (f32[776,128]{1,0:T(8,128)S(1)}, f32[776,128]{1,0:T(8,128)S(1)}, u32[]{:S(2)}, u32[]{:S(2)}) collective-permute-start(f32[776,128]{1,0:T(8,128)S(1)} %collective-permute-done.1.refs_0_), channel_id=1, source_target_pairs={{0,1},{1,0},{2,3},{3,2},{4,5},{5,4},{6,7},{7,6},{8,9},{9,8},{10,11... | collective-permute-start | bytes 1191944 | tf_op jit(solution)/shard_map/ppermute | solution.py:453
  16.7 19.8 %collective-permute-start.7 = (f32[776,128]{1,0:T(8,128)S(1)}, f32[776,128]{1,0:T(8,128)S(1)}, u32[]{:S(2)}, u32[]{:S(2)}) collective-permute-start(f32[776,128]{1,0:T(8,128)S(1)} %collective-permute-done.3.refs_0_), channel_id=1, source_target_pairs={{0,1},{1,0},{2,3},{3,2},{4,5},{5,4},{6,7},{7,6},{8,9},{9,8},{10,11... | collective-permute-start | bytes 1191944 | tf_op jit(solution)/shard_map/ppermute | solution.py:453
  25.8 18.8 %collective-permute-start.8 = (f32[776,128]{1,0:T(8,128)S(1)}, f32[776,128]{1,0:T(8,128)S(1)}, u32[]{:S(2)}, u32[]{:S(2)}) collective-permute-start(f32[776,128]{1,0:T(8,128)S(1)} %collective-permute-done.5.refs_0_), channel_id=1, source_target_pairs={{0,1},{1,0},{2,3},{3,2},{4,5},{5,4},{6,7},{7,6},{8,9},{9,8},{10,11... | collective-permute-start | bytes 1191944 | tf_op jit(solution)/shard_map/ppermute | solution.py:453
  25.8 23.8 %collective-permute-start = (f32[776,128]{1,0:T(8,128)}, f32[776,128]{1,0:T(8,128)S(1)}, u32[]{:S(2)}, u32[]{:S(2)}) collective-permute-start(f32[776,128]{1,0:T(8,128)} %get-tuple-element.40.refs_0_), channel_id=1, source_target_pairs={{1,2},{2,1},{3,4},{4,3},{5,6},{6,5},{9,10},{10,9},{11,12},{12,11},... | collective-permute-start | bytes 1191944 | tf_op jit(solution)/shard_map/ppermute | solution.py:452
  29.4 0.8 %copy-start.3 = (f32[776,128]{1,0:T(8,128)}, f32[776,128]{1,0:T(8,128)S(1)}, u32[]{:S(2)}) copy-start(f32[776,128]{1,0:T(8,128)S(1)} %collective-permute-done.10.refs_1_) | copy-start | bytes 1191940
  30.2 19.4 %collective-permute-start.2 = (f32[776,128]{1,0:T(8,128)S(1)}, f32[776,128]{1,0:T(8,128)S(1)}, u32[]{:S(2)}, u32[]{:S(2)}) collective-permute-start(f32[776,128]{1,0:T(8,128)S(1)} %collective-permute-done.1.refs_0_), channel_id=1, source_target_pairs={{1,2},{2,1},{3,4},{4,3},{5,6},{6,5},{9,10},{10,9},{11,12},{12,11},... | collective-permute-start | bytes 1191944 | tf_op jit(solution)/shard_map/ppermute | solution.py:452
  32.1 0.8 %copy-start.1 = (f32[776,128]{1,0:T(8,128)}, f32[776,128]{1,0:T(8,128)S(1)}, u32[]{:S(2)}) copy-start(f32[776,128]{1,0:T(8,128)S(1)} %collective-permute-done.9.refs_1_) | copy-start | bytes 1191940
  32.9 16.7 %collective-permute-start.4 = (f32[776,128]{1,0:T(8,128)S(1)}, f32[776,128]{1,0:T(8,128)S(1)}, u32[]{:S(2)}, u32[]{:S(2)}) collective-permute-start(f32[776,128]{1,0:T(8,128)S(1)} %collective-permute-done.3.refs_0_), channel_id=1, source_target_pairs={{1,2},{2,1},{3,4},{4,3},{5,6},{6,5},{9,10},{10,9},{11,12},{12,11},... | collective-permute-start | bytes 1191944 | tf_op jit(solution)/shard_map/ppermute | solution.py:452
  36.5 13.1 %collective-permute-start.6 = (f32[776,128]{1,0:T(8,128)S(1)}, f32[776,128]{1,0:T(8,128)}, u32[]{:S(2)}, u32[]{:S(2)}) collective-permute-start(f32[776,128]{1,0:T(8,128)S(1)} %collective-permute-done.5.refs_0_), channel_id=1, source_target_pairs={{1,2},{2,1},{3,4},{4,3},{5,6},{6,5},{9,10},{10,9},{11,12},{12,11},... | collective-permute-start | bytes 1191944 | tf_op jit(solution)/shard_map/ppermute | solution.py:452
  38.6 1.0 %copy-start = (f32[776,128]{1,0:T(8,128)S(1)}, f32[776,128]{1,0:T(8,128)}, u32[]{:S(2)}) copy-start(f32[776,128]{1,0:T(8,128)} %get-tuple-element.40.refs_0_) | copy-start | bytes 1191940
  39.6 0.7 %copy-start.5 = (f32[8,128]{1,0:T(8,128)S(1)}, f32[8,128]{1,0:T(8,128)}, u32[]{:S(2)}) copy-start(f32[8,128]{1,0:T(8,128)} %get-tuple-element.41.refs_1_.refs_2_.refs_3_.refs_4_) | copy-start | bytes 12292
  41.0 1.0 %copy-start.4 = (f32[776,128]{1,0:T(8,128)S(1)}, f32[776,128]{1,0:T(8,128)}, u32[]{:S(2)}) copy-start(f32[776,128]{1,0:T(8,128)} %copy-done.3) | copy-start | bytes 1191940
  42.0 0.7 %copy-start.6 = (f32[8,128]{1,0:T(8,128)S(1)}, f32[8,128]{1,0:T(8,128)}, u32[]{:S(2)}) copy-start(f32[8,128]{1,0:T(8,128)} %get-tuple-element.41.refs_1_.refs_2_.refs_3_.refs_4_) | copy-start | bytes 12292
  42.7 1.0 %copy-start.2 = (f32[776,128]{1,0:T(8,128)S(1)}, f32[776,128]{1,0:T(8,128)}, u32[]{:S(2)}) copy-start(f32[776,128]{1,0:T(8,128)} %copy-done.1) | copy-start | bytes 1191940

commit v4 on v3

--- a/solution.py
+++ b/solution.py
@@ -18,11 +18,13 @@
 ratio = outer_coef / inner_coef
 time_step = 0.08
 friction = 0.4
+half_step = 0.5 * time_step
+largest = 3.0e38
 
 VEL, STR, MEM, COD = 0, 3, 9, 15
 FIELDS = 16
 NORMAL = (0, 4, 5)
-UNROLL = 1
+UNROLL = (8, 7)
 
 
 def round_up(value, step):
@@ -64,7 +66,7 @@
             kinds[1, k] * per_step,
             kinds[2, k] * per_step,
             decay,
-            (1.0 - decay) * kinds[4, k] * (1.0 / time_step),
+            (1.0 - decay) * kinds[4, k] * (half_step / time_step),
             kinds[5, k],
         )
         for i, value in enumerate(values):
@@ -75,6 +77,10 @@
         copy.wait()
 
 
+def divisor(n, top):
+    return max(k for k in range(1, top + 1) if n % k == 0)
+
+
 class Layout:
     def __init__(self, cx, cy, steps, sources, window, dests, fixed):
         self.cx, self.cy, self.steps, self.sources = cx, cy, steps, sources
@@ -99,6 +105,7 @@
         need = max(
             min(w + self.cx + reach, self.window) - max(w - reach, 0) for w in own
         )
+        need += need % 2 if need < self.window else 0
         return jnp.clip(me * self.cx - reach, 0, self.window - need), need
 
 
@@ -137,7 +144,7 @@
                 state.vel[c, plane + p + 2, pl.ds(row, cy), :] = piece(VEL + c, p)
             for c in range(6):
                 state.stress[c, plane + p + 2, pl.ds(row, cy), :] = piece(STR + c, p)
-                state.mem[c, plane + p, pl.ds(row, cy), :] = piece(MEM + c, p)
+                state.mem[c, plane + p, pl.ds(row, cy), :] = piece(MEM + c, p) * half_step
             code = jnp.clip(piece(COD, p).astype(jnp.int32), 0, LANES - 1)
             for lo in range(0, cy, SUB):
                 n = min(SUB, cy - lo)
@@ -214,7 +221,7 @@
                 new.vel[c, p + 2, pl.ds(r, SUB), :] = now + push * forces[c]
         return carry
 
-    lax.fori_loop(0, n, body, 0, unroll=UNROLL)
+    lax.fori_loop(0, n, body, 0, unroll=divisor(n, UNROLL[0]))
 
 
 def stress_phase(lay, old, new, props, push_in, t, first, n, start, count, outs=None):
@@ -253,7 +260,7 @@
                 now = old.stress[c, p + 2, here, :]
                 if c in NORMAL:
                     now = now + source
-                trial.append((now + moves[c]) - (0.5 * time_step) * (before + after))
+                trial.append((now + moves[c]) - (before + after))
             mean = (trial[0] + trial[4] + trial[5]) * (1.0 / 3.0)
             dxx, dyy, dzz = trial[0] - mean, trial[4] - mean, trial[5] - mean
             dxz, dxy, dyz = trial[1], trial[2], trial[3]
@@ -263,7 +270,8 @@
             soft = jnp.maximum(-mean, 0.0) + jnp.log(1.0 + jnp.exp(-jnp.abs(mean)))
             level = props[5, p, here, :] + friction * soft
             scaled = second / (level * level)
-            factor = lax.rsqrt(jnp.sqrt(1.0 + scaled * scaled))
+            grown = jnp.minimum(1.0 + scaled * scaled, largest)
+            factor = lax.rsqrt(grown * lax.rsqrt(grown))
             done = (
                 mean + factor * dxx,
                 factor * dxz,
@@ -284,95 +292,104 @@
                     put(outs[0], c, part.at())
                 for c in range(6):
                     put(outs[1], c, done[c])
-                    put(outs[2], c, rest[c])
+                    put(outs[2], c, rest[c] * (1.0 / half_step))
             else:
                 for c in range(6):
                     new.stress[c, p + 2, here, :] = done[c]
                     new.mem[c, p, here, :] = rest[c]
         return carry
 
-    lax.fori_loop(0, n, body, 0, unroll=UNROLL)
-
-
-def stage_kernel(*refs, lay, jobs, initial, final):
+    lax.fori_loop(0, n, body, 0, unroll=divisor(n, UNROLL[1]))
+
+
+CENTER, INNER, OUTER = 0, 1, 2
+EARLY_STEPS = 2
+
+
+def unpack_jobs(lay, blocks, jobs, table, state, props, push_in, me, odd):
+    cy, margin, steps = lay.cy, lay.margin, lay.steps
+    rows = (
+        margin + cy,
+        jnp.where(odd == 0, margin + 2 * cy, margin),
+        jnp.where(odd == 0, margin, margin + 2 * cy),
+    )
+    for block, (s, kind) in zip(blocks, jobs):
+        plane = lay.base_plane(s, me)
+        pushes = steps if kind == CENTER else steps - 1
+        unpack(lay, block, table, state, props, push_in, plane, rows[kind], pushes)
+
+
+def states_of(refs):
+    return [State(*refs[i : i + 3]) for i in range(0, len(refs), 3)]
+
+
+def stage_kernel(*refs, lay, jobs, initial, final, held):
     blocks = refs[: len(jobs)]
     table, place = refs[len(jobs) : len(jobs) + 2]
-    v0, s0, m0, v1, s1, m1, props, push_in = refs[-8:]
-    zero, one = State(v0, s0, m0), State(v1, s1, m1)
+    refs = refs[-held:]
+    props, push_in = refs[:2]
+    states = states_of(refs[2:])
     me, odd = place[0], lax.rem(place[1], 2)
-    cy, margin, steps = lay.cy, lay.margin, lay.steps
 
     if initial:
         blank = jnp.zeros((lay.rows, LANES), jnp.float32)
         for p in (0, 1, lay.window + 2, lay.window + 3):
             for c in range(3):
-                v1[c, p] = blank
-                s0[c, p] = blank
-                s1[c, p] = blank
-
-    inner_row = jnp.where(odd == 0, margin + 2 * cy, margin)
-    for block, (s, inner) in zip(blocks, jobs):
-        plane = lay.base_plane(s, me)
-        row, pushes = (inner_row, steps - 1) if inner else (margin + cy, steps)
-        unpack(lay, block, table, zero, props, push_in, plane, row, pushes)
+                for i, state in enumerate(states):
+                    if i > 0:
+                        state.vel[c, p] = blank
+                    state.stress[c, p] = blank
+    unpack_jobs(lay, blocks, jobs, table, states[0], props, push_in, me, odd)
     if not final:
         return
 
-    reach = 3 * steps - 1
-    start, count = lay.tiles(reach)
-    late = late_tiles(lay, reach)
-    first, n = lay.planes(reach, me)
-    end = start + lay.cy + 2 * reach
-    at = jnp.where(odd == 0, end - SUB * (count - late), start)
-    velocity_phase(zero, one, props, first, n, at, count - late)
-    reach -= 2
-    start, count = lay.tiles(reach)
-    late = late_tiles(lay, reach)
-    first, n = lay.planes(reach, me)
-    end = start + lay.cy + 2 * reach
-    at = jnp.where(odd == 0, end - SUB * (count - late), start)
-    stress_phase(lay, zero, one, props, push_in, 0, first, n, at, count - late)
-
-
-def late_tiles(lay, reach):
-    into = 2 if reach == 3 * lay.steps - 1 else 4
-    return -(-(reach + into) // SUB)
-
-
-def late_kernel(*refs, lay):
-    count = len(lay.dests)
+    for t in range(len(states) - 1):
+        for k in (0, 1):
+            reach, late = split(lay, t, k)
+            start, count = lay.tiles(reach)
+            first, n = lay.planes(reach, me)
+            end = start + lay.cy + 2 * reach
+            at = jnp.where(odd == 0, end - SUB * (count - late), start)
+            part = (first, n, at, count - late)
+            if k == 0:
+                velocity_phase(states[t], states[t + 1], props, *part)
+            else:
+                stress_phase(lay, states[t], states[t + 1], props, push_in, t, *part)
+
+
+def split(lay, t, k):
+    reach = 3 * (lay.steps - 1 - t) + (2 if k == 0 else 0)
+    return reach, -(-(reach + 4 * t + 2 * k + 2) // SUB)
+
+
+def late_kernel(*refs, lay, jobs, held):
+    count = len(jobs)
     blocks = refs[:count]
     table, place = refs[count : count + 2]
-    out_vel, out_str, out_mem, v0, s0, m0, v1, s1, m1, props, push_in = refs[count + 10 :]
-    zero, one = State(v0, s0, m0), State(v1, s1, m1)
+    outs = refs[count + 2 + held : count + 5 + held]
+    refs = refs[-held:]
+    props, push_in = refs[:2]
+    states = states_of(refs[2:])
     me, odd = place[0], lax.rem(place[1], 2)
-    cy, margin, steps = lay.cy, lay.margin, lay.steps
-
-    outer_row = jnp.where(odd == 0, margin, margin + 2 * cy)
-    for s in range(count):
-        plane = lay.base_plane(s, me)
-        unpack(lay, blocks[s], table, zero, props, push_in, plane, outer_row, steps - 1)
-
-    reach = 3 * steps - 1
-    start, _ = lay.tiles(reach)
-    late = late_tiles(lay, reach)
-    first, n = lay.planes(reach, me)
-    at = jnp.where(odd == 0, start, start + cy + 2 * reach - SUB * late)
-    velocity_phase(zero, one, props, first, n, at, late)
-    reach -= 2
-    start, _ = lay.tiles(reach)
-    late = late_tiles(lay, reach)
-    first, n = lay.planes(reach, me)
-    at = jnp.where(odd == 0, start, start + cy + 2 * reach - SUB * late)
-    stress_phase(lay, zero, one, props, push_in, 0, first, n, at, late)
-
-    for t in range(1, steps):
-        left = 3 * (steps - 1 - t)
-        velocity_phase(one, one, props, *lay.planes(left + 2, me), *lay.tiles(left + 2))
-        outs = (out_vel, out_str, out_mem) if t == steps - 1 else None
-        stress_phase(
-            lay, one, one, props, push_in, t, *lay.planes(left, me), *lay.tiles(left), outs
-        )
+    unpack_jobs(lay, blocks, jobs, table, states[0], props, push_in, me, odd)
+
+    for t in range(lay.steps):
+        for k in (0, 1):
+            reach, late = split(lay, t, k)
+            start, count = lay.tiles(reach)
+            first, n = lay.planes(reach, me)
+            if t + 1 < len(states):
+                old, new = states[t], states[t + 1]
+                end = start + lay.cy + 2 * reach
+                part = (first, n, jnp.where(odd == 0, start, end - SUB * late), late)
+            else:
+                old = new = states[-1]
+                part = (first, n, start, count)
+            if k == 0:
+                velocity_phase(old, new, props, *part)
+            else:
+                final = outs if t == lay.steps - 1 else None
+                stress_phase(lay, old, new, props, push_in, t, *part, final)
 
 
 def sees_all(n_we, width):
@@ -442,43 +459,58 @@
     def frames(n, extra):
         return jax.ShapeDtypeStruct((n, window + extra, lay.rows, LANES), jnp.float32)
 
-    state = [frames(3, 4), frames(6, 4), frames(6, 0)]
-    state = state + state + [frames(6, 0), frames(steps, 0)]
-    params = pltpu.CompilerParams(vmem_limit_bytes=24 << 20)
-    centers, inners, outers = [], [], []
+    early = min(EARLY_STEPS, steps - 1)
+    state = [frames(6, 0), frames(steps, 0)]
+    state += (early + 1) * [frames(3, 4), frames(6, 4), frames(6, 0)]
+    params = pltpu.CompilerParams(vmem_limit_bytes=16 << 20)
+    ready = {}
     for i, move in enumerate(moves):
         block = own if i == 0 else lax.ppermute(own, "we", move)
-        centers.append(block)
-        outers.append(lax.ppermute(block, "sn", outer))
-        inners.append(lax.ppermute(block, "sn", inner))
+        ready[i, CENTER] = block
+        ready[i, OUTER] = lax.ppermute(block, "sn", outer)
+        ready[i, INNER] = lax.ppermute(block, "sn", inner)
 
     held = []
     last = len(dests) - 1
     assert last + 1 == devices_in_view(n_we, width)
     for i in range(last + 1):
-        jobs = [(i, False)] + ([(i - 1, True)] if i > 0 else [])
+        jobs = [(i, CENTER)]
+        if i > 0:
+            jobs.append((i - 1, INNER))
         if i == last:
-            jobs.append((i, True))
-        parts = [(inners if inner else centers)[k] for k, inner in jobs]
+            jobs.append((i, INNER))
+        elif i > 0:
+            jobs.append((i - 1, OUTER))
+        parts = [ready.pop(job) if job[1] else ready[job] for job in jobs]
         extra = len(parts) + 2
         held = pl.pallas_call(
-            functools.partial(stage_kernel, lay=lay, jobs=jobs, initial=i == 0, final=i == last),
+            functools.partial(
+                stage_kernel,
+                lay=lay,
+                jobs=jobs,
+                initial=i == 0,
+                final=i == last,
+                held=len(state),
+            ),
             out_shape=state,
             in_specs=[vmem] * (extra - 1) + [smem] + [vmem] * len(held),
             out_specs=[vmem] * len(state),
             input_output_aliases={extra + k: k for k in range(len(held))},
             compiler_params=params,
         )(*parts, table, place, *held)
+    jobs = [job for job in ready if job[1] != CENTER]
+    parts = [ready[job] for job in jobs]
+    extra = len(parts) + 2
     results = [jax.ShapeDtypeStruct((n * cx * cy, LANES), jnp.float32) for n in (3, 6, 6)]
     outs = pl.pallas_call(
-        functools.partial(late_kernel, lay=lay),
+        functools.partial(late_kernel, lay=lay, jobs=jobs, held=len(state)),
         out_shape=results + state,
-        in_specs=[vmem] * (len(outers) + 1) + [smem] + [vmem] * len(state),
+        in_specs=[vmem] * (extra - 1) + [smem] + [vmem] * len(state),
         out_specs=[vmem] * (3 + len(state)),
-        input_output_aliases={len(outers) + 2 + i: 3 + i for i in range(len(state))},
+        input_output_aliases={extra + i: 3 + i for i in range(len(state))},
         compiler_params=params,
         name="late",
-    )(*outers, table, place, *held)
+    )(*parts, table, place, *held)
     return tuple(jnp.swapaxes(x.reshape(-1, cy, cx, cz), 1, 2) for x in outs[:3])
 
 

time: 64.4 us -> 52.1 us (0.81)
  Pallas kernels: 24.5 us -> 16.1 us
  starting transfers between devices: 26.9 us -> 20.1 us
  waiting for transfers between devices: 6.65 us -> 10.6 us
  local copies, waits for them, and re-layouts: 5.01 us -> 4.11 us
    pallas_call x1, Pallas kernels: 14.3 us -> 6.74 us  [shards(): pl.pallas_call(functools.partial(late_kernel, lay=lay, jobs=jobs, held=le...]
    ppermute x8, starting transfers between devices: 23.6 us -> 16.5 us  [the longest x4 13.9 us: shards(): ready[i, OUTER] = lax.ppermute(block, 'sn', outer)]
    ppermute x3, waiting for transfers between devices: 6.63 us -> 10.5 us  [shards(): block = own if i == 0 else lax.ppermute(own, 'we', move)]
    unnamed x14 -> x10, local copies, waits for them, and re-layouts: 5.01 us -> 4.11 us
    pallas_call x4, Pallas kernels: 7.49 us -> 6.62 us  [shards(): pl.pallas_call(functools.partial(stage_kernel, lay=lay, jobs=jobs, initia...]
  transfers between devices with their start and end apart: 11 -> 11, of which waited for: 1 -> 2; matrix products, arithmetic and copies ran while one was open for 0% -> 0% of each run, Pallas kernels for 12% -> 13%
where the time goes in v4:
time: 52.1 us; the launch traced here: 51.7 us
  starting transfers between devices  20.1 us (39%)
  Pallas kernels  16.1 us (31%)
  waiting for transfers between devices  10.6 us (20%)
  local copies, waits for them, and re-layouts  4.11 us (8%)
  between operations  0.73 us (1%)
    ppermute x4, starting transfers between devices, shards(): ready[i, OUTER] = lax.ppermute(block, 'sn', outer)  13.9 us
    ppermute x3, waiting for transfers between devices, shards(): block = own if i == 0 else lax.ppermute(own, 'we', move)  10.5 us
    pallas_call x1, Pallas kernels, shards(): pl.pallas_call(functools.partial(late_kernel, lay=lay, jobs=jobs, held=le...  6.74 us
    pallas_call x4, Pallas kernels, shards(): pl.pallas_call(functools.partial(stage_kernel, lay=lay, jobs=jobs, initia...  6.62 us
    unnamed x10, local copies, waits for them, and re-layouts  4.11 us
    ppermute x3, starting transfers between devices, shards(): block = own if i == 0 else lax.ppermute(own, 'we', move)  3.6 us
    pallas_call x1, Pallas kernels, shards(): pl.pallas_call(functools.partial(pack_kernel, field=cx * cy), out_shape=[...  2.72 us
    ppermute x4, starting transfers between devices, shards(): ready[i, INNER] = lax.ppermute(block, 'sn', inner)  2.61 us
  transfers between devices with their start and end apart: 11, of which 2 were waited for; matrix products, arithmetic and copies ran while one was open for 0% of the time, Pallas kernels for 13%

profile of v4, /device:TPU:1, one launch (start us, length us, event | category | flops | bytes accessed | tf_op | source)
XLA Modules:
  0.0 51.7 jit_solution(10300369496356173702)
XLA Ops:
  0.6 2.7 %pack.1 = (f32[776,128]{1,0:T(8,128)}, f32[8,128]{1,0:T(8,128)}) custom-call(f32[144,128]{1,0:T(8,128)} %bitcast.26, f32[288,128]{1,0:T(8,128)} %bitcast.24, f32[288,128]{1,0:T(8,128)} %bitcast.25, s32[48,128]{1,0:T(8,128)} %bitcast.27, f32[3,1,4]{2,1,0:T(1,128)} %bitcast.28, s32[1,1,4]{2,1,0:T(1,128)} %cell.1, f32[1,1,4,4]{3,2,1,0:T(4,128)} %amp.1, ...), custom_call_target="tpu_custom_call" | custom-call | tf_op jit(solution)/shard_map/pack/pallas_call | solution.py:422
  3.4 2.1 %collective-permute-start.6 = (f32[776,128]{1,0:T(8,128)}, f32[776,128]{1,0:T(8,128)S(1)}, u32[]{:S(2)}, u32[]{:S(2)}) collective-permute-start(f32[776,128]{1,0:T(8,128)} %get-tuple-element.52.refs_0_), channel_id=1, source_target_pairs={{0,8},{8,0},{16,24},{24,16},{1,9},{9,1},{17,25},{25,17},{2,10},{10... | collective-permute-start | bytes 1191944 | tf_op jit(solution)/shard_map/ppermute | solution.py:468
  5.5 4.0 %collective-permute-start.10 = (f32[776,128]{1,0:T(8,128)}, f32[776,128]{1,0:T(8,128)S(1)}, u32[]{:S(2)}, u32[]{:S(2)}) collective-permute-start(f32[776,128]{1,0:T(8,128)} %get-tuple-element.52.refs_0_), channel_id=1, source_target_pairs={{1,2},{2,1},{3,4},{4,3},{5,6},{6,5},{9,10},{10,9},{11,12},{12,11},... | collective-permute-start | bytes 1191944 | tf_op jit(solution)/shard_map/ppermute | solution.py:470
  9.5 1.3 %collective-permute-start = (f32[776,128]{1,0:T(8,128)}, f32[776,128]{1,0:T(8,128)S(1)}, u32[]{:S(2)}, u32[]{:S(2)}) collective-permute-start(f32[776,128]{1,0:T(8,128)} %get-tuple-element.52.refs_0_), channel_id=1, source_target_pairs={{0,16},{8,24},{16,0},{24,8},{1,17},{9,25},{17,1},{25,9},{2,18},{10... | collective-permute-start | bytes 1191944 | tf_op jit(solution)/shard_map/ppermute | solution.py:468
  10.8 0.2 collective-permute-start.2
  11.0 0.0 collective-permute-start.9
  11.0 3.6 %collective-permute-done.6.refs_0_ = f32[776,128]{1,0:T(8,128)S(1)} collective-permute-done((f32[776,128]{1,0:T(8,128)}, f32[776,128]{1,0:T(8,128)S(1)}, u32[]{:S(2)}, u32[]{:S(2)}) %collective-permute-start.6) | collective-permute-done | bytes 397344 | tf_op jit(solution)/shard_map/ppermute | solution.py:468
  14.6 2.1 %collective-permute-start.7 = (f32[776,128]{1,0:T(8,128)S(1)}, f32[776,128]{1,0:T(8,128)S(1)}, u32[]{:S(2)}, u32[]{:S(2)}) collective-permute-start(f32[776,128]{1,0:T(8,128)S(1)} %collective-permute-done.6.refs_0_), channel_id=1, source_target_pairs={{0,1},{1,0},{2,3},{3,2},{4,5},{5,4},{6,7},{7,6},{8,9},{9,8},{10,11... | collective-permute-start | bytes 1191944 | tf_op jit(solution)/shard_map/ppermute | solution.py:471
  16.7 0.0 collective-permute-done.10.refs_2_
  16.7 3.6 %collective-permute-start.8 = (f32[776,128]{1,0:T(8,128)S(1)}, f32[776,128]{1,0:T(8,128)S(1)}, u32[]{:S(2)}, u32[]{:S(2)}) collective-permute-start(f32[776,128]{1,0:T(8,128)S(1)} %collective-permute-done.6.refs_0_), channel_id=1, source_target_pairs={{1,2},{2,1},{3,4},{4,3},{5,6},{6,5},{9,10},{10,9},{11,12},{12,11},... | collective-permute-start | bytes 1191944 | tf_op jit(solution)/shard_map/ppermute | solution.py:470
  20.3 7.0 %collective-permute-done.refs_0_ = f32[776,128]{1,0:T(8,128)S(1)} collective-permute-done((f32[776,128]{1,0:T(8,128)}, f32[776,128]{1,0:T(8,128)S(1)}, u32[]{:S(2)}, u32[]{:S(2)}) %collective-permute-start) | collective-permute-done | bytes 397344 | tf_op jit(solution)/shard_map/ppermute | solution.py:468
  27.3 0.0 collective-permute-start.4
  27.3 0.0 collective-permute-done.2.refs_0_
  27.3 0.5 collective-permute-start.5
  27.8 0.0 collective-permute-done.9.refs_1_
  27.8 0.0 copy-start
  27.8 0.7 %copy-done = f32[776,128]{1,0:T(8,128)} copy-done((f32[776,128]{1,0:T(8,128)}, f32[776,128]{1,0:T(8,128)S(1)}, u32[]{:S(2)}) %copy-start) | copy-done | bytes 397336
  28.5 4.3 %collective-permute-start.1 = (f32[776,128]{1,0:T(8,128)S(1)}, f32[776,128]{1,0:T(8,128)}, u32[]{:S(2)}, u32[]{:S(2)}) collective-permute-start(f32[776,128]{1,0:T(8,128)S(1)} %collective-permute-done.refs_0_), channel_id=1, source_target_pairs={{1,2},{2,1},{3,4},{4,3},{5,6},{6,5},{9,10},{10,9},{11,12},{12,11},... | collective-permute-start | bytes 1191944 | tf_op jit(solution)/shard_map/ppermute | solution.py:470
  32.9 0.0 collective-permute-done.7.refs_1_
  32.9 1.9 %collective-permute-start.3 = (f32[776,128]{1,0:T(8,128)S(1)}, f32[776,128]{1,0:T(8,128)}, u32[]{:S(2)}, u32[]{:S(2)}) collective-permute-start(f32[776,128]{1,0:T(8,128)S(1)} %collective-permute-done.2.refs_0_), channel_id=1, source_target_pairs={{1,2},{2,1},{3,4},{4,3},{5,6},{6,5},{9,10},{10,9},{11,12},{12,11},... | collective-permute-start | bytes 1191944 | tf_op jit(solution)/shard_map/ppermute | solution.py:470
  34.8 0.1 pad_add_fusion.refs_2_.refs_4_.refs_3_
  34.9 0.0 copy-start.2
  34.9 1.0 %copy-done.2 = f32[776,128]{1,0:T(8,128)S(1)} copy-done((f32[776,128]{1,0:T(8,128)S(1)}, f32[776,128]{1,0:T(8,128)}, u32[]{:S(2)}) %copy-start.2) | copy-done | bytes 397336
  35.9 0.0 copy-start.3
  35.9 0.7 %copy-done.3 = f32[8,128]{1,0:T(8,128)S(1)} copy-done((f32[8,128]{1,0:T(8,128)S(1)}, f32[8,128]{1,0:T(8,128)}, u32[]{:S(2)}) %copy-start.3) | copy-done | bytes 4120
  36.6 0.8 %shard_map.103 = (f32[6,16,48,128]{3,2,1,0:T(8,128)S(1)}, f32[4,16,48,128]{3,2,1,0:T(8,128)S(1)}, f32[3,20,48,128]{3,2,1,0:T(8,128)S(1)}, f32[6,20,48,128]{3,2,1...) custom-call(f32[776,128]{1,0:T(8,128)S(1)} %copy-done.2, ...), custom_call_target="tpu_custom_call" | custom-call | tf_op jit(solution)/shard_map/pallas_call | solution.py:486
  37.4 0.0 copy-start.1
  37.4 1.0 %copy-done.1 = f32[776,128]{1,0:T(8,128)S(1)} copy-done((f32[776,128]{1,0:T(8,128)S(1)}, f32[776,128]{1,0:T(8,128)}, u32[]{:S(2)}) %copy-start.1) | copy-done | bytes 397336
  38.4 0.0 copy-start.4
  38.4 0.7 %copy-done.4 = f32[8,128]{1,0:T(8,128)S(1)} copy-done((f32[8,128]{1,0:T(8,128)S(1)}, f32[8,128]{1,0:T(8,128)}, u32[]{:S(2)}) %copy-start.4) | copy-done | bytes 4120
  39.1 1.1 %shard_map.104 = (f32[6,16,48,128]{3,2,1,0:T(8,128)S(1)}, f32[4,16,48,128]{3,2,1,0:T(8,128)S(1)}, f32[3,20,48,128]{3,2,1,0:T(8,128)S(1)}, f32[6,20,48,128]{3,2,1...) custom-call(f32[776,128]{1,0:T(8,128)S(1)} %collective-permute-done., ...), custom_call_target="tpu_custom_call", output_to_operand_aliasing={{0}: (5, {}), {1}: (6, {}), {2}: (7, {}), {3}: (8, {}), {4}... | custom-call | tf_op jit(solution)/shard_map/pallas_call | solution.py:486
  40.1 0.0 collective-permute-done.8.refs_2_
  40.1 1.1 %shard_map.105 = (f32[6,16,48,128]{3,2,1,0:T(8,128)S(1)}, f32[4,16,48,128]{3,2,1,0:T(8,128)S(1)}, f32[3,20,48,128]{3,2,1,0:T(8,128)S(1)}, f32[6,20,48,128]{3,2,1...) custom-call(f32[776,128]{1,0:T(8,128)S(1)} %collective-permute-done., ...), custom_call_target="tpu_custom_call", output_to_operand_aliasing={{0}: (5, {}), {1}: (6, {}), {2}: (7, {}), {3}: (8, {}), {4}... | custom-call | tf_op jit(solution)/shard_map/pallas_call | solution.py:486
  41.2 0.0 collective-permute-done.4.refs_1_
  41.2 0.0 collective-permute-done.5.refs_2_
  41.3 3.6 %shard_map.106 = (f32[6,16,48,128]{3,2,1,0:T(8,128)S(1)}, f32[4,16,48,128]{3,2,1,0:T(8,128)S(1)}, f32[3,20,48,128]{3,2,1,0:T(8,128)S(1)}, f32[6,20,48,128]{3,2,1...) custom-call(f32[776,128]{1,0:T(8,128)S(1)} %collective-permute-done., ...), custom_call_target="tpu_custom_call", output_to_operand_aliasing={{0}: (5, {}), {1}: (6, {}), {2}: (7, {}), {3}: (8, {}), {4}... | custom-call | tf_op jit(solution)/shard_map/pallas_call | solution.py:486
  44.9 0.0 collective-permute-done.1.refs_0_
  44.9 0.0 collective-permute-done.3.refs_1_
  44.9 6.7 %late.1 = (f32[144,128]{1,0:T(8,128)}, f32[288,128]{1,0:T(8,128)}, f32[288,128]{1,0:T(8,128)}, f32[6,16,48,128]{3,2,1,0:T(8,128)S(1)}, f32[4,16,48,128]{3,2,1,0:...) custom-call(f32[776,128]{1,0:T(8,128)} %collective-permute-done.1.re, ...), custom_call_target="tpu_custom_call", output_to_operand_aliasing={{3}: (4, {}), {4}: (5, {}), {5}: (6, {}), {6}: (7, {}), {7}... | custom-call | tf_op jit(solution)/shard_map/late/pallas_call | solution.py:505
Async XLA Ops:
  3.4 11.2 %collective-permute-start.6 = (f32[776,128]{1,0:T(8,128)}, f32[776,128]{1,0:T(8,128)S(1)}, u32[]{:S(2)}, u32[]{:S(2)}) collective-permute-start(f32[776,128]{1,0:T(8,128)} %get-tuple-element.52.refs_0_), channel_id=1, source_target_pairs={{0,8},{8,0},{16,24},{24,16},{1,9},{9,1},{17,25},{25,17},{2,10},{10... | collective-permute-start | bytes 1191944 | tf_op jit(solution)/shard_map/ppermute | solution.py:468
  5.5 11.2 %collective-permute-start.10 = (f32[776,128]{1,0:T(8,128)}, f32[776,128]{1,0:T(8,128)S(1)}, u32[]{:S(2)}, u32[]{:S(2)}) collective-permute-start(f32[776,128]{1,0:T(8,128)} %get-tuple-element.52.refs_0_), channel_id=1, source_target_pairs={{1,2},{2,1},{3,4},{4,3},{5,6},{6,5},{9,10},{10,9},{11,12},{12,11},... | collective-permute-start | bytes 1191944 | tf_op jit(solution)/shard_map/ppermute | solution.py:470
  9.5 17.8 %collective-permute-start = (f32[776,128]{1,0:T(8,128)}, f32[776,128]{1,0:T(8,128)S(1)}, u32[]{:S(2)}, u32[]{:S(2)}) collective-permute-start(f32[776,128]{1,0:T(8,128)} %get-tuple-element.52.refs_0_), channel_id=1, source_target_pairs={{0,16},{8,24},{16,0},{24,8},{1,17},{9,25},{17,1},{25,9},{2,18},{10... | collective-permute-start | bytes 1191944 | tf_op jit(solution)/shard_map/ppermute | solution.py:468
  10.8 16.5 %collective-permute-start.2 = (f32[776,128]{1,0:T(8,128)}, f32[776,128]{1,0:T(8,128)S(1)}, u32[]{:S(2)}, u32[]{:S(2)}) collective-permute-start(f32[776,128]{1,0:T(8,128)} %get-tuple-element.52.refs_0_), channel_id=1, source_target_pairs={{0,24},{8,16},{16,8},{24,0},{1,25},{9,17},{17,9},{25,1},{2,26},{10... | collective-permute-start | bytes 1191944 | tf_op jit(solution)/shard_map/ppermute | solution.py:468
  11.0 16.8 %collective-permute-start.9 = (f32[776,128]{1,0:T(8,128)}, f32[776,128]{1,0:T(8,128)S(1)}, u32[]{:S(2)}, u32[]{:S(2)}) collective-permute-start(f32[776,128]{1,0:T(8,128)} %get-tuple-element.52.refs_0_), channel_id=1, source_target_pairs={{0,1},{1,0},{2,3},{3,2},{4,5},{5,4},{6,7},{7,6},{8,9},{9,8},{10,11... | collective-permute-start | bytes 1191944 | tf_op jit(solution)/shard_map/ppermute | solution.py:471
  14.6 18.3 %collective-permute-start.7 = (f32[776,128]{1,0:T(8,128)S(1)}, f32[776,128]{1,0:T(8,128)S(1)}, u32[]{:S(2)}, u32[]{:S(2)}) collective-permute-start(f32[776,128]{1,0:T(8,128)S(1)} %collective-permute-done.6.refs_0_), channel_id=1, source_target_pairs={{0,1},{1,0},{2,3},{3,2},{4,5},{5,4},{6,7},{7,6},{8,9},{9,8},{10,11... | collective-permute-start | bytes 1191944 | tf_op jit(solution)/shard_map/ppermute | solution.py:471
  16.7 23.5 %collective-permute-start.8 = (f32[776,128]{1,0:T(8,128)S(1)}, f32[776,128]{1,0:T(8,128)S(1)}, u32[]{:S(2)}, u32[]{:S(2)}) collective-permute-start(f32[776,128]{1,0:T(8,128)S(1)} %collective-permute-done.6.refs_0_), channel_id=1, source_target_pairs={{1,2},{2,1},{3,4},{4,3},{5,6},{6,5},{9,10},{10,9},{11,12},{12,11},... | collective-permute-start | bytes 1191944 | tf_op jit(solution)/shard_map/ppermute | solution.py:470
  27.3 14.0 %collective-permute-start.4 = (f32[776,128]{1,0:T(8,128)S(1)}, f32[776,128]{1,0:T(8,128)S(1)}, u32[]{:S(2)}, u32[]{:S(2)}) collective-permute-start(f32[776,128]{1,0:T(8,128)S(1)} %collective-permute-done.refs_0_), channel_id=1, source_target_pairs={{0,1},{1,0},{2,3},{3,2},{4,5},{5,4},{6,7},{7,6},{8,9},{9,8},{10,11... | collective-permute-start | bytes 1191944 | tf_op jit(solution)/shard_map/ppermute | solution.py:471
  27.3 14.0 %collective-permute-start.5 = (f32[776,128]{1,0:T(8,128)S(1)}, f32[776,128]{1,0:T(8,128)S(1)}, u32[]{:S(2)}, u32[]{:S(2)}) collective-permute-start(f32[776,128]{1,0:T(8,128)S(1)} %collective-permute-done.2.refs_0_), channel_id=1, source_target_pairs={{0,1},{1,0},{2,3},{3,2},{4,5},{5,4},{6,7},{7,6},{8,9},{9,8},{10,11... | collective-permute-start | bytes 1191944 | tf_op jit(solution)/shard_map/ppermute | solution.py:471
  27.8 0.7 %copy-start = (f32[776,128]{1,0:T(8,128)}, f32[776,128]{1,0:T(8,128)S(1)}, u32[]{:S(2)}) copy-start(f32[776,128]{1,0:T(8,128)S(1)} %collective-permute-done.9.refs_1_) | copy-start | bytes 1191940
  28.5 16.4 %collective-permute-start.1 = (f32[776,128]{1,0:T(8,128)S(1)}, f32[776,128]{1,0:T(8,128)}, u32[]{:S(2)}, u32[]{:S(2)}) collective-permute-start(f32[776,128]{1,0:T(8,128)S(1)} %collective-permute-done.refs_0_), channel_id=1, source_target_pairs={{1,2},{2,1},{3,4},{4,3},{5,6},{6,5},{9,10},{10,9},{11,12},{12,11},... | collective-permute-start | bytes 1191944 | tf_op jit(solution)/shard_map/ppermute | solution.py:470
  32.9 12.0 %collective-permute-start.3 = (f32[776,128]{1,0:T(8,128)S(1)}, f32[776,128]{1,0:T(8,128)}, u32[]{:S(2)}, u32[]{:S(2)}) collective-permute-start(f32[776,128]{1,0:T(8,128)S(1)} %collective-permute-done.2.refs_0_), channel_id=1, source_target_pairs={{1,2},{2,1},{3,4},{4,3},{5,6},{6,5},{9,10},{10,9},{11,12},{12,11},... | collective-permute-start | bytes 1191944 | tf_op jit(solution)/shard_map/ppermute | solution.py:470
  34.9 1.0 %copy-start.2 = (f32[776,128]{1,0:T(8,128)S(1)}, f32[776,128]{1,0:T(8,128)}, u32[]{:S(2)}) copy-start(f32[776,128]{1,0:T(8,128)} %get-tuple-element.52.refs_0_) | copy-start | bytes 1191940
  35.9 0.7 %copy-start.3 = (f32[8,128]{1,0:T(8,128)S(1)}, f32[8,128]{1,0:T(8,128)}, u32[]{:S(2)}) copy-start(f32[8,128]{1,0:T(8,128)} %get-tuple-element.53.refs_1_.refs_3_.refs_2_) | copy-start | bytes 12292
  37.4 1.0 %copy-start.1 = (f32[776,128]{1,0:T(8,128)S(1)}, f32[776,128]{1,0:T(8,128)}, u32[]{:S(2)}) copy-start(f32[776,128]{1,0:T(8,128)} %copy-done) | copy-start | bytes 1191940
  38.4 0.7 %copy-start.4 = (f32[8,128]{1,0:T(8,128)S(1)}, f32[8,128]{1,0:T(8,128)}, u32[]{:S(2)}) copy-start(f32[8,128]{1,0:T(8,128)} %get-tuple-element.53.refs_1_.refs_3_.refs_2_) | copy-start | bytes 12292
